TPU v7x, 32 devices: a whole 2x2x4 slice. The times are simulated.
32 devices in a mesh: dp: 8 (over y, x, core), table: 4 (over z).
Axes of the slice: x: 2, y: 2, z: 4, core: 2. Of those that a mesh axis runs over, the one named last changes fastest.
Arguments:
- item_ids: int32 [64, 384], P(('dp', 'table')), may hold values from 0 to 393215, as said below
- table_ids: int32 [64, 384], P(('dp', 'table')), may hold values from 0 to 3
- lengths: int32 [64], P(('dp', 'table')), may hold values from 24 to 384
- assignment: int32 [64], P(('dp', 'table')), may hold values from 0 to 63, as said below
- table_a: bfloat16 [393216, 64], P(('dp', 'table')), may hold values from -6 to 6
- table_b: bfloat16 [393216, 64], P(('dp', 'table')), may hold values from -6 to 6
- table_c: bfloat16 [196608, 128], P(('dp', 'table')), may hold values from -6 to 6
- table_d: bfloat16 [65536, 256], P(('dp', 'table')), may hold values from -6 to 6
- proj_weight: bfloat16 [512, 512], P('dp'), may hold values from -0.5 to 0.5
- in_weight: bfloat16 [512, 2048], P('dp'), may hold values from -0.25 to 0.25
- out_weight: bfloat16 [512, 512], P('dp'), may hold values from -0.25 to 0.25
- cotangent: bfloat16 [64, 384, 512], P(('dp', 'table')), may hold values from -6 to 6
Outputs:
- output: bfloat16 [64, 384, 512], P(('dp', 'table'))
- grad_a: bfloat16 [393216, 64], P(('dp', 'table'))
- grad_b: bfloat16 [393216, 64], P(('dp', 'table'))
- grad_c: bfloat16 [196608, 128], P(('dp', 'table'))
- grad_d: bfloat16 [65536, 256], P(('dp', 'table'))
- grad_proj: float32 [512, 512], P('dp')
- grad_in: float32 [512, 2048], P('dp')
- grad_out: float32 [512, 512], P('dp')
Inputs may be any that keep to these rules, and one draw needn't show every extreme that they name: `item_ids`: A sequence's events past its length name rows too. An event's item is below 32 times the rows one device holds of the event's table (row r of a table lies on device r // (rows a device of that table) along dp+table). After the move, the events of the 2 slots of one device name at most 12 times rows of one table held by one device, and for some table and device exactly 12 times, from every device. `assignment`: A permutation of the sequence slots; a sequence moves only among the devices of its own table index, and each device receives 2 sequences.
All inputs are finite; a program needn't handle non-finite values.
Results may differ from a plain program's by a relative error of at most 0.028.
Values may be sent and summed in bfloat16 or wider, within the bound.
No kernel may reach another device: no remote copies, remote signals or barrier semaphores. Data moves between devices by JAX's collectives and lax.ppermute only.
A program may use at most 128 MiB of HBM per device.

v0:
```python
import functools

import jax
import jax.numpy as jnp
from jax import lax
from jax.experimental import pallas as pl
from jax.experimental.pallas import tpu as pltpu
from jax.sharding import PartitionSpec as P

HEADS = 4
SPLIT = 1024
F32 = jnp.float32
BF16 = jnp.bfloat16
NN = (((1,), (0,)), ((), ()))
NT = (((1,), (1,)), ((), ()))
TN = (((0,), (0,)), ((), ()))
VM = pl.BlockSpec(memory_space=pltpu.VMEM)
SM = pl.BlockSpec(memory_space=pltpu.SMEM)
HB = pl.BlockSpec(memory_space=pl.ANY)


def dot(left, right, dims=NN):
    return lax.dot_general(left, right, dims, preferred_element_type=F32)


def iota(shape, dim):
    return lax.broadcasted_iota(jnp.int32, shape, dim)


def onehot(flags):
    return jnp.where(flags, 1.0, 0.0).astype(BF16)


def floor_div(values, by):
    return jnp.floor((values.astype(F32) + 0.5) * (1.0 / by)).astype(jnp.int32)


def sigmoid(values):
    return 0.5 * jnp.tanh(0.5 * values) + 0.5


def log2(value):
    assert value & (value - 1) == 0
    return value.bit_length() - 1


def mask_of(index, seq):
    mask = 0
    for place, bit in enumerate(reversed(seq)):
        if (index >> place) & 1:
            mask |= 1 << bit
    return mask


def place_of(mask, seq):
    index = 0
    for place, bit in enumerate(reversed(seq)):
        index = index | (((mask >> bit) & 1) << place)
    return index


def owner_and_row(items, kinds, row_counts):
    rows = jnp.zeros_like(items)
    inverse = jnp.zeros(items.shape, F32)
    for which in range(4):
        hit = kinds == which
        rows = jnp.where(hit, row_counts[which], rows)
        inverse = jnp.where(hit, 1.0 / row_counts[which], inverse)
    owner = jnp.floor(items.astype(F32) * inverse).astype(jnp.int32)
    rest = items - owner * rows
    low = rest < 0
    owner = jnp.where(low, owner - 1, owner)
    rest = jnp.where(low, rest + rows, rest)
    high = rest >= rows
    owner = jnp.where(high, owner + 1, owner)
    rest = jnp.where(high, rest - rows, rest)
    return owner, rest


def plan_kernel(planes, devices, seq_count, span, capacity, row_counts, widths, *refs):
    me_ref, refs = refs[0], refs[1:]
    ids_refs, refs = refs[:planes], refs[planes:]
    table_refs, refs = refs[:4], refs[4:]
    send_ref, idxc_ref, idxr_ref, info_ref, infot_ref = refs[:5]
    held = refs[5:9]
    rows_scr, pack_scr, sems = refs[9:]
    copies = [pltpu.make_async_copy(table_refs[i], held[i], sems.at[i]) for i in range(4)]
    for copy in copies:
        copy.start()
    me = me_ref[0]
    seqs = devices * seq_count
    slots = devices * capacity
    toks = seq_count * span
    ids = jnp.concatenate([ref[...] for ref in ids_refs], axis=0)
    items = ids[:, :span]
    kinds = ids[:, span : 2 * span]
    tail = ids[:, 2 * span : 2 * span + 128]
    lens = tail[:, 0:1]
    target = tail[:, 1:2]
    own_items, own_kinds, own_valid = [], [], []
    for q in range(seq_count):
        hit = target == me * seq_count + q
        own_items.append(jnp.sum(jnp.where(hit, items, 0), axis=0, keepdims=True))
        own_kinds.append(jnp.sum(jnp.where(hit, kinds, 0), axis=0, keepdims=True))
        length = jnp.sum(jnp.where(hit, lens, 0), axis=0, keepdims=True)
        own_valid.append(jnp.where(iota((1, span), 1) < length, 1.0, 0.0))
    e_items = jnp.concatenate(own_items, axis=1)
    e_kinds = jnp.concatenate(own_kinds, axis=1)
    e_valid = jnp.concatenate(own_valid, axis=1)
    e_owner, _ = owner_and_row(e_items, e_kinds, row_counts)
    bucket = e_kinds * devices + e_owner
    member = onehot(iota((4 * devices, toks), 0) == bucket)
    before = onehot(iota((toks, toks), 0) < iota((toks, toks), 1))
    counts = dot(member, before)
    rank = jnp.sum(counts * member.astype(F32), axis=0, keepdims=True)
    slot = e_owner.astype(F32) * capacity + rank
    info = jnp.concatenate([slot, e_kinds.astype(F32), e_valid, jnp.zeros((5, toks), F32)], axis=0)
    info_ref[...] = info
    infot_ref[...] = jnp.transpose(
        jnp.concatenate([info, jnp.zeros((120, toks), F32)], axis=0), (1, 0)
    )
    owner, row = owner_and_row(items, kinds, row_counts)
    fields = jnp.concatenate(
        [
            jnp.where(owner == me, kinds, 4).astype(F32).astype(BF16),
            (row >> 7).astype(F32).astype(BF16),
            (row & 127).astype(F32).astype(BF16),
        ],
        axis=1,
    )
    moves = onehot(target == iota((seqs, seqs), 1))
    moved = dot(moves, fields, TN)
    m_kind = moved[:, :span]
    m_row = moved[:, span : 2 * span] * 128.0 + moved[:, 2 * span : 3 * span]
    hits = jnp.concatenate([onehot(m_kind == float(which)) for which in range(4)], axis=0)
    earlier = before[:span, :span]
    ahead = dot(hits, earlier)
    totals = jnp.sum(hits.astype(F32), axis=1, keepdims=True)
    si, sj = iota((seqs, seqs), 0), iota((seqs, seqs), 1)
    sibling = (floor_div(si, seq_count) == floor_div(sj, seq_count)) & (sj < si)
    code = jnp.full((seqs, span), -1.0, F32)
    for which in range(4):
        lo, hi = which * seqs, (which + 1) * seqs
        total = jnp.broadcast_to(totals[lo:hi], (seqs, 128)).astype(BF16)
        shift = dot(onehot(sibling), total)[:, 0:1]
        code = jnp.where(
            m_kind == float(which), ahead[lo:hi] + shift + float(which * capacity), code
        )
    asked = jnp.zeros((seqs, 128), F32)
    lane = iota((seqs, 128), 1)
    for tk in range(4 * capacity):
        value = jnp.sum(jnp.where(code == float(tk), m_row, 0.0), axis=1, keepdims=True)
        asked = jnp.where(lane == tk, value, asked)
    asked_high = jnp.floor(asked * (1.0 / 128.0))
    asked_low = asked - asked_high * 128.0
    spread = onehot(
        floor_div(iota((slots, seqs), 0), capacity) == floor_div(iota((slots, seqs), 1), seq_count)
    )
    full = dot(spread, asked_high.astype(BF16)) * 128.0 + dot(spread, asked_low.astype(BF16))
    place = iota((slots, 128), 0)
    place = place - floor_div(place, capacity) * capacity
    wide = iota((slots, 128), 1)
    columns = jnp.zeros((slots, 128), F32)
    highs, lows = [], []
    for which in range(4):
        index = jnp.sum(
            jnp.where(wide == place + which * capacity, full, 0.0), axis=1, keepdims=True
        )
        high = jnp.floor(index * (1.0 / SPLIT))
        low = index - high * SPLIT
        highs.append(high)
        lows.append(low)
        columns = jnp.where(wide == which, high, columns)
        columns = jnp.where(wide == which + 4, low, columns)
    idxc_ref[...] = columns
    idxr_ref[...] = jnp.transpose(columns, (1, 0))
    for copy in copies:
        copy.wait()
    low_lane = iota((slots, SPLIT), 1)

    def pick(which):
        return onehot(low_lane == lows[which].astype(jnp.int32))

    narrow = []
    for which in range(2):
        width = widths[which]
        steps = row_counts[which] // SPLIT
        group = 256 // width
        while steps % group:
            group //= 2
        chosen = pick(which)
        block = iota((slots, group * width), 1) >> log2(width)
        total = jnp.zeros((slots, group * width), F32)
        for g in range(steps // group):
            stack = jnp.concatenate(
                [
                    held[which][:, (g * group + b) * SPLIT : (g * group + b + 1) * SPLIT]
                    for b in range(group)
                ],
                axis=0,
            )
            found = dot(chosen, stack, NT)
            total = jnp.where(
                block + g * group == highs[which].astype(jnp.int32), found, total
            )
        folded = total[:, :128]
        for b in range(1, group * width // 128):
            folded = folded + total[:, b * 128 : (b + 1) * 128]
        folded = folded + pltpu.roll(folded, 64, 1)
        narrow.append(folded)
    rows_scr[0] = jnp.where(iota((slots, 128), 1) < widths[0], narrow[0], narrow[1])
    for which in range(2, 4):
        width = widths[which]
        chosen = pick(which)
        total = jnp.zeros((slots, width), F32)
        for step in range(row_counts[which] // SPLIT):
            found = dot(chosen, held[which][step * SPLIT : (step + 1) * SPLIT, :])
            total = jnp.where(highs[which] == float(step), found, total)
        for b in range(width // 128):
            rows_scr[which - 1 + b] = total[:, b * 128 : (b + 1) * 128]

    def pack(device, carry):
        for j in range(4):
            pack_scr[device, j * capacity : (j + 1) * capacity, :] = rows_scr[
                j, pl.ds(device * capacity, capacity), :
            ]
        return carry

    lax.fori_loop(0, devices, pack, 0)
    send_ref[...] = pack_scr[...].astype(BF16)


def layer_kernel(
    devices, seq_count, span, capacity, widths, dp_count, half, seq_a, seq_b, pieces, *refs
):
    me_ref, got_ref, info_ref, infot_ref, cot_ref = refs[:5]
    refs = refs[5:]
    a_refs, refs = refs[:pieces], refs[pieces:]
    b_refs, refs = refs[:pieces], refs[pieces:]
    out_ref, back_ref, ga_ref, gb_ref = refs[:4]
    (
        wa, wb, slot_scr, pack_scr, cat_scr, norm_scr, act_scr, slope_scr, attn_scr, tilt_scr,
        att_scr, datt_scr, dproj_scr, gated_scr, og_scr, demb_scr, drow_scr, dact_scr,
    ) = refs[4:]
    dp = me_ref[1]
    width = out_ref.shape[2]
    slots = devices * capacity
    toks = seq_count * span
    rows_each = width // dp_count
    head_dim = width // HEADS
    scale = head_dim**-0.5
    for refs_in, held, seq in ((a_refs, wa, seq_a), (b_refs, wb, seq_b)):
        index = 0
        for ref in refs_in:
            for k in range(ref.shape[0]):
                chunk = dp ^ mask_of(index, seq)
                start = pl.multiple_of(chunk * rows_each, rows_each)
                held[pl.ds(start, rows_each), :] = ref[k]
                index += 1
    pack_scr[...] = got_ref[...].astype(F32)

    def unpack(device, carry):
        for j in range(4):
            slot_scr[j, pl.ds(device * capacity, capacity), :] = pack_scr[
                device, j * capacity : (j + 1) * capacity, :
            ]
        return carry

    lax.fori_loop(0, devices, unpack, 0)
    arrived = jnp.concatenate([slot_scr[j].astype(BF16) for j in range(4)], axis=1)

    def in_part(j):
        return wa[:, j * width : (j + 1) * width] if j < 3 else wb[:, :width]

    lane = iota((span, width), 1)
    kind_of_lane = jnp.zeros((span, width), jnp.int32)
    edge = 0
    for which in range(3):
        edge += widths[which]
        kind_of_lane = kind_of_lane + jnp.where(lane >= edge, 1, 0)
    blocks = span // 128

    def sequence(q, carry):
        base = pl.multiple_of(q * span, span)
        rows = pl.ds(base, span)
        slot = infot_ref[rows, 0:1].astype(jnp.int32)
        kind = infot_ref[rows, 1:2].astype(jnp.int32)
        valid = infot_ref[rows, 2:3]
        chosen = onehot(iota((span, slots), 1) == slot)
        cat = jnp.where(kind_of_lane == kind, dot(chosen, arrived), 0.0).astype(BF16)
        cat_scr[rows, :] = cat
        emb = dot(cat, wb[:, 2 * width : 3 * width]).astype(BF16).astype(F32)
        centred = emb - jnp.mean(emb, axis=1, keepdims=True)
        inv = lax.rsqrt(jnp.mean(centred * centred, axis=1, keepdims=True) + 1e-05)
        normed = centred * inv
        norm_scr[rows, :] = normed.astype(BF16)
        for j in range(4):
            mixed = dot(norm_scr[rows, :], in_part(j))
            sig = sigmoid(mixed)
            part = mixed * sig
            act_scr[j] = part.astype(BF16)
            slope_scr[j] = sig + part * (1.0 - sig)
        for head in range(HEADS):
            cols = slice(head * head_dim, (head + 1) * head_dim)
            for rb in range(blocks):
                keys = (rb + 1) * 128
                here = slice(rb * 128, keys)
                scores = dot(act_scr[2, here, cols], act_scr[3, :keys, cols], NT) * scale
                key_pos = iota((128, keys), 1)
                keep = (key_pos <= iota((128, keys), 0) + rb * 128) & (
                    key_pos < carry_len(q, info_ref, span)
                )
                sig = sigmoid(scores)
                attn = scores * sig
                attn_scr[head, here, :keys] = jnp.where(keep, attn, 0.0).astype(BF16)
                tilt_scr[head, here, :keys] = jnp.where(
                    keep, (sig + attn * (1.0 - sig)) * scale, 0.0
                )
                att_scr[here, cols] = dot(
                    attn_scr[head, here, :keys], act_scr[1, :keys, cols]
                )
        attended = att_scr[...]
        att_c = attended - jnp.mean(attended, axis=1, keepdims=True)
        att_inv = lax.rsqrt(jnp.mean(att_c * att_c, axis=1, keepdims=True) + 1e-05)
        att_n = att_c * att_inv
        gate = act_scr[0].astype(F32)
        gated = (att_n * gate).astype(BF16)
        gated_scr[rows, :] = gated
        out_w = wb[:, width : 2 * width]
        out_ref[q] = (emb + dot(gated, out_w)).astype(BF16)
        og = jnp.where(valid > 0.5, cot_ref[q].astype(F32), 0.0).astype(BF16)
        og_scr[rows, :] = og
        d_gated = dot(og, out_w, NT).astype(BF16).astype(F32)
        d_gate = (d_gated * att_n).astype(BF16).astype(F32)
        dproj_scr[rows, :width] = (d_gate * slope_scr[0]).astype(BF16)
        d_n = d_gated * gate
        d_att = att_inv * (
            d_n
            - jnp.mean(d_n, axis=1, keepdims=True)
            - att_n * jnp.mean(d_n * att_n, axis=1, keepdims=True)
        )
        datt_scr[...] = d_att.astype(BF16)
        for head in range(HEADS):
            cols = slice(head * head_dim, (head + 1) * head_dim)
            for rb in range(blocks):
                keys = (rb + 1) * 128
                here = slice(rb * 128, keys)
                d_attn = dot(datt_scr[here, cols], act_scr[1, :keys, cols], NT)
                d_attn = d_attn.astype(BF16).astype(F32)
                tilt = (d_attn * tilt_scr[head, here, :keys]).astype(BF16)
                dact_scr[head, here, :keys] = tilt
                d_query = dot(tilt, act_scr[3, :keys, cols]).astype(BF16).astype(F32)
                low = 2 * width + head * head_dim
                dproj_scr[pl.ds(base + rb * 128, 128), low : low + head_dim] = (
                    d_query * slope_scr[2, here, cols]
                ).astype(BF16)
            for kb in range(blocks):
                here = slice(kb * 128, (kb + 1) * 128)
                rest = slice(kb * 128, span)
                d_value = dot(attn_scr[head, rest, here], datt_scr[rest, cols], TN)
                d_key = dot(dact_scr[head, rest, here], act_scr[2, rest, cols], TN)
                low = width + head * head_dim
                dproj_scr[pl.ds(base + kb * 128, 128), low : low + head_dim] = (
                    d_value.astype(BF16).astype(F32) * slope_scr[1, here, cols]
                ).astype(BF16)
                low = 3 * width + head * head_dim
                dproj_scr[pl.ds(base + kb * 128, 128), low : low + head_dim] = (
                    d_key.astype(BF16).astype(F32) * slope_scr[3, here, cols]
                ).astype(BF16)
        d_normed = jnp.zeros((span, width), F32)
        for j in range(4):
            d_normed = d_normed + dot(
                dproj_scr[rows, j * width : (j + 1) * width], in_part(j), NT
            )
        d_normed = d_normed.astype(BF16).astype(F32)
        d_emb = inv * (
            d_normed
            - jnp.mean(d_normed, axis=1, keepdims=True)
            - normed * jnp.mean(d_normed * normed, axis=1, keepdims=True)
        )
        d_emb = (d_emb + og.astype(F32)).astype(BF16)
        demb_scr[rows, :] = d_emb
        d_rows = dot(d_emb, wb[:, 2 * width : 3 * width], NT)
        drow_scr[rows, :] = jnp.where(kind_of_lane == kind, d_rows, 0.0).astype(BF16)
        return carry

    lax.fori_loop(0, seq_count, sequence, 0)
    chosen = onehot(iota((slots, toks), 0) == info_ref[0:1, :].astype(jnp.int32))
    outgoing = dot(chosen, drow_scr[...])
    for j in range(4):
        slot_scr[j] = outgoing[:, j * 128 : (j + 1) * 128]

    def pack(device, carry):
        for j in range(4):
            pack_scr[device, j * capacity : (j + 1) * capacity, :] = slot_scr[
                j, pl.ds(device * capacity, capacity), :
            ]
        return carry

    lax.fori_loop(0, devices, pack, 0)
    back_ref[...] = pack_scr[...].astype(BF16)

    def emit(grad, target, seq, low):
        grad = grad.astype(BF16)
        for chunk in range(dp_count):
            index = place_of(dp ^ chunk, seq)
            target[index, :, low : low + width] = grad[
                chunk * rows_each : (chunk + 1) * rows_each, :
            ]

    for j in range(4):
        grad = dot(norm_scr[...], dproj_scr[:, j * width : (j + 1) * width], TN)
        if j < 3:
            emit(grad, ga_ref, seq_a, j * width)
        else:
            emit(grad, gb_ref, seq_b, 0)
    emit(dot(gated_scr[...], og_scr[...], TN), gb_ref, seq_b, width)
    emit(dot(cat_scr[...], demb_scr[...], TN), gb_ref, seq_b, 2 * width)


def carry_len(q, info_ref, span):
    flags = info_ref[2:3, pl.ds(pl.multiple_of(q * span, 128), span)]
    return jnp.sum(flags, axis=1, keepdims=True).astype(jnp.int32)


def scatter_kernel(devices, capacity, row_counts, widths, *refs):
    got_ref, idxc_ref, idxr_ref = refs[:3]
    outs = refs[3:7]
    held = refs[7:11]
    slot_scr, pack_scr, sems = refs[11:]
    slots = devices * capacity
    pack_scr[...] = got_ref[...].astype(F32)

    def unpack(device, carry):
        for j in range(4):
            slot_scr[j, pl.ds(device * capacity, capacity), :] = pack_scr[
                device, j * capacity : (j + 1) * capacity, :
            ]
        return carry

    lax.fori_loop(0, devices, unpack, 0)
    copies = [pltpu.make_async_copy(held[i], outs[i], sems.at[i]) for i in range(4)]
    first = slot_scr[0]
    rolled = pltpu.roll(first, 64, 1)
    left = iota((slots, 128), 1) < widths[0]
    pairs = [jnp.where(left, first, rolled), jnp.where(left, rolled, first)]
    for which in range(2):
        width = widths[which]
        steps = row_counts[which] // SPLIT
        group = 256 // width
        while steps % group:
            group //= 2
        span = group * width
        high = idxc_ref[:, which : which + 1].astype(jnp.int32)
        low = idxc_ref[:, 4 + which : 5 + which].astype(jnp.int32)
        chosen = onehot(iota((slots, SPLIT), 1) == low)
        wide = jnp.concatenate([pairs[which]] * (span // 128), axis=1)
        block = iota((slots, span), 1) >> log2(width)
        for g in range(steps // group):
            part = jnp.where(block + g * group == high, wide, 0.0).astype(BF16)
            found = dot(part, chosen, TN).astype(BF16)
            for b in range(group):
                at = (g * group + b) * SPLIT
                held[which][:, at : at + SPLIT] = found[b * width : (b + 1) * width, :]
        copies[which].start()
    for which in range(2, 4):
        width = widths[which]
        steps = row_counts[which] // SPLIT
        group = 256 // width
        while steps % group:
            group //= 2
        high = idxc_ref[:, which : which + 1].astype(jnp.int32)
        low = idxr_ref[4 + which : 5 + which, :].astype(jnp.int32)
        chosen = onehot(iota((SPLIT, slots), 0) == low)
        wide = jnp.concatenate(
            [slot_scr[which - 1 + b] for b in range(width // 128)], axis=1
        )
        for g in range(steps // group):
            part = jnp.concatenate(
                [jnp.where(high == g * group + b, wide, 0.0).astype(BF16) for b in range(group)],
                axis=1,
            )
            found = dot(chosen, part).astype(BF16)
            for b in range(group):
                at = (g * group + b) * SPLIT
                held[which][at : at + SPLIT, :] = found[:, b * width : (b + 1) * width]
        copies[which].start()
    for copy in copies:
        copy.wait()


def split_kernel(planes, me_ref, ka_ref, ra_ref, kb_ref, rb_ref, *refs):
    outs, scr = refs[:planes], refs[planes]
    half = ka_ref.shape[1]
    scr[:, :half] = (ka_ref[...].astype(F32) + ra_ref[...].astype(F32)).astype(BF16)
    scr[:, half:] = (kb_ref[...].astype(F32) + rb_ref[...].astype(F32)).astype(BF16)
    size = outs[0].shape[1]
    for m in range(planes):
        at = pl.multiple_of((me_ref[2] ^ m) * size, 128)
        outs[m][...] = scr[:, pl.ds(at, size)]


def sum_kernel(*refs):
    total = refs[0][...].astype(F32)
    for ref in refs[1:-1]:
        total = total + ref[...].astype(F32)
    refs[-1][...] = total.astype(BF16)


def join_kernel(planes, width, me_ref, *refs):
    parts = refs[:planes]
    proj_ref, in_ref, out_ref, scr = refs[planes:]
    size = parts[0].shape[1]
    for m in range(planes):
        at = pl.multiple_of((me_ref[2] ^ m) * size, 128)
        scr[:, pl.ds(at, size)] = parts[m][...].astype(F32)
    in_ref[...] = scr[:, : 4 * width]
    out_ref[...] = scr[:, 4 * width : 5 * width]
    proj_ref[...] = scr[:, 5 * width :]


def exchange(value, axis, mask):
    count = lax.axis_size(axis)
    return lax.ppermute(value, axis, [(i, i ^ mask) for i in range(count)])


def params():
    return pltpu.CompilerParams(vmem_limit_bytes=60 * 1024 * 1024)


def shards(
    item_ids, table_ids, lengths, assignment, table_a, table_b, table_c, table_d,
    proj_weight, in_weight, out_weight, cotangent,
):
    tables = (table_a, table_b, table_c, table_d)
    dp_count = lax.axis_size("dp")
    planes = lax.axis_size("table")
    devices = dp_count * planes
    seq_count, span = item_ids.shape
    toks = seq_count * span
    width = cotangent.shape[2]
    capacity = max(2, toks // (2 * devices))
    slots = devices * capacity
    row_counts = tuple(piece.shape[0] for piece in tables)
    widths = tuple(piece.shape[1] for piece in tables)
    rows_each = width // dp_count
    dp_bits = log2(dp_count)
    dp = lax.axis_index("dp")
    plane = lax.axis_index("table")
    me = jnp.stack([dp * planes + plane, dp, plane]).astype(jnp.int32)
    half = 3 * width
    far = list(range(1, dp_bits))
    seq_a = [0] + far
    seq_b = [0] + far[::-1]
    own_a = in_weight[:, :half][None]
    own_b = jnp.concatenate([in_weight[:, half:], out_weight, proj_weight], axis=1)[None]

    def gather(own, seq):
        held = own
        for bit in seq[:0:-1]:
            held = jnp.concatenate([held, exchange(held, "dp", 1 << bit)], axis=0)
        return held, exchange(held, "dp", 1 << seq[0])

    pad = jnp.zeros((seq_count, 126), jnp.int32)
    packed = jnp.concatenate(
        [item_ids, table_ids, lengths[:, None], assignment[:, None], pad], axis=1
    )
    near = lax.all_gather(packed, "dp", axis=0, tiled=True)
    ids = [near] + [exchange(near, "table", m) for m in range(1, planes)]
    wa = gather(own_a, seq_a)
    wb = gather(own_b, seq_b)
    send, idxc, idxr, info, infot = pl.pallas_call(
        functools.partial(
            plan_kernel, planes, devices, seq_count, span, capacity, row_counts, widths
        ),
        out_shape=(
            jax.ShapeDtypeStruct((devices, 4 * capacity, 128), BF16),
            jax.ShapeDtypeStruct((slots, 128), F32),
            jax.ShapeDtypeStruct((128, slots), F32),
            jax.ShapeDtypeStruct((8, toks), F32),
            jax.ShapeDtypeStruct((toks, 128), F32),
        ),
        in_specs=[SM] + [VM] * planes + [HB] * 4,
        out_specs=(VM,) * 5,
        scratch_shapes=[
            pltpu.VMEM((widths[0], row_counts[0]), BF16),
            pltpu.VMEM((widths[1], row_counts[1]), BF16),
            pltpu.VMEM((row_counts[2], widths[2]), BF16),
            pltpu.VMEM((row_counts[3], widths[3]), BF16),
            pltpu.VMEM((4, slots, 128), F32),
            pltpu.VMEM((devices, 4 * capacity, 128), F32),
            pltpu.SemaphoreType.DMA((4,)),
        ],
        compiler_params=params(),
        name="plan",
    )(me, *ids, table_a.T, table_b.T, table_c, table_d)
    got = lax.all_to_all(send, ("dp", "table"), 0, 0, tiled=True)
    pieces = len(wa)
    output, back, grad_a, grad_b = pl.pallas_call(
        functools.partial(
            layer_kernel, devices, seq_count, span, capacity, widths, dp_count, half,
            seq_a, seq_b, pieces,
        ),
        out_shape=(
            jax.ShapeDtypeStruct((seq_count, span, width), BF16),
            jax.ShapeDtypeStruct((devices, 4 * capacity, 128), BF16),
            jax.ShapeDtypeStruct((dp_count, rows_each, half), BF16),
            jax.ShapeDtypeStruct((dp_count, rows_each, half), BF16),
        ),
        in_specs=[SM] + [VM] * (4 + 2 * pieces),
        out_specs=(VM,) * 4,
        scratch_shapes=[
            pltpu.VMEM((width, half), BF16),
            pltpu.VMEM((width, half), BF16),
            pltpu.VMEM((4, slots, 128), F32),
            pltpu.VMEM((devices, 4 * capacity, 128), F32),
            pltpu.VMEM((toks, width), BF16),
            pltpu.VMEM((toks, width), BF16),
            pltpu.VMEM((4, span, width), BF16),
            pltpu.VMEM((4, span, width), F32),
            pltpu.VMEM((HEADS, span, span), BF16),
            pltpu.VMEM((HEADS, span, span), F32),
            pltpu.VMEM((span, width), F32),
            pltpu.VMEM((span, width), BF16),
            pltpu.VMEM((toks, 4 * width), BF16),
            pltpu.VMEM((toks, width), BF16),
            pltpu.VMEM((toks, width), BF16),
            pltpu.VMEM((toks, width), BF16),
            pltpu.VMEM((toks, width), BF16),
            pltpu.VMEM((HEADS, span, span), BF16),
        ],
        compiler_params=params(),
        name="layer",
    )(me, got, info, infot, cotangent, *wa, *wb)

    def halve(held, seq):
        for place, bit in enumerate(seq):
            mid = held.shape[0] // 2
            taken = exchange(held[mid:], "dp", 1 << bit)
            if place == len(seq) - 1:
                return held[0], taken[0]
            held = (held[:mid].astype(F32) + taken.astype(F32)).astype(BF16)

    returned = lax.all_to_all(back, ("dp", "table"), 0, 0, tiled=True)
    kept_a, sent_a = halve(grad_a, seq_a)
    kept_b, sent_b = halve(grad_b, seq_b)
    size = 2 * half // planes
    parts = pl.pallas_call(
        functools.partial(split_kernel, planes),
        out_shape=(jax.ShapeDtypeStruct((rows_each, size), BF16),) * planes,
        in_specs=[SM] + [VM] * 4,
        out_specs=(VM,) * planes,
        scratch_shapes=[pltpu.VMEM((rows_each, 2 * half), BF16)],
        compiler_params=params(),
        name="split",
    )(me, kept_a, sent_a, kept_b, sent_b)
    terms = [parts[0]] + [exchange(parts[m], "table", m) for m in range(1, planes)]
    summed = pl.pallas_call(
        sum_kernel,
        out_shape=jax.ShapeDtypeStruct((rows_each, size), BF16),
        in_specs=[VM] * planes,
        out_specs=VM,
        compiler_params=params(),
        name="total",
    )(*terms)
    whole = [summed] + [exchange(summed, "table", m) for m in range(1, planes)]
    grad_proj, grad_in, grad_out = pl.pallas_call(
        functools.partial(join_kernel, planes, width),
        out_shape=(
            jax.ShapeDtypeStruct((rows_each, width), F32),
            jax.ShapeDtypeStruct((rows_each, 4 * width), F32),
            jax.ShapeDtypeStruct((rows_each, width), F32),
        ),
        in_specs=[SM] + [VM] * planes,
        out_specs=(VM,) * 3,
        scratch_shapes=[pltpu.VMEM((rows_each, 2 * half), F32)],
        compiler_params=params(),
        name="join",
    )(me, *whole)
    g_a, g_b, g_c, g_d = pl.pallas_call(
        functools.partial(scatter_kernel, devices, capacity, row_counts, widths),
        out_shape=(
            jax.ShapeDtypeStruct((widths[0], row_counts[0]), BF16),
            jax.ShapeDtypeStruct((widths[1], row_counts[1]), BF16),
            jax.ShapeDtypeStruct((row_counts[2], widths[2]), BF16),
            jax.ShapeDtypeStruct((row_counts[3], widths[3]), BF16),
        ),
        in_specs=[VM] * 3,
        out_specs=(HB,) * 4,
        scratch_shapes=[
            pltpu.VMEM((widths[0], row_counts[0]), BF16),
            pltpu.VMEM((widths[1], row_counts[1]), BF16),
            pltpu.VMEM((row_counts[2], widths[2]), BF16),
            pltpu.VMEM((row_counts[3], widths[3]), BF16),
            pltpu.VMEM((4, slots, 128), F32),
            pltpu.VMEM((devices, 4 * capacity, 128), F32),
            pltpu.SemaphoreType.DMA((4,)),
        ],
        compiler_params=params(),
        name="scatter",
    )(returned, idxc, idxr)
    return output, g_a.T, g_b.T, g_c, g_d, grad_proj, grad_in, grad_out


def solution(mesh):
    both = ("dp", "table")
    return jax.shard_map(
        shards,
        mesh=mesh,
        in_specs=(
            P(both, None), P(both, None), P(both), P(both),
            P(both, None), P(both, None), P(both, None), P(both, None),
            P("dp", None), P("dp", None), P("dp", None), P(both, None, None),
        ),
        out_specs=(
            P(both, None, None), P(both, None), P(both, None), P(both, None), P(both, None),
            P("dp", None), P("dp", None), P("dp", None),
        ),
        check_vma=False,
    )
```

profile of v0, /device:TPU:0, one launch (start us, length us, event | category | flops | bytes accessed | tf_op | source)
XLA Modules:
  0.0 150.9 jit_solution(5273690875160977693)
XLA Ops:
  2.4 3.0 %collective-permute-start.6 = (bf16[1,64,1536]{2,1,0:T(8,128)(2,1)S(1)}, bf16[1,64,1536]{2,1,0:T(8,128)(2,1)S(1)}, u32[]{:S(2)}, u32[]{:S(2)}) collective-permute-start(bf16[1,64,1536]{2,1,0:T(8,128)(2,1)S(1)} %maximum_bitcast_fusion), channel_id=1, source_target_pairs={{0,8},{4,12},{8,0},{12,4},{16,24},{20,28},{24,16},{28,20},{1,9},{5... | collective-permute-start | bytes 589832 | tf_op jit(solution)/shard_map/ppermute | solution.py:524
  6.4 1.6 %collective-permute-start.3 = (bf16[1,64,1536]{2,1,0:T(8,128)(2,1)S(1)}, bf16[1,64,1536]{2,1,0:T(8,128)(2,1)S(1)}, u32[]{:S(2)}, u32[]{:S(2)}) collective-permute-start(bf16[1,64,1536]{2,1,0:T(8,128)(2,1)S(1)} %slice_bitcast_fusion.2), channel_id=1, source_target_pairs={{0,16},{4,20},{8,24},{12,28},{16,0},{20,4},{24,8},{28,12},{1,17},{... | collective-permute-start | bytes 589832 | tf_op jit(solution)/shard_map/ppermute | solution.py:524
  8.0 2.4 %collective-permute-done.6 = bf16[1,64,1536]{2,1,0:T(8,128)(2,1)S(1)} collective-permute-done((bf16[1,64,1536]{2,1,0:T(8,128)(2,1)S(1)}, bf16[1,64,1536]{2,1,0:T(8,128)(2,1)S(1)}, u32[]{:S(2)}, u32[]{:S(2)}) %collective-permute-start.6) | collective-permute-done | bytes 196640 | tf_op jit(solution)/shard_map/ppermute | solution.py:524
  10.4 1.8 %collective-permute-start.7 = (bf16[2,64,1536]{2,1,0:T(8,128)(2,1)S(1)}, bf16[2,64,1536]{2,1,0:T(8,128)(2,1)S(1)}, u32[]{:S(2)}, u32[]{:S(2)}) collective-permute-start(bf16[2,64,1536]{2,1,0:T(8,128)(2,1)S(1)} %pad_maximum_fusion.3), channel_id=1, source_target_pairs={{0,16},{4,20},{8,24},{12,28},{16,0},{20,4},{24,8},{28,12},{1,17},{... | collective-permute-start | bytes 1179656 | tf_op jit(solution)/shard_map/ppermute | solution.py:524
  12.2 1.1 collective-permute-done.3
  14.1 12.9 %all-gather = s32[8,2,896]{2,1,0:T(2,128)S(1)} all-gather(s32[1,2,896]{2,1,0:T(2,128)S(1)} %bitcast.24), channel_id=1, replica_groups=mesh['dp'=8,'table'=4] {'dp'}, dimensions={0}, use_global_device_ids=true | all-gather | bytes 64512 | tf_op jit(solution)/shard_map/all_gather | solution.py:568
  27.7 3.6 %collective-permute-start.2 = (s32[16,896]{1,0:T(8,128)}, s32[16,896]{1,0:T(8,128)}, u32[]{:S(2)}, u32[]{:S(2)}) collective-permute-start(s32[16,896]{1,0:T(8,128)} %reshape.17.refs_1_), channel_id=1, source_target_pairs={{0,3},{1,2},{2,1},{3,0},{4,7},{5,6},{6,5},{7,4},{8,11},{9,10},{10,... | collective-permute-start | bytes 172040 | tf_op jit(solution)/shard_map/ppermute | solution.py:524
  34.2 2.9 %collective-permute-done.1.refs_3_ = s32[16,896]{1,0:T(8,128)} collective-permute-done((s32[16,896]{1,0:T(8,128)}, s32[16,896]{1,0:T(8,128)}, u32[]{:S(2)}, u32[]{:S(2)}) %collective-permute-start.1) | collective-permute-done | bytes 57376 | tf_op jit(solution)/shard_map/ppermute | solution.py:524
  37.1 8.0 %plan.1 = (bf16[32,48,128]{2,1,0:T(8,128)(2,1)}, f32[384,128]{1,0:T(8,128)}, f32[128,384]{1,0:T(8,128)}, f32[8,768]{1,0:T(8,128)}, f32[768,128]{1,0:T(8,128)}) custom-call(s32[3]{0:T(128)} %pad_add_fusion.refs_0_.me_ref, s32[16,896]{1,0:T(8,128)} %reshape.17.refs_1_, s32[16,896]{1,0:T(8,128)} %collective-permute-done.refs_2_, ...), custom_call_target="tpu_custom_call" | custom-call | tf_op jit(solution)/shard_map/plan/pallas_call | solution.py:572
  45.1 15.6 %all_to_all.10.refs_1_ = bf16[32,48,128]{2,1,0:T(8,128)(2,1)} all-to-all(bf16[32,48,128]{2,1,0:T(8,128)(2,1)} %get-tuple-element.28), channel_id=1, replica_groups=mesh['dp'=8,'table'=4] {'dp','table'}, dimensions={0} | all-to-all | bytes 786432 | tf_op jit(solution)/shard_map/all_to_all | solution.py:597
  61.8 26.1 %layer.1 = (bf16[2,384,512]{2,1,0:T(8,128)(2,1)}, bf16[32,48,128]{2,1,0:T(8,128)(2,1)}, bf16[8,64,1536]{2,1,0:T(8,128)(2,1)}, bf16[8,64,1536]{2,1,0:T(8,128)(2,1)}) custom-call(s32[3]{0:T(128)} %pad_add_fusion.refs_0_.me_ref, bf16[32,48,128]{2,1,0:T(8,128)(2,1)} %all_to_all.10.refs_1_, f32[8,768]{1,0:T(8,128)} %get-tuple-element.29.refs_2_, ...), custom_call_target="tpu_custom_call" | custom-call | tf_op jit(solution)/shard_map/layer/pallas_call | solution.py:599
  87.9 2.2 %slice.51 = bf16[4,64,1536]{2,1,0:T(8,128)(2,1)} slice(bf16[8,64,1536]{2,1,0:T(8,128)(2,1)} %get-tuple-element.40), slice={[4:8], [0:64], [0:1536]} | slice | bytes 1572864 | tf_op jit(solution)/shard_map/slice | solution.py:639
  90.1 1.2 collective-permute-start.12
  92.3 3.3 %all-to-all-start.1 = ((bf16[32,48,128]{2,1,0:T(8,128)(2,1)}), bf16[32,48,128]{2,1,0:T(8,128)(2,1)S(1)}, u32[]{:S(2)}, u32[]{:S(2)}) async-start(bf16[32,48,128]{2,1,0:T(8,128)(2,1)} %get-tuple-element.32), calls=%async_computation.1 | async-start | bytes 786432 | tf_op jit(solution)/shard_map/all_to_all | solution.py:644
  95.6 1.3 add_convert_fusion
  97.0 1.6 %collective-permute-start.13 = (bf16[2,64,1536]{2,1,0:T(8,128)(2,1)S(1)}, bf16[2,64,1536]{2,1,0:T(8,128)(2,1)S(1)}, u32[]{:S(2)}, u32[]{:S(2)}) collective-permute-start(bf16[2,64,1536]{2,1,0:T(8,128)(2,1)S(1)} %slice.61), channel_id=1, source_target_pairs={{0,16},{4,20},{8,24},{12,28},{16,0},{20,4},{24,8},{28,12},{1,17},{... | collective-permute-start | bytes 1179656 | tf_op jit(solution)/shard_map/ppermute | solution.py:524
  98.6 1.3 add_convert_fusion.1
  100.0 1.5 %collective-permute-start.10 = (bf16[2,64,1536]{2,1,0:T(8,128)(2,1)S(1)}, bf16[2,64,1536]{2,1,0:T(8,128)(2,1)S(1)}, u32[]{:S(2)}, u32[]{:S(2)}) collective-permute-start(bf16[2,64,1536]{2,1,0:T(8,128)(2,1)S(1)} %slice.57), channel_id=1, source_target_pairs={{0,8},{4,12},{8,0},{12,4},{16,24},{20,28},{24,16},{28,20},{1,9},{5... | collective-permute-start | bytes 1179656 | tf_op jit(solution)/shard_map/ppermute | solution.py:524
  101.5 9.9 %collective-permute-done.13 = bf16[2,64,1536]{2,1,0:T(8,128)(2,1)S(1)} collective-permute-done((bf16[2,64,1536]{2,1,0:T(8,128)(2,1)S(1)}, bf16[2,64,1536]{2,1,0:T(8,128)(2,1)S(1)}, u32[]{:S(2)}, u32[]{:S(2)}) %collective-permute-start.13) | collective-permute-done | bytes 393248 | tf_op jit(solution)/shard_map/ppermute | solution.py:524
  112.2 1.2 collective-permute-start.14
  115.0 3.8 %collective-permute-done.14 = bf16[1,64,1536]{2,1,0:T(8,128)(2,1)S(1)} collective-permute-done((bf16[1,64,1536]{2,1,0:T(8,128)(2,1)S(1)}, bf16[1,64,1536]{2,1,0:T(8,128)(2,1)S(1)}, u32[]{:S(2)}, u32[]{:S(2)}) %collective-permute-start.14) | collective-permute-done | bytes 196640 | tf_op jit(solution)/shard_map/ppermute | solution.py:524
  118.8 1.6 %collective-permute-done.11 = bf16[1,64,1536]{2,1,0:T(8,128)(2,1)S(1)} collective-permute-done((bf16[1,64,1536]{2,1,0:T(8,128)(2,1)S(1)}, bf16[1,64,1536]{2,1,0:T(8,128)(2,1)S(1)}, u32[]{:S(2)}, u32[]{:S(2)}) %collective-permute-start.11) | collective-permute-done | bytes 196640 | tf_op jit(solution)/shard_map/ppermute | solution.py:524
  121.1 2.1 %split.1 = (bf16[64,768]{1,0:T(8,128)(2,1)}, bf16[64,768]{1,0:T(8,128)(2,1)}, bf16[64,768]{1,0:T(8,128)(2,1)}, bf16[64,768]{1,0:T(8,128)(2,1)}) custom-call(s32[3]{0:T(128)} %pad_add_fusion.refs_0_.me_ref, bf16[64,1536]{1,0:T(8,128)(2,1)} %get-tuple-element.51.ka_ref, bf16[64,1536]{1,0:T(8,128)(2,1)} %bitcast.23, bf16[64,1536]{1,0:T(8,128)(2,1)} %get-tuple-element.49.kb_ref, ...), custom_call_target="tpu_custom_call" | custom-call | tf_op jit(solution)/shard_map/split/pallas_call | solution.py:648
  123.2 1.2 collective-permute-start.15
  124.5 2.7 %collective-permute-start.16 = (bf16[64,768]{1,0:T(8,128)(2,1)}, bf16[64,768]{1,0:T(8,128)(2,1)S(1)}, u32[]{:S(2)}, u32[]{:S(2)}) collective-permute-start(bf16[64,768]{1,0:T(8,128)(2,1)} %get-tuple-element.43), channel_id=1, source_target_pairs={{0,2},{1,3},{2,0},{3,1},{4,6},{5,7},{6,4},{7,5},{8,10},{9,11},{10,... | collective-permute-start | bytes 294920 | tf_op jit(solution)/shard_map/ppermute | solution.py:524
  127.6 1.1 collective-permute-done.15.refs_1_
  128.7 5.4 %collective-permute-done.16.refs_2_ = bf16[64,768]{1,0:T(8,128)(2,1)S(1)} collective-permute-done((bf16[64,768]{1,0:T(8,128)(2,1)}, bf16[64,768]{1,0:T(8,128)(2,1)S(1)}, u32[]{:S(2)}, u32[]{:S(2)}) %collective-permute-start.16) | collective-permute-done | bytes 98336 | tf_op jit(solution)/shard_map/ppermute | solution.py:524
  134.7 1.7 %total.1.refs_0_ = bf16[64,768]{1,0:T(8,128)(2,1)} custom-call(bf16[64,768]{1,0:T(8,128)(2,1)} %get-tuple-element.41.refs_0_, bf16[64,768]{1,0:T(8,128)(2,1)} %copy-done.12, bf16[64,768]{1,0:T(8,128)(2,1)} %copy-done.13, bf16[64,768]{1,0:T(8,128)(2,1)} %copy-done.14), custom_call_target="tpu_custom_call" | custom-call | tf_op jit(solution)/shard_map/total/pallas_call | solution.py:658
  136.5 2.4 %collective-permute-start.20 = (bf16[64,768]{1,0:T(8,128)(2,1)}, bf16[64,768]{1,0:T(8,128)(2,1)S(1)}, u32[]{:S(2)}, u32[]{:S(2)}) collective-permute-start(bf16[64,768]{1,0:T(8,128)(2,1)} %total.1.refs_0_), channel_id=1, source_target_pairs={{0,3},{1,2},{2,1},{3,0},{4,7},{5,6},{6,5},{7,4},{8,11},{9,10},{10,... | collective-permute-start | bytes 294920 | tf_op jit(solution)/shard_map/ppermute | solution.py:524
  139.5 1.3 collective-permute-start.18
  141.6 5.9 %scatter.1 = (bf16[64,12288]{1,0:T(8,128)(2,1)}, bf16[64,12288]{1,0:T(8,128)(2,1)}, bf16[6144,128]{1,0:T(8,128)(2,1)}, bf16[2048,256]{1,0:T(8,128)(2,1)}) custom-call(bf16[32,48,128]{2,1,0:T(8,128)(2,1)} %copy-done.2, f32[384,128]{1,0:T(8,128)} %get-tuple-element.33.refs_1_, f32[128,384]{1,0:T(8,128)} %get-tuple-element.34.refs_2_), custom_call_target="tpu_custom_call" | custom-call | tf_op jit(solution)/shard_map/scatter/pallas_call | solution.py:680
  148.9 2.0 %join.1 = (f32[64,512]{1,0:T(8,128)}, f32[64,2048]{1,0:T(8,128)}, f32[64,512]{1,0:T(8,128)}) custom-call(s32[3]{0:T(128)} %pad_add_fusion.refs_0_.me_ref, bf16[64,768]{1,0:T(8,128)(2,1)} %total.1.refs_0_, bf16[64,768]{1,0:T(8,128)(2,1)} %copy-done.11, bf16[64,768]{1,0:T(8,128)(2,1)} %copy-done.10, bf16[64,768]{1,0:T(8,128)(2,1)} %copy-done.9), custom_call_target="tpu_custom_call" | custom-call | tf_op jit(solution)/shard_map/join/pallas_call | solution.py:667
  (81 shorter events, 16.1 us)
Async XLA Ops:
  0.6 13.2 %copy-start.17 = (s32[2]{0:T(128)S(1)}, s32[2]{0:T(128)}, u32[]{:S(2)}) copy-start(s32[2]{0:T(128)} %param.14) | copy-start | bytes 28
  0.6 13.3 %copy-start.18 = (s32[2]{0:T(128)S(1)}, s32[2]{0:T(128)}, u32[]{:S(2)}) copy-start(s32[2]{0:T(128)} %param.15) | copy-start | bytes 28
  0.7 13.4 %copy-start.16 = (s32[2,384]{1,0:T(2,128)S(1)}, s32[2,384]{1,0:T(2,128)}, u32[]{:S(2)}) copy-start(s32[2,384]{1,0:T(2,128)} %param.13) | copy-start | bytes 9220
  0.7 13.4 %copy-start.15 = (s32[2,384]{1,0:T(2,128)S(1)}, s32[2,384]{1,0:T(2,128)}, u32[]{:S(2)}) copy-start(s32[2,384]{1,0:T(2,128)} %param.12) | copy-start | bytes 9220
  2.4 7.9 %collective-permute-start.6 = (bf16[1,64,1536]{2,1,0:T(8,128)(2,1)S(1)}, bf16[1,64,1536]{2,1,0:T(8,128)(2,1)S(1)}, u32[]{:S(2)}, u32[]{:S(2)}) collective-permute-start(bf16[1,64,1536]{2,1,0:T(8,128)(2,1)S(1)} %maximum_bitcast_fusion), channel_id=1, source_target_pairs={{0,8},{4,12},{8,0},{12,4},{16,24},{20,28},{24,16},{28,20},{1,9},{5... | collective-permute-start | bytes 589832 | tf_op jit(solution)/shard_map/ppermute | solution.py:524
  6.4 6.9 %collective-permute-start.3 = (bf16[1,64,1536]{2,1,0:T(8,128)(2,1)S(1)}, bf16[1,64,1536]{2,1,0:T(8,128)(2,1)S(1)}, u32[]{:S(2)}, u32[]{:S(2)}) collective-permute-start(bf16[1,64,1536]{2,1,0:T(8,128)(2,1)S(1)} %slice_bitcast_fusion.2), channel_id=1, source_target_pairs={{0,16},{4,20},{8,24},{12,28},{16,0},{20,4},{24,8},{28,12},{1,17},{... | collective-permute-start | bytes 589832 | tf_op jit(solution)/shard_map/ppermute | solution.py:524
  10.4 21.7 %collective-permute-start.7 = (bf16[2,64,1536]{2,1,0:T(8,128)(2,1)S(1)}, bf16[2,64,1536]{2,1,0:T(8,128)(2,1)S(1)}, u32[]{:S(2)}, u32[]{:S(2)}) collective-permute-start(bf16[2,64,1536]{2,1,0:T(8,128)(2,1)S(1)} %pad_maximum_fusion.3), channel_id=1, source_target_pairs={{0,16},{4,20},{8,24},{12,28},{16,0},{20,4},{24,8},{28,12},{1,17},{... | collective-permute-start | bytes 1179656 | tf_op jit(solution)/shard_map/ppermute | solution.py:524
  13.4 18.9 %collective-permute-start.4 = (bf16[2,64,1536]{2,1,0:T(8,128)(2,1)S(1)}, bf16[2,64,1536]{2,1,0:T(8,128)(2,1)S(1)}, u32[]{:S(2)}, u32[]{:S(2)}) collective-permute-start(bf16[2,64,1536]{2,1,0:T(8,128)(2,1)S(1)} %pad_maximum_fusion.2), channel_id=1, source_target_pairs={{0,8},{4,12},{8,0},{12,4},{16,24},{20,28},{24,16},{28,20},{1,9},{5... | collective-permute-start | bytes 1179656 | tf_op jit(solution)/shard_map/ppermute | solution.py:524
  27.7 6.4 %collective-permute-start.2 = (s32[16,896]{1,0:T(8,128)}, s32[16,896]{1,0:T(8,128)}, u32[]{:S(2)}, u32[]{:S(2)}) collective-permute-start(s32[16,896]{1,0:T(8,128)} %reshape.17.refs_1_), channel_id=1, source_target_pairs={{0,3},{1,2},{2,1},{3,0},{4,7},{5,6},{6,5},{7,4},{8,11},{9,10},{10,... | collective-permute-start | bytes 172040 | tf_op jit(solution)/shard_map/ppermute | solution.py:524
  31.3 5.7 %collective-permute-start.1 = (s32[16,896]{1,0:T(8,128)}, s32[16,896]{1,0:T(8,128)}, u32[]{:S(2)}, u32[]{:S(2)}) collective-permute-start(s32[16,896]{1,0:T(8,128)} %reshape.17.refs_1_), channel_id=1, source_target_pairs={{0,2},{1,3},{2,0},{3,1},{4,6},{5,7},{6,4},{7,5},{8,10},{9,11},{10,... | collective-permute-start | bytes 172040 | tf_op jit(solution)/shard_map/ppermute | solution.py:524
  31.3 5.7 %collective-permute-start = (s32[16,896]{1,0:T(8,128)}, s32[16,896]{1,0:T(8,128)}, u32[]{:S(2)}, u32[]{:S(2)}) collective-permute-start(s32[16,896]{1,0:T(8,128)} %reshape.17.refs_1_), channel_id=1, source_target_pairs={{0,1},{1,0},{2,3},{3,2},{4,5},{5,4},{6,7},{7,6},{8,9},{9,8},{10,11... | collective-permute-start | bytes 172040 | tf_op jit(solution)/shard_map/ppermute | solution.py:524
  32.2 12.8 %copy-start = (bf16[4,64,1536]{2,1,0:T(8,128)(2,1)}, bf16[4,64,1536]{2,1,0:T(8,128)(2,1)S(1)}, u32[]{:S(2)}) copy-start(bf16[4,64,1536]{2,1,0:T(8,128)(2,1)S(1)} %pad_maximum_fusion.1.refs_7_) | copy-start | bytes 2359300
  32.2 28.5 %collective-permute-start.8 = (bf16[4,64,1536]{2,1,0:T(8,128)(2,1)S(1)}, bf16[4,64,1536]{2,1,0:T(8,128)(2,1)S(1)}, u32[]{:S(2)}, u32[]{:S(2)}) collective-permute-start(bf16[4,64,1536]{2,1,0:T(8,128)(2,1)S(1)} %pad_maximum_fusion.1.refs_7_), channel_id=1, source_target_pairs={{0,4},{4,0},{8,12},{12,8},{16,20},{20,16},{24,28},{28,24},{1,5},{5... | collective-permute-start | bytes 2359304 | tf_op jit(solution)/shard_map/ppermute | solution.py:524
  32.4 12.7 %copy-start.1 = (bf16[4,64,1536]{2,1,0:T(8,128)(2,1)}, bf16[4,64,1536]{2,1,0:T(8,128)(2,1)S(1)}, u32[]{:S(2)}) copy-start(bf16[4,64,1536]{2,1,0:T(8,128)(2,1)S(1)} %pad_maximum_fusion.refs_5_) | copy-start | bytes 2359300
  32.4 28.3 %collective-permute-start.5 = (bf16[4,64,1536]{2,1,0:T(8,128)(2,1)S(1)}, bf16[4,64,1536]{2,1,0:T(8,128)(2,1)S(1)}, u32[]{:S(2)}, u32[]{:S(2)}) collective-permute-start(bf16[4,64,1536]{2,1,0:T(8,128)(2,1)S(1)} %pad_maximum_fusion.refs_5_), channel_id=1, source_target_pairs={{0,4},{4,0},{8,12},{12,8},{16,20},{20,16},{24,28},{28,24},{1,5},{5... | collective-permute-start | bytes 2359304 | tf_op jit(solution)/shard_map/ppermute | solution.py:524
  87.9 3.4 %copy-start.3 = (bf16[8,64,1536]{2,1,0:T(8,128)(2,1)S(1)}, bf16[8,64,1536]{2,1,0:T(8,128)(2,1)}, u32[]{:S(2)}) copy-start(bf16[8,64,1536]{2,1,0:T(8,128)(2,1)} %get-tuple-element.39) | copy-start | bytes 4718596
  90.1 5.5 %copy-start.4 = (bf16[8,64,1536]{2,1,0:T(8,128)(2,1)S(1)}, bf16[8,64,1536]{2,1,0:T(8,128)(2,1)}, u32[]{:S(2)}) copy-start(bf16[8,64,1536]{2,1,0:T(8,128)(2,1)} %get-tuple-element.40) | copy-start | bytes 4718596
  90.1 5.5 %collective-permute-start.12 = (bf16[4,64,1536]{2,1,0:T(8,128)(2,1)}, bf16[4,64,1536]{2,1,0:T(8,128)(2,1)}, u32[]{:S(2)}, u32[]{:S(2)}) collective-permute-start(bf16[4,64,1536]{2,1,0:T(8,128)(2,1)} %slice.51), channel_id=1, source_target_pairs={{0,4},{4,0},{8,12},{12,8},{16,20},{20,16},{24,28},{28,24},{1,5},{5... | collective-permute-start | bytes 2359304 | tf_op jit(solution)/shard_map/ppermute | solution.py:524
  92.3 6.3 %collective-permute-start.9 = (bf16[4,64,1536]{2,1,0:T(8,128)(2,1)}, bf16[4,64,1536]{2,1,0:T(8,128)(2,1)}, u32[]{:S(2)}, u32[]{:S(2)}) collective-permute-start(bf16[4,64,1536]{2,1,0:T(8,128)(2,1)} %slice.45), channel_id=1, source_target_pairs={{0,4},{4,0},{8,12},{12,8},{16,20},{20,16},{24,28},{28,24},{1,5},{5... | collective-permute-start | bytes 2359304 | tf_op jit(solution)/shard_map/ppermute | solution.py:524
  92.3 48.6 %all-to-all-start.1 = ((bf16[32,48,128]{2,1,0:T(8,128)(2,1)}), bf16[32,48,128]{2,1,0:T(8,128)(2,1)S(1)}, u32[]{:S(2)}, u32[]{:S(2)}) async-start(bf16[32,48,128]{2,1,0:T(8,128)(2,1)} %get-tuple-element.32), calls=%async_computation.1 | async-start | bytes 786432 | tf_op jit(solution)/shard_map/all_to_all | solution.py:644
  97.0 14.4 %collective-permute-start.13 = (bf16[2,64,1536]{2,1,0:T(8,128)(2,1)S(1)}, bf16[2,64,1536]{2,1,0:T(8,128)(2,1)S(1)}, u32[]{:S(2)}, u32[]{:S(2)}) collective-permute-start(bf16[2,64,1536]{2,1,0:T(8,128)(2,1)S(1)} %slice.61), channel_id=1, source_target_pairs={{0,16},{4,20},{8,24},{12,28},{16,0},{20,4},{24,8},{28,12},{1,17},{... | collective-permute-start | bytes 1179656 | tf_op jit(solution)/shard_map/ppermute | solution.py:524
  100.0 13.3 %collective-permute-start.10 = (bf16[2,64,1536]{2,1,0:T(8,128)(2,1)S(1)}, bf16[2,64,1536]{2,1,0:T(8,128)(2,1)S(1)}, u32[]{:S(2)}, u32[]{:S(2)}) collective-permute-start(bf16[2,64,1536]{2,1,0:T(8,128)(2,1)S(1)} %slice.57), channel_id=1, source_target_pairs={{0,8},{4,12},{8,0},{12,4},{16,24},{20,28},{24,16},{28,20},{1,9},{5... | collective-permute-start | bytes 1179656 | tf_op jit(solution)/shard_map/ppermute | solution.py:524
  112.2 6.7 %collective-permute-start.14 = (bf16[1,64,1536]{2,1,0:T(8,128)(2,1)S(1)}, bf16[1,64,1536]{2,1,0:T(8,128)(2,1)S(1)}, u32[]{:S(2)}, u32[]{:S(2)}) collective-permute-start(bf16[1,64,1536]{2,1,0:T(8,128)(2,1)S(1)} %get-tuple-element.48), channel_id=1, source_target_pairs={{0,8},{4,12},{8,0},{12,4},{16,24},{20,28},{24,16},{28,20},{1,9},{5... | collective-permute-start | bytes 589832 | tf_op jit(solution)/shard_map/ppermute | solution.py:524
  114.1 6.3 %collective-permute-start.11 = (bf16[1,64,1536]{2,1,0:T(8,128)(2,1)S(1)}, bf16[1,64,1536]{2,1,0:T(8,128)(2,1)S(1)}, u32[]{:S(2)}, u32[]{:S(2)}) collective-permute-start(bf16[1,64,1536]{2,1,0:T(8,128)(2,1)S(1)} %get-tuple-element.50), channel_id=1, source_target_pairs={{0,16},{4,20},{8,24},{12,28},{16,0},{20,4},{24,8},{28,12},{1,17},{... | collective-permute-start | bytes 589832 | tf_op jit(solution)/shard_map/ppermute | solution.py:524
  118.8 1.6 %copy-start.7 = (bf16[1,64,1536]{2,1,0:T(8,128)(2,1)}, bf16[1,64,1536]{2,1,0:T(8,128)(2,1)S(1)}, u32[]{:S(2)}) copy-start(bf16[1,64,1536]{2,1,0:T(8,128)(2,1)S(1)} %collective-permute-done.14) | copy-start | bytes 589828
  123.2 5.4 %collective-permute-start.15 = (bf16[64,768]{1,0:T(8,128)(2,1)}, bf16[64,768]{1,0:T(8,128)(2,1)S(1)}, u32[]{:S(2)}, u32[]{:S(2)}) collective-permute-start(bf16[64,768]{1,0:T(8,128)(2,1)} %get-tuple-element.42), channel_id=1, source_target_pairs={{0,1},{1,0},{2,3},{3,2},{4,5},{5,4},{6,7},{7,6},{8,9},{9,8},{10,11... | collective-permute-start | bytes 294920 | tf_op jit(solution)/shard_map/ppermute | solution.py:524
  124.5 9.6 %collective-permute-start.16 = (bf16[64,768]{1,0:T(8,128)(2,1)}, bf16[64,768]{1,0:T(8,128)(2,1)S(1)}, u32[]{:S(2)}, u32[]{:S(2)}) collective-permute-start(bf16[64,768]{1,0:T(8,128)(2,1)} %get-tuple-element.43), channel_id=1, source_target_pairs={{0,2},{1,3},{2,0},{3,1},{4,6},{5,7},{6,4},{7,5},{8,10},{9,11},{10,... | collective-permute-start | bytes 294920 | tf_op jit(solution)/shard_map/ppermute | solution.py:524
  127.1 7.0 %collective-permute-start.17 = (bf16[64,768]{1,0:T(8,128)(2,1)}, bf16[64,768]{1,0:T(8,128)(2,1)S(1)}, u32[]{:S(2)}, u32[]{:S(2)}) collective-permute-start(bf16[64,768]{1,0:T(8,128)(2,1)} %get-tuple-element.44), channel_id=1, source_target_pairs={{0,3},{1,2},{2,1},{3,0},{4,7},{5,6},{6,5},{7,4},{8,11},{9,10},{10,... | collective-permute-start | bytes 294920 | tf_op jit(solution)/shard_map/ppermute | solution.py:524
  128.7 5.4 %copy-start.12 = (bf16[64,768]{1,0:T(8,128)(2,1)}, bf16[64,768]{1,0:T(8,128)(2,1)S(1)}, u32[]{:S(2)}) copy-start(bf16[64,768]{1,0:T(8,128)(2,1)S(1)} %collective-permute-done.15.refs_1_) | copy-start | bytes 294916
  136.5 11.1 %collective-permute-start.20 = (bf16[64,768]{1,0:T(8,128)(2,1)}, bf16[64,768]{1,0:T(8,128)(2,1)S(1)}, u32[]{:S(2)}, u32[]{:S(2)}) collective-permute-start(bf16[64,768]{1,0:T(8,128)(2,1)} %total.1.refs_0_), channel_id=1, source_target_pairs={{0,3},{1,2},{2,1},{3,0},{4,7},{5,6},{6,5},{7,4},{8,11},{9,10},{10,... | collective-permute-start | bytes 294920 | tf_op jit(solution)/shard_map/ppermute | solution.py:524
  138.9 8.7 %collective-permute-start.19 = (bf16[64,768]{1,0:T(8,128)(2,1)}, bf16[64,768]{1,0:T(8,128)(2,1)S(1)}, u32[]{:S(2)}, u32[]{:S(2)}) collective-permute-start(bf16[64,768]{1,0:T(8,128)(2,1)} %total.1.refs_0_), channel_id=1, source_target_pairs={{0,2},{1,3},{2,0},{3,1},{4,6},{5,7},{6,4},{7,5},{8,10},{9,11},{10,... | collective-permute-start | bytes 294920 | tf_op jit(solution)/shard_map/ppermute | solution.py:524
  139.5 8.1 %collective-permute-start.18 = (bf16[64,768]{1,0:T(8,128)(2,1)}, bf16[64,768]{1,0:T(8,128)(2,1)S(1)}, u32[]{:S(2)}, u32[]{:S(2)}) collective-permute-start(bf16[64,768]{1,0:T(8,128)(2,1)} %total.1.refs_0_), channel_id=1, source_target_pairs={{0,1},{1,0},{2,3},{3,2},{4,5},{5,4},{6,7},{7,6},{8,9},{9,8},{10,11... | collective-permute-start | bytes 294920 | tf_op jit(solution)/shard_map/ppermute | solution.py:524
  (9 other events, 6.7 us)
where the time goes:
time: 152 us; the launch traced here: 151 us
  Pallas kernels  45.8 us (30%)
  starting transfers between devices  30.5 us (20%)
  waiting for transfers between devices  28.7 us (19%)
  blocking collectives  28.6 us (19%)
  local copies, waits for them, and re-layouts  11.8 us (8%)
  other arithmetic  4.5 us (3%)
    ppermute x21, waiting for transfers between devices, exchange(): return lax.ppermute(value, axis, [(i, i ^ mask) for i in range(count)])  28.7 us
    ppermute x21, starting transfers between devices, exchange(): return lax.ppermute(value, axis, [(i, i ^ mask) for i in range(count)])  27.2 us
    pallas_call x1, Pallas kernels, shards(): pl.pallas_call(functools.partial(layer_kernel, devices, seq_count, span,...  26.1 us
    all_to_all x1, blocking collectives, shards(): got = lax.all_to_all(send, ('dp', 'table'), 0, 0, tiled=True)  15.6 us
    all_gather x1, blocking collectives, shards(): near = lax.all_gather(packed, 'dp', axis=0, tiled=True)  12.9 us
    pallas_call x1, Pallas kernels, shards(): pl.pallas_call(functools.partial(plan_kernel, planes, devices, seq_count,...  7.96 us
    pallas_call x1, Pallas kernels, shards(): pl.pallas_call(functools.partial(scatter_kernel, devices, capacity, row_c...  5.94 us
    unnamed x39, local copies, waits for them, and re-layouts  5.18 us
  transfers between devices with their start and end apart: 22, of which 9 were waited for; matrix products, arithmetic and copies ran while one was open for 5% of the time, Pallas kernels for 12%

commit v1 on v0

--- a/solution.py
+++ b/solution.py
@@ -50,13 +50,6 @@
         if (index >> place) & 1:
             mask |= 1 << bit
     return mask
-
-
-def place_of(mask, seq):
-    index = 0
-    for place, bit in enumerate(reversed(seq)):
-        index = index | (((mask >> bit) & 1) << place)
-    return index
 
 
 def owner_and_row(items, kinds, row_counts):
@@ -77,9 +70,25 @@
     return owner, rest
 
 
-def plan_kernel(planes, devices, seq_count, span, capacity, row_counts, widths, *refs):
-    me_ref, refs = refs[0], refs[1:]
-    ids_refs, refs = refs[:planes], refs[planes:]
+def key_kernel(devices, row_counts, len_ref, to_ref, item_ref, kind_ref, out_ref):
+    seq_count, span = item_ref.shape
+    keys = item_ref[...]
+    kinds = kind_ref[...]
+    for which in range(3):
+        edge = devices * sum(row_counts[: which + 1])
+        keys = jnp.where(kinds == which + 1, item_ref[...] + edge, keys)
+    lane = iota((1, 128), 1)
+    rows = []
+    for q in range(seq_count):
+        for c in range(span // 128):
+            rows.append(keys[q : q + 1, c * 128 : (c + 1) * 128])
+        rows.append(jnp.where(lane == 0, len_ref[q], jnp.where(lane == 1, to_ref[q], 0)))
+    block = jnp.concatenate(rows, axis=0)
+    out_ref[...] = jnp.broadcast_to(block[None], out_ref.shape)
+
+
+def plan_kernel(devices, seq_count, span, capacity, row_counts, widths, *refs):
+    me_ref, ids_ref, refs = refs[0], refs[1], refs[2:]
     table_refs, refs = refs[:4], refs[4:]
     send_ref, idxc_ref, idxr_ref, info_ref, infot_ref = refs[:5]
     held = refs[5:9]
@@ -91,10 +100,24 @@
     seqs = devices * seq_count
     slots = devices * capacity
     toks = seq_count * span
-    ids = jnp.concatenate([ref[...] for ref in ids_refs], axis=0)
-    items = ids[:, :span]
-    kinds = ids[:, span : 2 * span]
-    tail = ids[:, 2 * span : 2 * span + 128]
+    lanes = ids_ref.shape[1] // seq_count
+    chunks = span // 128
+    keys = jnp.concatenate(
+        [
+            jnp.concatenate([ids_ref[:, q * lanes + c, :] for c in range(chunks)], axis=1)
+            for q in range(seq_count)
+        ],
+        axis=0,
+    )
+    tail = jnp.concatenate(
+        [ids_ref[:, q * lanes + chunks, :] for q in range(seq_count)], axis=0
+    )
+    kinds = jnp.zeros_like(keys)
+    items = keys
+    for which in range(3):
+        edge = devices * sum(row_counts[: which + 1])
+        kinds = kinds + jnp.where(keys >= edge, 1, 0)
+        items = jnp.where(keys >= edge, keys - edge, items)
     lens = tail[:, 0:1]
     target = tail[:, 1:2]
     own_items, own_kinds, own_valid = [], [], []
@@ -231,17 +254,18 @@
 
 
 def layer_kernel(
-    devices, seq_count, span, capacity, widths, dp_count, half, seq_a, seq_b, pieces, *refs
+    devices, planes, seq_count, span, capacity, widths, dp_count, half, seq_a, seq_b, pieces, *refs
 ):
     me_ref, got_ref, info_ref, infot_ref, cot_ref = refs[:5]
     refs = refs[5:]
     a_refs, refs = refs[:pieces], refs[pieces:]
     b_refs, refs = refs[:pieces], refs[pieces:]
-    out_ref, back_ref, ga_ref, gb_ref = refs[:4]
+    out_ref, back_ref, ga_keep, ga_send, gb_keep, gb_send = refs[:6]
     (
         wa, wb, slot_scr, pack_scr, cat_scr, norm_scr, act_scr, slope_scr, attn_scr, tilt_scr,
         att_scr, datt_scr, dproj_scr, gated_scr, og_scr, demb_scr, drow_scr, dact_scr,
-    ) = refs[4:]
+        grad_scr,
+    ) = refs[6:]
     dp = me_ref[1]
     width = out_ref.shape[2]
     slots = devices * capacity
@@ -400,22 +424,26 @@
     lax.fori_loop(0, devices, pack, 0)
     back_ref[...] = pack_scr[...].astype(BF16)
 
-    def emit(grad, target, seq, low):
-        grad = grad.astype(BF16)
-        for chunk in range(dp_count):
-            index = place_of(dp ^ chunk, seq)
-            target[index, :, low : low + width] = grad[
-                chunk * rows_each : (chunk + 1) * rows_each, :
-            ]
+    def emit(grad, low):
+        grad_scr[:, low : low + width] = grad.astype(BF16)
 
     for j in range(4):
-        grad = dot(norm_scr[...], dproj_scr[:, j * width : (j + 1) * width], TN)
-        if j < 3:
-            emit(grad, ga_ref, seq_a, j * width)
-        else:
-            emit(grad, gb_ref, seq_b, 0)
-    emit(dot(gated_scr[...], og_scr[...], TN), gb_ref, seq_b, width)
-    emit(dot(cat_scr[...], demb_scr[...], TN), gb_ref, seq_b, 2 * width)
+        emit(dot(norm_scr[...], dproj_scr[:, j * width : (j + 1) * width], TN), j * width)
+    emit(dot(gated_scr[...], og_scr[...], TN), 4 * width)
+    emit(dot(cat_scr[...], demb_scr[...], TN), 5 * width)
+    middle = dp_count // 2
+    size = 2 * half // planes
+    for part in range(planes):
+        side, slot_at = divmod(part, planes // 2)
+        seq = (seq_a, seq_b)[side]
+        pair = ((ga_keep, ga_send), (gb_keep, gb_send))[side]
+        lanes = pl.ds(pl.multiple_of((me_ref[2] ^ part) * size, 128), size)
+        for index in range(dp_count):
+            chunk = dp ^ mask_of(index, seq)
+            rows = pl.ds(pl.multiple_of(chunk * rows_each, rows_each), rows_each)
+            pair[index // middle][
+                index % middle, :, slot_at * size : (slot_at + 1) * size
+            ] = grad_scr[rows, lanes]
 
 
 def carry_len(q, info_ref, span):
@@ -489,24 +517,6 @@
         copy.wait()
 
 
-def split_kernel(planes, me_ref, ka_ref, ra_ref, kb_ref, rb_ref, *refs):
-    outs, scr = refs[:planes], refs[planes]
-    half = ka_ref.shape[1]
-    scr[:, :half] = (ka_ref[...].astype(F32) + ra_ref[...].astype(F32)).astype(BF16)
-    scr[:, half:] = (kb_ref[...].astype(F32) + rb_ref[...].astype(F32)).astype(BF16)
-    size = outs[0].shape[1]
-    for m in range(planes):
-        at = pl.multiple_of((me_ref[2] ^ m) * size, 128)
-        outs[m][...] = scr[:, pl.ds(at, size)]
-
-
-def sum_kernel(*refs):
-    total = refs[0][...].astype(F32)
-    for ref in refs[1:-1]:
-        total = total + ref[...].astype(F32)
-    refs[-1][...] = total.astype(BF16)
-
-
 def join_kernel(planes, width, me_ref, *refs):
     parts = refs[:planes]
     proj_ref, in_ref, out_ref, scr = refs[planes:]
@@ -524,11 +534,11 @@
     return lax.ppermute(value, axis, [(i, i ^ mask) for i in range(count)])
 
 
-def params():
-    return pltpu.CompilerParams(vmem_limit_bytes=60 * 1024 * 1024)
-
-
-def shards(
+def params(mib):
+    return pltpu.CompilerParams(vmem_limit_bytes=mib * 1024 * 1024)
+
+
+def step(
     item_ids, table_ids, lengths, assignment, table_a, table_b, table_c, table_d,
     proj_weight, in_weight, out_weight, cotangent,
 ):
@@ -552,26 +562,35 @@
     far = list(range(1, dp_bits))
     seq_a = [0] + far
     seq_b = [0] + far[::-1]
+    lanes = span // 128 + 1
+    packed = pl.pallas_call(
+        functools.partial(key_kernel, devices, row_counts),
+        out_shape=jax.ShapeDtypeStruct((devices, seq_count * lanes, 128), jnp.int32),
+        in_specs=[SM, SM, VM, VM],
+        out_specs=VM,
+        compiler_params=params(60),
+        name="key",
+    )(lengths, assignment, item_ids, table_ids)
+    packed, in_weight, out_weight, proj_weight = lax.optimization_barrier(
+        (packed, in_weight, out_weight, proj_weight)
+    )
+    ids = lax.all_to_all(packed, ("dp", "table"), 0, 0, tiled=True)
     own_a = in_weight[:, :half][None]
     own_b = jnp.concatenate([in_weight[:, half:], out_weight, proj_weight], axis=1)[None]
 
-    def gather(own, seq):
-        held = own
-        for bit in seq[:0:-1]:
-            held = jnp.concatenate([held, exchange(held, "dp", 1 << bit)], axis=0)
-        return held, exchange(held, "dp", 1 << seq[0])
-
-    pad = jnp.zeros((seq_count, 126), jnp.int32)
-    packed = jnp.concatenate(
-        [item_ids, table_ids, lengths[:, None], assignment[:, None], pad], axis=1
-    )
-    near = lax.all_gather(packed, "dp", axis=0, tiled=True)
-    ids = [near] + [exchange(near, "table", m) for m in range(1, planes)]
-    wa = gather(own_a, seq_a)
-    wb = gather(own_b, seq_b)
+    def gather(held, taken, seq):
+        bits = seq[:0:-1]
+        for place, bit in enumerate(bits):
+            if place:
+                taken = exchange(held, "dp", 1 << bit)
+            held = jnp.concatenate([held, taken], axis=0)
+        return held
+
+    first_a = exchange(own_a, "dp", 1 << seq_a[-1])
+    first_b = exchange(own_b, "dp", 1 << seq_b[-1])
     send, idxc, idxr, info, infot = pl.pallas_call(
         functools.partial(
-            plan_kernel, planes, devices, seq_count, span, capacity, row_counts, widths
+            plan_kernel, devices, seq_count, span, capacity, row_counts, widths
         ),
         out_shape=(
             jax.ShapeDtypeStruct((devices, 4 * capacity, 128), BF16),
@@ -580,7 +599,7 @@
             jax.ShapeDtypeStruct((8, toks), F32),
             jax.ShapeDtypeStruct((toks, 128), F32),
         ),
-        in_specs=[SM] + [VM] * planes + [HB] * 4,
+        in_specs=[SM, VM] + [HB] * 4,
         out_specs=(VM,) * 5,
         scratch_shapes=[
             pltpu.VMEM((widths[0], row_counts[0]), BF16),
@@ -591,24 +610,28 @@
             pltpu.VMEM((devices, 4 * capacity, 128), F32),
             pltpu.SemaphoreType.DMA((4,)),
         ],
-        compiler_params=params(),
+        compiler_params=params(60),
         name="plan",
-    )(me, *ids, table_a.T, table_b.T, table_c, table_d)
+    )(me, ids, table_a.T, table_b.T, table_c, table_d)
+    send, first_a, first_b = lax.optimization_barrier((send, first_a, first_b))
+    near_a = gather(own_a, first_a, seq_a)
+    near_b = gather(own_b, first_b, seq_b)
     got = lax.all_to_all(send, ("dp", "table"), 0, 0, tiled=True)
+    wa = (near_a, exchange(near_a, "dp", 1 << seq_a[0]))
+    wb = (near_b, exchange(near_b, "dp", 1 << seq_b[0]))
     pieces = len(wa)
-    output, back, grad_a, grad_b = pl.pallas_call(
+    output, back, keep_a, send_a, keep_b, send_b = pl.pallas_call(
         functools.partial(
-            layer_kernel, devices, seq_count, span, capacity, widths, dp_count, half,
+            layer_kernel, devices, planes, seq_count, span, capacity, widths, dp_count, half,
             seq_a, seq_b, pieces,
         ),
         out_shape=(
             jax.ShapeDtypeStruct((seq_count, span, width), BF16),
             jax.ShapeDtypeStruct((devices, 4 * capacity, 128), BF16),
-            jax.ShapeDtypeStruct((dp_count, rows_each, half), BF16),
-            jax.ShapeDtypeStruct((dp_count, rows_each, half), BF16),
-        ),
+        )
+        + (jax.ShapeDtypeStruct((dp_count // 2, rows_each, half), BF16),) * 4,
         in_specs=[SM] + [VM] * (4 + 2 * pieces),
-        out_specs=(VM,) * 4,
+        out_specs=(VM,) * 6,
         scratch_shapes=[
             pltpu.VMEM((width, half), BF16),
             pltpu.VMEM((width, half), BF16),
@@ -628,41 +651,34 @@
             pltpu.VMEM((toks, width), BF16),
             pltpu.VMEM((toks, width), BF16),
             pltpu.VMEM((HEADS, span, span), BF16),
+            pltpu.VMEM((width, 2 * half), BF16),
         ],
-        compiler_params=params(),
+        compiler_params=params(48),
         name="layer",
     )(me, got, info, infot, cotangent, *wa, *wb)
 
-    def halve(held, seq):
+    def halve(keep, send, seq):
         for place, bit in enumerate(seq):
-            mid = held.shape[0] // 2
-            taken = exchange(held[mid:], "dp", 1 << bit)
+            taken = exchange(send, "dp", 1 << bit)
             if place == len(seq) - 1:
-                return held[0], taken[0]
-            held = (held[:mid].astype(F32) + taken.astype(F32)).astype(BF16)
+                return keep[0], taken[0]
+            mid = keep.shape[0] // 2
+            send = (keep[mid:].astype(F32) + taken[mid:].astype(F32)).astype(BF16)
+            keep = (keep[:mid].astype(F32) + taken[:mid].astype(F32)).astype(BF16)
 
     returned = lax.all_to_all(back, ("dp", "table"), 0, 0, tiled=True)
-    kept_a, sent_a = halve(grad_a, seq_a)
-    kept_b, sent_b = halve(grad_b, seq_b)
+    kept_a, sent_a = halve(keep_a, send_a, seq_a)
+    kept_b, sent_b = halve(keep_b, send_b, seq_b)
     size = 2 * half // planes
-    parts = pl.pallas_call(
-        functools.partial(split_kernel, planes),
-        out_shape=(jax.ShapeDtypeStruct((rows_each, size), BF16),) * planes,
-        in_specs=[SM] + [VM] * 4,
-        out_specs=(VM,) * planes,
-        scratch_shapes=[pltpu.VMEM((rows_each, 2 * half), BF16)],
-        compiler_params=params(),
-        name="split",
-    )(me, kept_a, sent_a, kept_b, sent_b)
-    terms = [parts[0]] + [exchange(parts[m], "table", m) for m in range(1, planes)]
-    summed = pl.pallas_call(
-        sum_kernel,
-        out_shape=jax.ShapeDtypeStruct((rows_each, size), BF16),
-        in_specs=[VM] * planes,
-        out_specs=VM,
-        compiler_params=params(),
-        name="total",
-    )(*terms)
+    parts = []
+    for kept, sent in ((kept_a, sent_a), (kept_b, sent_b)):
+        for low in range(0, half, size):
+            cut = slice(low, low + size)
+            parts.append((kept[:, cut].astype(F32) + sent[:, cut].astype(F32)).astype(BF16))
+    total = parts[0].astype(F32)
+    for m in range(1, planes):
+        total = total + exchange(parts[m], "table", m).astype(F32)
+    summed = total.astype(BF16)
     whole = [summed] + [exchange(summed, "table", m) for m in range(1, planes)]
     grad_proj, grad_in, grad_out = pl.pallas_call(
         functools.partial(join_kernel, planes, width),
@@ -674,7 +690,7 @@
         in_specs=[SM] + [VM] * planes,
         out_specs=(VM,) * 3,
         scratch_shapes=[pltpu.VMEM((rows_each, 2 * half), F32)],
-        compiler_params=params(),
+        compiler_params=params(6),
         name="join",
     )(me, *whole)
     g_a, g_b, g_c, g_d = pl.pallas_call(
@@ -696,7 +712,7 @@
             pltpu.VMEM((devices, 4 * capacity, 128), F32),
             pltpu.SemaphoreType.DMA((4,)),
         ],
-        compiler_params=params(),
+        compiler_params=params(26),
         name="scatter",
     )(returned, idxc, idxr)
     return output, g_a.T, g_b.T, g_c, g_d, grad_proj, grad_in, grad_out
@@ -705,7 +721,7 @@
 def solution(mesh):
     both = ("dp", "table")
     return jax.shard_map(
-        shards,
+        step,
         mesh=mesh,
         in_specs=(
             P(both, None), P(both, None), P(both), P(both),

time: 152 us -> 129 us (0.85)
  blocking collectives: 28.6 us -> 14.6 us
  local copies, waits for them, and re-layouts: 11.8 us -> 3.6 us
  Pallas kernels: 45.8 us -> 41.2 us
  waiting for transfers between devices: 28.7 us -> 31.5 us
    all_gather x1 -> x0, blocking collectives: 12.9 us -> none  [shards(): near = lax.all_gather(packed, 'dp', axis=0, tiled=True)]
    all_to_all x1 -> x2, starting transfers between devices: 3.32 us -> 10.7 us  [the longest x1 7.33 us: step(): ids = lax.all_to_all(packed, ('dp', 'table'), 0, 0, tiled=True)]
    ppermute x21 -> x18, starting transfers between devices: 27.2 us -> 21.3 us  [exchange(): return lax.ppermute(value, axis, [(i, i ^ mask) for i in range(count)])]
    pallas_call x6 -> x5, Pallas kernels: 45.8 us -> 41.2 us  [the longest x1 24.7 us: step(): pl.pallas_call(functools.partial(layer_kernel, devices, planes, seq_count...]
    slice x7 -> x1, local copies, waits for them, and re-layouts: 5.45 us -> 0.84 us  [step(): in_weight[:, half:]]
    unnamed x39 -> x22, local copies, waits for them, and re-layouts: 5.18 us -> 1.82 us
    all_to_all x1 -> x2, waiting for transfers between devices: 0.01 us -> 1.83 us  [the longest x1 1.83 us: step(): ids = lax.all_to_all(packed, ('dp', 'table'), 0, 0, tiled=True)]
    ppermute x21 -> x18, waiting for transfers between devices: 28.7 us -> 29.7 us  [exchange(): return lax.ppermute(value, axis, [(i, i ^ mask) for i in range(count)])]
  transfers between devices with their start and end apart: 22 -> 20, of which waited for: 9 -> 8; matrix products, arithmetic and copies ran while one was open for 5% -> 5% of each run, Pallas kernels for 12% -> 11%
where the time goes in v1:
time: 129 us
  Pallas kernels  41.2 us (32%)
  starting transfers between devices  32 us (25%)
  waiting for transfers between devices  31.5 us (24%)
  blocking collectives  14.6 us (11%)
  other arithmetic  4.78 us (4%)
  local copies, waits for them, and re-layouts  3.6 us (3%)
    ppermute x18, waiting for transfers between devices, exchange(): return lax.ppermute(value, axis, [(i, i ^ mask) for i in range(count)])  29.7 us
    pallas_call x1, Pallas kernels, step(): pl.pallas_call(functools.partial(layer_kernel, devices, planes, seq_count...  24.7 us
    ppermute x18, starting transfers between devices, exchange(): return lax.ppermute(value, axis, [(i, i ^ mask) for i in range(count)])  21.3 us
    all_to_all x1, blocking collectives, step(): got = lax.all_to_all(send, ('dp', 'table'), 0, 0, tiled=True)  14.6 us
    pallas_call x1, Pallas kernels, step(): pl.pallas_call(functools.partial(plan_kernel, devices, seq_count, span, c...  7.99 us
    all_to_all x1, starting transfers between devices, step(): ids = lax.all_to_all(packed, ('dp', 'table'), 0, 0, tiled=True)  7.33 us
    pallas_call x1, Pallas kernels, step(): pl.pallas_call(functools.partial(scatter_kernel, devices, capacity, row_c...  5.68 us
    all_to_all x1, starting transfers between devices, step(): returned = lax.all_to_all(back, ('dp', 'table'), 0, 0, tiled=True)  3.34 us
  transfers between devices with their start and end apart: 20, of which 8 were waited for; matrix products, arithmetic and copies ran while one was open for 5% of the time, Pallas kernels for 11%

profile of v1, /device:TPU:0, one launch (start us, length us, event | category | flops | bytes accessed | tf_op | source)
XLA Modules:
  0.0 128.5 jit_solution(5264079092075897847)
XLA Ops:
  0.6 1.4 %key.1 = s32[32,8,128]{2,1,0:T(8,128)} custom-call(s32[2]{0:T(128)} %len_ref.1, s32[2]{0:T(128)} %to_ref.1, s32[2,384]{1,0:T(2,128)} %item_ref.1, s32[2,384]{1,0:T(2,128)} %kind_ref.1), custom_call_target="tpu_custom_call" | custom-call | tf_op jit(solution)/shard_map/key/pallas_call | solution.py:566
  2.0 7.3 %all-to-all-start = ((s32[32,8,128]{2,1,0:T(8,128)}), s32[32,8,128]{2,1,0:T(8,128)S(1)}, u32[]{:S(2)}, u32[]{:S(2)}) async-start(s32[32,8,128]{2,1,0:T(8,128)} %key.1), calls=%async_computation | async-start | bytes 262144 | tf_op jit(solution)/shard_map/all_to_all | solution.py:577
  9.3 0.9 slice_bitcast_fusion
  10.3 1.8 %collective-permute-start = (bf16[1,64,1536]{2,1,0:T(8,128)(2,1)S(1)}, bf16[1,64,1536]{2,1,0:T(8,128)(2,1)S(1)}, u32[]{:S(2)}, u32[]{:S(2)}) collective-permute-start(bf16[1,64,1536]{2,1,0:T(8,128)(2,1)S(1)} %slice_bitcast_fusion), channel_id=1, source_target_pairs={{0,16},{4,20},{8,24},{12,28},{16,0},{20,4},{24,8},{28,12},{1,17},{... | collective-permute-start | bytes 589832 | tf_op jit(solution)/shard_map/ppermute | solution.py:534
  12.1 0.8 slice.79
  13.0 0.9 maximum_bitcast_fusion
  13.9 1.5 %collective-permute-start.1 = (bf16[1,64,1536]{2,1,0:T(8,128)(2,1)S(1)}, bf16[1,64,1536]{2,1,0:T(8,128)(2,1)S(1)}, u32[]{:S(2)}, u32[]{:S(2)}) collective-permute-start(bf16[1,64,1536]{2,1,0:T(8,128)(2,1)S(1)} %maximum_bitcast_fusion), channel_id=1, source_target_pairs={{0,8},{4,12},{8,0},{12,4},{16,24},{20,28},{24,16},{28,20},{1,9},{5... | collective-permute-start | bytes 589832 | tf_op jit(solution)/shard_map/ppermute | solution.py:534
  16.0 1.8 %all-to-all-done.refs_1_ = s32[32,8,128]{2,1,0:T(8,128)S(1)} async-done(((s32[32,8,128]{2,1,0:T(8,128)}), s32[32,8,128]{2,1,0:T(8,128)S(1)}, u32[]{:S(2)}, u32[]{:S(2)}) %all-to-all-start) | async-done | bytes 131104 | tf_op jit(solution)/shard_map/all_to_all | solution.py:577
  18.5 8.0 %plan.1 = (bf16[32,48,128]{2,1,0:T(8,128)(2,1)}, f32[384,128]{1,0:T(8,128)}, f32[128,384]{1,0:T(8,128)}, f32[8,768]{1,0:T(8,128)}, f32[768,128]{1,0:T(8,128)}) custom-call(s32[3]{0:T(128)} %pad_add_fusion.refs_0_.me_ref, s32[32,8,128]{2,1,0:T(8,128)} %copy-done.9, bf16[64,12288]{1,0:T(8,128)(2,1)} %bitcast.17, bf16[64,12288]{1,0:T(8,128)(2,1)} %bitcast.18, ...), custom_call_target="tpu_custom_call" | custom-call | tf_op jit(solution)/shard_map/plan/pallas_call | solution.py:591
  26.6 0.7 collective-permute-start.2
  27.9 8.9 %collective-permute-done.2 = bf16[2,64,1536]{2,1,0:T(8,128)(2,1)S(1)} collective-permute-done((bf16[2,64,1536]{2,1,0:T(8,128)(2,1)S(1)}, bf16[2,64,1536]{2,1,0:T(8,128)(2,1)S(1)}, u32[]{:S(2)}, u32[]{:S(2)}) %collective-permute-start.2) | collective-permute-done | bytes 393248 | tf_op jit(solution)/shard_map/ppermute | solution.py:534
  37.8 14.6 %all_to_all.15.refs_1_ = bf16[32,48,128]{2,1,0:T(8,128)(2,1)S(1)} all-to-all(bf16[32,48,128]{2,1,0:T(8,128)(2,1)S(1)} %copy-done.10), channel_id=1, replica_groups=mesh['dp'=8,'table'=4] {'dp','table'}, dimensions={0} | all-to-all | bytes 786432 | tf_op jit(solution)/shard_map/all_to_all | solution.py:619
  52.4 0.9 copy-done.7
  53.5 24.7 %layer.1 = (bf16[2,384,512]{2,1,0:T(8,128)(2,1)}, bf16[32,48,128]{2,1,0:T(8,128)(2,1)}, bf16[4,64,1536]{2,1,0:T(8,128)(2,1)S(1)}, bf16[4,64,1536]{2,1,0:T(8,128)...) custom-call(s32[3]{0:T(128)S(1)} %copy-done.5, ...), custom_call_target="tpu_custom_call" | custom-call | tf_op jit(solution)/shard_map/layer/pallas_call | solution.py:623
  78.2 1.2 collective-permute-start.6
  79.4 3.3 %all-to-all-start.2 = ((bf16[32,48,128]{2,1,0:T(8,128)(2,1)}), bf16[32,48,128]{2,1,0:T(8,128)(2,1)S(1)}, u32[]{:S(2)}, u32[]{:S(2)}) async-start(bf16[32,48,128]{2,1,0:T(8,128)(2,1)} %get-tuple-element.44), calls=%async_computation.2 | async-start | bytes 786432 | tf_op jit(solution)/shard_map/all_to_all | solution.py:669
  82.7 1.4 %add_convert_fusion.3 = (bf16[2,64,1536]{2,1,0:T(8,128)(2,1)S(1)}, bf16[2,64,1536]{2,1,0:T(8,128)(2,1)S(1)}) fusion(bf16[4,64,1536]{2,1,0:T(8,128)(2,1)} %collective-permute-done.6, bf16[4,64,1536]{2,1,0:T(8,128)(2,1)S(1)} %get-tuple-element.51), kind=kLoop, calls=%fused_computation.5 | loop fusion | flops 1572864 | bytes 2359296 | tf_op jit(solution)/shard_map/convert_element_type | solution.py:667
  84.1 1.6 %collective-permute-start.7 = (bf16[2,64,1536]{2,1,0:T(8,128)(2,1)S(1)}, bf16[2,64,1536]{2,1,0:T(8,128)(2,1)S(1)}, u32[]{:S(2)}, u32[]{:S(2)}) collective-permute-start(bf16[2,64,1536]{2,1,0:T(8,128)(2,1)S(1)} %get-tuple-element.59), channel_id=1, source_target_pairs={{0,8},{4,12},{8,0},{12,4},{16,24},{20,28},{24,16},{28,20},{1,9},{5... | collective-permute-start | bytes 1179656 | tf_op jit(solution)/shard_map/ppermute | solution.py:534
  85.7 1.4 %add_convert_fusion.1 = (bf16[2,64,1536]{2,1,0:T(8,128)(2,1)S(1)}, bf16[2,64,1536]{2,1,0:T(8,128)(2,1)S(1)}) fusion(bf16[4,64,1536]{2,1,0:T(8,128)(2,1)} %collective-permute-done.10, bf16[4,64,1536]{2,1,0:T(8,128)(2,1)S(1)} %get-tuple-element.53), kind=kLoop, calls=%fused_computation.3 | loop fusion | flops 1572864 | bytes 2359296 | tf_op jit(solution)/shard_map/convert_element_type | solution.py:667
  87.1 1.5 %collective-permute-start.11 = (bf16[2,64,1536]{2,1,0:T(8,128)(2,1)S(1)}, bf16[2,64,1536]{2,1,0:T(8,128)(2,1)S(1)}, u32[]{:S(2)}, u32[]{:S(2)}) collective-permute-start(bf16[2,64,1536]{2,1,0:T(8,128)(2,1)S(1)} %get-tuple-element.61), channel_id=1, source_target_pairs={{0,16},{4,20},{8,24},{12,28},{16,0},{20,4},{24,8},{28,12},{1,17},{... | collective-permute-start | bytes 1179656 | tf_op jit(solution)/shard_map/ppermute | solution.py:534
  88.6 9.5 %collective-permute-done.7 = bf16[2,64,1536]{2,1,0:T(8,128)(2,1)S(1)} collective-permute-done((bf16[2,64,1536]{2,1,0:T(8,128)(2,1)S(1)}, bf16[2,64,1536]{2,1,0:T(8,128)(2,1)S(1)}, u32[]{:S(2)}, u32[]{:S(2)}) %collective-permute-start.7) | collective-permute-done | bytes 393248 | tf_op jit(solution)/shard_map/ppermute | solution.py:534
  98.2 1.6 %collective-permute-start.8 = (bf16[1,64,1536]{2,1,0:T(8,128)(2,1)S(1)}, bf16[1,64,1536]{2,1,0:T(8,128)(2,1)S(1)}, u32[]{:S(2)}, u32[]{:S(2)}) collective-permute-start(bf16[1,64,1536]{2,1,0:T(8,128)(2,1)S(1)} %get-tuple-element.63), channel_id=1, source_target_pairs={{0,16},{4,20},{8,24},{12,28},{16,0},{20,4},{24,8},{28,12},{1,17},{... | collective-permute-start | bytes 589832 | tf_op jit(solution)/shard_map/ppermute | solution.py:534
  99.9 1.0 collective-permute-start.12
  101.0 3.8 %collective-permute-done.8 = bf16[1,64,1536]{2,1,0:T(8,128)(2,1)S(1)} collective-permute-done((bf16[1,64,1536]{2,1,0:T(8,128)(2,1)S(1)}, bf16[1,64,1536]{2,1,0:T(8,128)(2,1)S(1)}, u32[]{:S(2)}, u32[]{:S(2)}) %collective-permute-start.8) | collective-permute-done | bytes 196640 | tf_op jit(solution)/shard_map/ppermute | solution.py:534
  104.8 1.4 %collective-permute-start.9 = (bf16[64,768]{1,0:T(8,128)(2,1)S(1)}, bf16[64,768]{1,0:T(8,128)(2,1)S(1)}, u32[]{:S(2)}, u32[]{:S(2)}) collective-permute-start(bf16[64,768]{1,0:T(8,128)(2,1)S(1)} %add_convert_fusion.11), channel_id=1, source_target_pairs={{0,1},{1,0},{2,3},{3,2},{4,5},{5,4},{6,7},{7,6},{8,9},{9,8},{10,11... | collective-permute-start | bytes 294920 | tf_op jit(solution)/shard_map/ppermute | solution.py:534
  106.3 2.8 %collective-permute-start.13 = (bf16[64,768]{1,0:T(8,128)(2,1)S(1)}, bf16[64,768]{1,0:T(8,128)(2,1)S(1)}, u32[]{:S(2)}, u32[]{:S(2)}) collective-permute-start(bf16[64,768]{1,0:T(8,128)(2,1)S(1)} %get-tuple-element.66), channel_id=1, source_target_pairs={{0,2},{1,3},{2,0},{3,1},{4,6},{5,7},{6,4},{7,5},{8,10},{9,11},{10,... | collective-permute-start | bytes 294920 | tf_op jit(solution)/shard_map/ppermute | solution.py:534
  109.1 0.9 collective-permute-start.14
  110.0 6.1 %collective-permute-done.13 = bf16[64,768]{1,0:T(8,128)(2,1)S(1)} collective-permute-done((bf16[64,768]{1,0:T(8,128)(2,1)S(1)}, bf16[64,768]{1,0:T(8,128)(2,1)S(1)}, u32[]{:S(2)}, u32[]{:S(2)}) %collective-permute-start.13) | collective-permute-done | bytes 98336 | tf_op jit(solution)/shard_map/ppermute | solution.py:534
  116.2 3.0 %collective-permute-start.17 = (bf16[64,768]{1,0:T(8,128)(2,1)S(1)}, bf16[64,768]{1,0:T(8,128)(2,1)S(1)}, u32[]{:S(2)}, u32[]{:S(2)}) collective-permute-start(bf16[64,768]{1,0:T(8,128)(2,1)S(1)} %add_convert_fusion.8.refs_0_), channel_id=1, source_target_pairs={{0,3},{1,2},{2,1},{3,0},{4,7},{5,6},{6,5},{7,4},{8,11},{9,10},{10,... | collective-permute-start | bytes 294920 | tf_op jit(solution)/shard_map/ppermute | solution.py:534
  119.6 1.1 collective-permute-start.15
  120.6 5.7 %scatter.1 = (bf16[64,12288]{1,0:T(8,128)(2,1)}, bf16[64,12288]{1,0:T(8,128)(2,1)}, bf16[6144,128]{1,0:T(8,128)(2,1)}, bf16[2048,256]{1,0:T(8,128)(2,1)}) custom-call(bf16[32,48,128]{2,1,0:T(8,128)(2,1)S(1)} %all-to-all-done.2.refs_0_, f32[384,128]{1,0:T(8,128)S(1)} %copy-done.2, f32[128,384]{1,0:T(8,128)S(1)} %copy-done.3), custom_call_target="tpu_custom_call" | custom-call | tf_op jit(solution)/shard_map/scatter/pallas_call | solution.py:696
  127.0 1.5 %join.1 = (f32[64,512]{1,0:T(8,128)}, f32[64,2048]{1,0:T(8,128)}, f32[64,512]{1,0:T(8,128)}) custom-call(s32[3]{0:T(128)S(1)} %copy-done.5, bf16[64,768]{1,0:T(8,128)(2,1)S(1)} %add_convert_fusion.8.refs_0_, bf16[64,768]{1,0:T(8,128)(2,1)S(1)} %collective-permute-done.15.refs_1_, bf16[64,768]{1,0:T(8,128)(2,1)S(1)} %collective-permute-done.16.refs_2_, ...), custom_call_target="tpu_custom_call" | custom-call | tf_op jit(solution)/shard_map/join/pallas_call | solution.py:683
  (51 shorter events, 4.7 us)
Async XLA Ops:
  2.0 15.8 %all-to-all-start = ((s32[32,8,128]{2,1,0:T(8,128)}), s32[32,8,128]{2,1,0:T(8,128)S(1)}, u32[]{:S(2)}, u32[]{:S(2)}) async-start(s32[32,8,128]{2,1,0:T(8,128)} %key.1), calls=%async_computation | async-start | bytes 262144 | tf_op jit(solution)/shard_map/all_to_all | solution.py:577
  10.3 16.2 %collective-permute-start = (bf16[1,64,1536]{2,1,0:T(8,128)(2,1)S(1)}, bf16[1,64,1536]{2,1,0:T(8,128)(2,1)S(1)}, u32[]{:S(2)}, u32[]{:S(2)}) collective-permute-start(bf16[1,64,1536]{2,1,0:T(8,128)(2,1)S(1)} %slice_bitcast_fusion), channel_id=1, source_target_pairs={{0,16},{4,20},{8,24},{12,28},{16,0},{20,4},{24,8},{28,12},{1,17},{... | collective-permute-start | bytes 589832 | tf_op jit(solution)/shard_map/ppermute | solution.py:534
  13.9 12.6 %collective-permute-start.1 = (bf16[1,64,1536]{2,1,0:T(8,128)(2,1)S(1)}, bf16[1,64,1536]{2,1,0:T(8,128)(2,1)S(1)}, u32[]{:S(2)}, u32[]{:S(2)}) collective-permute-start(bf16[1,64,1536]{2,1,0:T(8,128)(2,1)S(1)} %maximum_bitcast_fusion), channel_id=1, source_target_pairs={{0,8},{4,12},{8,0},{12,4},{16,24},{20,28},{24,16},{28,20},{1,9},{5... | collective-permute-start | bytes 589832 | tf_op jit(solution)/shard_map/ppermute | solution.py:534
  17.8 0.7 copy-start.9
  26.6 10.2 %collective-permute-start.2 = (bf16[2,64,1536]{2,1,0:T(8,128)(2,1)S(1)}, bf16[2,64,1536]{2,1,0:T(8,128)(2,1)S(1)}, u32[]{:S(2)}, u32[]{:S(2)}) collective-permute-start(bf16[2,64,1536]{2,1,0:T(8,128)(2,1)S(1)} %pad_maximum_fusion.2), channel_id=1, source_target_pairs={{0,8},{4,12},{8,0},{12,4},{16,24},{20,28},{24,16},{28,20},{1,9},{5... | collective-permute-start | bytes 1179656 | tf_op jit(solution)/shard_map/ppermute | solution.py:534
  27.3 10.4 %copy-start.10 = (bf16[32,48,128]{2,1,0:T(8,128)(2,1)S(1)}, bf16[32,48,128]{2,1,0:T(8,128)(2,1)}, u32[]{:S(2)}) copy-start(bf16[32,48,128]{2,1,0:T(8,128)(2,1)} %get-tuple-element.38) | copy-start | bytes 1179652
  27.3 10.2 %collective-permute-start.4 = (bf16[2,64,1536]{2,1,0:T(8,128)(2,1)S(1)}, bf16[2,64,1536]{2,1,0:T(8,128)(2,1)S(1)}, u32[]{:S(2)}, u32[]{:S(2)}) collective-permute-start(bf16[2,64,1536]{2,1,0:T(8,128)(2,1)S(1)} %pad_maximum_fusion.3), channel_id=1, source_target_pairs={{0,16},{4,20},{8,24},{12,28},{16,0},{20,4},{24,8},{28,12},{1,17},{... | collective-permute-start | bytes 1179656 | tf_op jit(solution)/shard_map/ppermute | solution.py:534
  36.9 16.6 %copy-start = (bf16[2,384,512]{2,1,0:T(8,128)(2,1)S(1)}, bf16[2,384,512]{2,1,0:T(8,128)(2,1)}, u32[]{:S(2)}) copy-start(bf16[2,384,512]{2,1,0:T(8,128)(2,1)} %refs_4_.3) | copy-start | bytes 2359300
  36.9 16.6 %copy-start.1 = (f32[768,128]{1,0:T(8,128)S(1)}, f32[768,128]{1,0:T(8,128)}, u32[]{:S(2)}) copy-start(f32[768,128]{1,0:T(8,128)} %get-tuple-element.40.refs_3_) | copy-start | bytes 1179652
  36.9 16.6 %copy-start.4 = (f32[8,768]{1,0:T(8,128)S(1)}, f32[8,768]{1,0:T(8,128)}, u32[]{:S(2)}) copy-start(f32[8,768]{1,0:T(8,128)} %get-tuple-element.39.refs_2_) | copy-start | bytes 73732
  36.9 16.6 %copy-start.5 = (s32[3]{0:T(128)S(1)}, s32[3]{0:T(128)}, u32[]{:S(2)}) copy-start(s32[3]{0:T(128)} %pad_add_fusion.refs_0_.me_ref) | copy-start | bytes 40
  36.9 15.4 %collective-permute-start.3 = (bf16[4,64,1536]{2,1,0:T(8,128)(2,1)S(1)}, bf16[4,64,1536]{2,1,0:T(8,128)(2,1)S(1)}, u32[]{:S(2)}, u32[]{:S(2)}) collective-permute-start(bf16[4,64,1536]{2,1,0:T(8,128)(2,1)S(1)} %pad_maximum_fusion.refs_5_), channel_id=1, source_target_pairs={{0,4},{4,0},{8,12},{12,8},{16,20},{20,16},{24,28},{28,24},{1,5},{5... | collective-permute-start | bytes 2359304 | tf_op jit(solution)/shard_map/ppermute | solution.py:534
  37.7 14.7 %copy-start.6 = (bf16[4,64,1536]{2,1,0:T(8,128)(2,1)}, bf16[4,64,1536]{2,1,0:T(8,128)(2,1)S(1)}, u32[]{:S(2)}) copy-start(bf16[4,64,1536]{2,1,0:T(8,128)(2,1)S(1)} %pad_maximum_fusion.1.refs_7_) | copy-start | bytes 2359300
  37.7 14.7 %collective-permute-start.5 = (bf16[4,64,1536]{2,1,0:T(8,128)(2,1)S(1)}, bf16[4,64,1536]{2,1,0:T(8,128)(2,1)S(1)}, u32[]{:S(2)}, u32[]{:S(2)}) collective-permute-start(bf16[4,64,1536]{2,1,0:T(8,128)(2,1)S(1)} %pad_maximum_fusion.1.refs_7_), channel_id=1, source_target_pairs={{0,4},{4,0},{8,12},{12,8},{16,20},{20,16},{24,28},{28,24},{1,5},{5... | collective-permute-start | bytes 2359304 | tf_op jit(solution)/shard_map/ppermute | solution.py:534
  52.3 0.9 copy-start.7
  52.4 1.1 copy-start.8
  78.2 4.6 %collective-permute-start.6 = (bf16[4,64,1536]{2,1,0:T(8,128)(2,1)S(1)}, bf16[4,64,1536]{2,1,0:T(8,128)(2,1)}, u32[]{:S(2)}, u32[]{:S(2)}) collective-permute-start(bf16[4,64,1536]{2,1,0:T(8,128)(2,1)S(1)} %get-tuple-element.52), channel_id=1, source_target_pairs={{0,4},{4,0},{8,12},{12,8},{16,20},{20,16},{24,28},{28,24},{1,5},{5... | collective-permute-start | bytes 2359304 | tf_op jit(solution)/shard_map/ppermute | solution.py:534
  79.4 6.3 %collective-permute-start.10 = (bf16[4,64,1536]{2,1,0:T(8,128)(2,1)S(1)}, bf16[4,64,1536]{2,1,0:T(8,128)(2,1)}, u32[]{:S(2)}, u32[]{:S(2)}) collective-permute-start(bf16[4,64,1536]{2,1,0:T(8,128)(2,1)S(1)} %get-tuple-element.54), channel_id=1, source_target_pairs={{0,4},{4,0},{8,12},{12,8},{16,20},{20,16},{24,28},{28,24},{1,5},{5... | collective-permute-start | bytes 2359304 | tf_op jit(solution)/shard_map/ppermute | solution.py:534
  79.4 41.3 %all-to-all-start.2 = ((bf16[32,48,128]{2,1,0:T(8,128)(2,1)}), bf16[32,48,128]{2,1,0:T(8,128)(2,1)S(1)}, u32[]{:S(2)}, u32[]{:S(2)}) async-start(bf16[32,48,128]{2,1,0:T(8,128)(2,1)} %get-tuple-element.44), calls=%async_computation.2 | async-start | bytes 786432 | tf_op jit(solution)/shard_map/all_to_all | solution.py:669
  84.1 14.0 %collective-permute-start.7 = (bf16[2,64,1536]{2,1,0:T(8,128)(2,1)S(1)}, bf16[2,64,1536]{2,1,0:T(8,128)(2,1)S(1)}, u32[]{:S(2)}, u32[]{:S(2)}) collective-permute-start(bf16[2,64,1536]{2,1,0:T(8,128)(2,1)S(1)} %get-tuple-element.59), channel_id=1, source_target_pairs={{0,8},{4,12},{8,0},{12,4},{16,24},{20,28},{24,16},{28,20},{1,9},{5... | collective-permute-start | bytes 1179656 | tf_op jit(solution)/shard_map/ppermute | solution.py:534
  87.1 12.8 %collective-permute-start.11 = (bf16[2,64,1536]{2,1,0:T(8,128)(2,1)S(1)}, bf16[2,64,1536]{2,1,0:T(8,128)(2,1)S(1)}, u32[]{:S(2)}, u32[]{:S(2)}) collective-permute-start(bf16[2,64,1536]{2,1,0:T(8,128)(2,1)S(1)} %get-tuple-element.61), channel_id=1, source_target_pairs={{0,16},{4,20},{8,24},{12,28},{16,0},{20,4},{24,8},{28,12},{1,17},{... | collective-permute-start | bytes 1179656 | tf_op jit(solution)/shard_map/ppermute | solution.py:534
  98.2 22.4 %copy-start.2 = (f32[384,128]{1,0:T(8,128)S(1)}, f32[384,128]{1,0:T(8,128)}, u32[]{:S(2)}) copy-start(f32[384,128]{1,0:T(8,128)} %get-tuple-element.45.refs_1_) | copy-start | bytes 589828
  98.2 22.4 %copy-start.3 = (f32[128,384]{1,0:T(8,128)S(1)}, f32[128,384]{1,0:T(8,128)}, u32[]{:S(2)}) copy-start(f32[128,384]{1,0:T(8,128)} %get-tuple-element.46.refs_2_) | copy-start | bytes 589828
  98.2 6.5 %collective-permute-start.8 = (bf16[1,64,1536]{2,1,0:T(8,128)(2,1)S(1)}, bf16[1,64,1536]{2,1,0:T(8,128)(2,1)S(1)}, u32[]{:S(2)}, u32[]{:S(2)}) collective-permute-start(bf16[1,64,1536]{2,1,0:T(8,128)(2,1)S(1)} %get-tuple-element.63), channel_id=1, source_target_pairs={{0,16},{4,20},{8,24},{12,28},{16,0},{20,4},{24,8},{28,12},{1,17},{... | collective-permute-start | bytes 589832 | tf_op jit(solution)/shard_map/ppermute | solution.py:534
  99.9 6.3 %collective-permute-start.12 = (bf16[1,64,1536]{2,1,0:T(8,128)(2,1)S(1)}, bf16[1,64,1536]{2,1,0:T(8,128)(2,1)S(1)}, u32[]{:S(2)}, u32[]{:S(2)}) collective-permute-start(bf16[1,64,1536]{2,1,0:T(8,128)(2,1)S(1)} %get-tuple-element.65), channel_id=1, source_target_pairs={{0,8},{4,12},{8,0},{12,4},{16,24},{20,28},{24,16},{28,20},{1,9},{5... | collective-permute-start | bytes 589832 | tf_op jit(solution)/shard_map/ppermute | solution.py:534
  104.8 5.2 %collective-permute-start.9 = (bf16[64,768]{1,0:T(8,128)(2,1)S(1)}, bf16[64,768]{1,0:T(8,128)(2,1)S(1)}, u32[]{:S(2)}, u32[]{:S(2)}) collective-permute-start(bf16[64,768]{1,0:T(8,128)(2,1)S(1)} %add_convert_fusion.11), channel_id=1, source_target_pairs={{0,1},{1,0},{2,3},{3,2},{4,5},{5,4},{6,7},{7,6},{8,9},{9,8},{10,11... | collective-permute-start | bytes 294920 | tf_op jit(solution)/shard_map/ppermute | solution.py:534
  106.3 9.8 %collective-permute-start.13 = (bf16[64,768]{1,0:T(8,128)(2,1)S(1)}, bf16[64,768]{1,0:T(8,128)(2,1)S(1)}, u32[]{:S(2)}, u32[]{:S(2)}) collective-permute-start(bf16[64,768]{1,0:T(8,128)(2,1)S(1)} %get-tuple-element.66), channel_id=1, source_target_pairs={{0,2},{1,3},{2,0},{3,1},{4,6},{5,7},{6,4},{7,5},{8,10},{9,11},{10,... | collective-permute-start | bytes 294920 | tf_op jit(solution)/shard_map/ppermute | solution.py:534
  109.1 7.0 %collective-permute-start.14 = (bf16[64,768]{1,0:T(8,128)(2,1)S(1)}, bf16[64,768]{1,0:T(8,128)(2,1)S(1)}, u32[]{:S(2)}, u32[]{:S(2)}) collective-permute-start(bf16[64,768]{1,0:T(8,128)(2,1)S(1)} %get-tuple-element.67), channel_id=1, source_target_pairs={{0,3},{1,2},{2,1},{3,0},{4,7},{5,6},{6,5},{7,4},{8,11},{9,10},{10,... | collective-permute-start | bytes 294920 | tf_op jit(solution)/shard_map/ppermute | solution.py:534
  116.2 10.2 %collective-permute-start.17 = (bf16[64,768]{1,0:T(8,128)(2,1)S(1)}, bf16[64,768]{1,0:T(8,128)(2,1)S(1)}, u32[]{:S(2)}, u32[]{:S(2)}) collective-permute-start(bf16[64,768]{1,0:T(8,128)(2,1)S(1)} %add_convert_fusion.8.refs_0_), channel_id=1, source_target_pairs={{0,3},{1,2},{2,1},{3,0},{4,7},{5,6},{6,5},{7,4},{8,11},{9,10},{10,... | collective-permute-start | bytes 294920 | tf_op jit(solution)/shard_map/ppermute | solution.py:534
  119.2 7.9 %collective-permute-start.16 = (bf16[64,768]{1,0:T(8,128)(2,1)S(1)}, bf16[64,768]{1,0:T(8,128)(2,1)S(1)}, u32[]{:S(2)}, u32[]{:S(2)}) collective-permute-start(bf16[64,768]{1,0:T(8,128)(2,1)S(1)} %add_convert_fusion.8.refs_0_), channel_id=1, source_target_pairs={{0,2},{1,3},{2,0},{3,1},{4,6},{5,7},{6,4},{7,5},{8,10},{9,11},{10,... | collective-permute-start | bytes 294920 | tf_op jit(solution)/shard_map/ppermute | solution.py:534
  119.6 7.5 %collective-permute-start.15 = (bf16[64,768]{1,0:T(8,128)(2,1)S(1)}, bf16[64,768]{1,0:T(8,128)(2,1)S(1)}, u32[]{:S(2)}, u32[]{:S(2)}) collective-permute-start(bf16[64,768]{1,0:T(8,128)(2,1)S(1)} %add_convert_fusion.8.refs_0_), channel_id=1, source_target_pairs={{0,1},{1,0},{2,3},{3,2},{4,5},{5,4},{6,7},{7,6},{8,9},{9,8},{10,11... | collective-permute-start | bytes 294920 | tf_op jit(solution)/shard_map/ppermute | solution.py:534

commit v2 on v1

--- a/solution.py
+++ b/solution.py
@@ -33,10 +33,6 @@
 
 def floor_div(values, by):
     return jnp.floor((values.astype(F32) + 0.5) * (1.0 / by)).astype(jnp.int32)
-
-
-def sigmoid(values):
-    return 0.5 * jnp.tanh(0.5 * values) + 0.5
 
 
 def log2(value):
@@ -87,19 +83,7 @@
     out_ref[...] = jnp.broadcast_to(block[None], out_ref.shape)
 
 
-def plan_kernel(devices, seq_count, span, capacity, row_counts, widths, *refs):
-    me_ref, ids_ref, refs = refs[0], refs[1], refs[2:]
-    table_refs, refs = refs[:4], refs[4:]
-    send_ref, idxc_ref, idxr_ref, info_ref, infot_ref = refs[:5]
-    held = refs[5:9]
-    rows_scr, pack_scr, sems = refs[9:]
-    copies = [pltpu.make_async_copy(table_refs[i], held[i], sems.at[i]) for i in range(4)]
-    for copy in copies:
-        copy.start()
-    me = me_ref[0]
-    seqs = devices * seq_count
-    slots = devices * capacity
-    toks = seq_count * span
+def read_ids(ids_ref, devices, seq_count, span, row_counts):
     lanes = ids_ref.shape[1] // seq_count
     chunks = span // 128
     keys = jnp.concatenate(
@@ -120,6 +104,15 @@
         items = jnp.where(keys >= edge, keys - edge, items)
     lens = tail[:, 0:1]
     target = tail[:, 1:2]
+    return items, kinds, lens, target
+
+
+def own_kernel(devices, seq_count, span, capacity, row_counts, *refs):
+    me_ref, ids_ref, idxc_ref, idxr_ref, info_ref, infot_ref = refs
+    me = me_ref[0]
+    toks = seq_count * span
+    idxr_ref[...] = jnp.transpose(idxc_ref[...], (1, 0))
+    items, kinds, lens, target = read_ids(ids_ref, devices, seq_count, span, row_counts)
     own_items, own_kinds, own_valid = [], [], []
     for q in range(seq_count):
         hit = target == me * seq_count + q
@@ -142,6 +135,21 @@
     infot_ref[...] = jnp.transpose(
         jnp.concatenate([info, jnp.zeros((120, toks), F32)], axis=0), (1, 0)
     )
+
+
+def plan_kernel(devices, seq_count, span, capacity, row_counts, widths, *refs):
+    me_ref, ids_ref, refs = refs[0], refs[1], refs[2:]
+    table_refs, refs = refs[:4], refs[4:]
+    send_ref, idxc_ref = refs[:2]
+    held = refs[2:6]
+    rows_scr, pack_scr, sems = refs[6:]
+    copies = [pltpu.make_async_copy(table_refs[i], held[i], sems.at[i]) for i in range(4)]
+    for copy in copies:
+        copy.start()
+    me = me_ref[0]
+    seqs = devices * seq_count
+    slots = devices * capacity
+    items, kinds, _, target = read_ids(ids_ref, devices, seq_count, span, row_counts)
     owner, row = owner_and_row(items, kinds, row_counts)
     fields = jnp.concatenate(
         [
@@ -156,7 +164,7 @@
     m_kind = moved[:, :span]
     m_row = moved[:, span : 2 * span] * 128.0 + moved[:, 2 * span : 3 * span]
     hits = jnp.concatenate([onehot(m_kind == float(which)) for which in range(4)], axis=0)
-    earlier = before[:span, :span]
+    earlier = onehot(iota((span, span), 0) < iota((span, span), 1))
     ahead = dot(hits, earlier)
     totals = jnp.sum(hits.astype(F32), axis=1, keepdims=True)
     si, sj = iota((seqs, seqs), 0), iota((seqs, seqs), 1)
@@ -196,7 +204,6 @@
         columns = jnp.where(wide == which, high, columns)
         columns = jnp.where(wide == which + 4, low, columns)
     idxc_ref[...] = columns
-    idxr_ref[...] = jnp.transpose(columns, (1, 0))
     for copy in copies:
         copy.wait()
     low_lane = iota((slots, SPLIT), 1)
@@ -254,18 +261,19 @@
 
 
 def layer_kernel(
-    devices, planes, seq_count, span, capacity, widths, dp_count, half, seq_a, seq_b, pieces, *refs
+    devices, seq_count, span, capacity, widths, dp_count, seq_a, seq_b, pieces, *refs
 ):
     me_ref, got_ref, info_ref, infot_ref, cot_ref = refs[:5]
     refs = refs[5:]
     a_refs, refs = refs[:pieces], refs[pieces:]
     b_refs, refs = refs[:pieces], refs[pieces:]
-    out_ref, back_ref, ga_keep, ga_send, gb_keep, gb_send = refs[:6]
+    out_ref, back_ref = refs[:2]
+    pairs, refs = refs[2:6], refs[6:]
     (
         wa, wb, slot_scr, pack_scr, cat_scr, norm_scr, act_scr, slope_scr, attn_scr, tilt_scr,
         att_scr, datt_scr, dproj_scr, gated_scr, og_scr, demb_scr, drow_scr, dact_scr,
-        grad_scr,
-    ) = refs[6:]
+        grad_scr, cot_scr, out_scr, back_scr, w_sems, io_sems,
+    ) = refs
     dp = me_ref[1]
     width = out_ref.shape[2]
     slots = devices * capacity
@@ -273,14 +281,21 @@
     rows_each = width // dp_count
     head_dim = width // HEADS
     scale = head_dim**-0.5
-    for refs_in, held, seq in ((a_refs, wa, seq_a), (b_refs, wb, seq_b)):
+    fetches = []
+    for refs_in, held, seq in ((b_refs, wb, seq_b), (a_refs, wa, seq_a)):
         index = 0
         for ref in refs_in:
             for k in range(ref.shape[0]):
-                chunk = dp ^ mask_of(index, seq)
-                start = pl.multiple_of(chunk * rows_each, rows_each)
-                held[pl.ds(start, rows_each), :] = ref[k]
+                start = pl.multiple_of((dp ^ mask_of(index, seq)) * rows_each, rows_each)
+                fetches.append(
+                    pltpu.make_async_copy(
+                        ref.at[k], held.at[pl.ds(start, rows_each), :], w_sems.at[len(fetches)]
+                    )
+                )
                 index += 1
+    fetches.append(pltpu.make_async_copy(cot_ref, cot_scr, io_sems.at[0]))
+    for copy in fetches:
+        copy.start()
     pack_scr[...] = got_ref[...].astype(F32)
 
     def unpack(device, carry):
@@ -303,6 +318,12 @@
         edge += widths[which]
         kind_of_lane = kind_of_lane + jnp.where(lane >= edge, 1, 0)
     blocks = span // 128
+    heads = [slice(head * head_dim, (head + 1) * head_dim) for head in range(HEADS)]
+    for copy in fetches:
+        copy.wait()
+
+    def out_copy(q):
+        return pltpu.make_async_copy(out_scr.at[q], out_ref.at[q], io_sems.at[2 + q])
 
     def sequence(q, carry):
         base = pl.multiple_of(q * span, span)
@@ -310,6 +331,7 @@
         slot = infot_ref[rows, 0:1].astype(jnp.int32)
         kind = infot_ref[rows, 1:2].astype(jnp.int32)
         valid = infot_ref[rows, 2:3]
+        length = carry_len(q, info_ref, span)
         chosen = onehot(iota((span, slots), 1) == slot)
         cat = jnp.where(kind_of_lane == kind, dot(chosen, arrived), 0.0).astype(BF16)
         cat_scr[rows, :] = cat
@@ -318,31 +340,45 @@
         inv = lax.rsqrt(jnp.mean(centred * centred, axis=1, keepdims=True) + 1e-05)
         normed = centred * inv
         norm_scr[rows, :] = normed.astype(BF16)
-        for j in range(4):
-            mixed = dot(norm_scr[rows, :], in_part(j))
-            sig = sigmoid(mixed)
-            part = mixed * sig
+        for j in (2, 3, 1, 0):
+            lean = dot(norm_scr[rows, :], in_part(j)) * 0.5
+            twice = jnp.tanh(lean) + 1.0
+            part = lean * twice
             act_scr[j] = part.astype(BF16)
-            slope_scr[j] = sig + part * (1.0 - sig)
-        for head in range(HEADS):
-            cols = slice(head * head_dim, (head + 1) * head_dim)
-            for rb in range(blocks):
-                keys = (rb + 1) * 128
-                here = slice(rb * 128, keys)
-                scores = dot(act_scr[2, here, cols], act_scr[3, :keys, cols], NT) * scale
-                key_pos = iota((128, keys), 1)
-                keep = (key_pos <= iota((128, keys), 0) + rb * 128) & (
-                    key_pos < carry_len(q, info_ref, span)
-                )
-                sig = sigmoid(scores)
-                attn = scores * sig
-                attn_scr[head, here, :keys] = jnp.where(keep, attn, 0.0).astype(BF16)
-                tilt_scr[head, here, :keys] = jnp.where(
-                    keep, (sig + attn * (1.0 - sig)) * scale, 0.0
-                )
-                att_scr[here, cols] = dot(
-                    attn_scr[head, here, :keys], act_scr[1, :keys, cols]
-                )
+            slope_scr[j] = twice + part * (2.0 - twice)
+        order = [(rb, head) for rb in range(blocks) for head in range(HEADS)]
+
+        def scores_of(rb, head):
+            keys = (rb + 1) * 128
+            return dot(
+                act_scr[2, rb * 128 : keys, heads[head]], act_scr[3, :keys, heads[head]], NT
+            )
+
+        def attend(rb, head):
+            keys = (rb + 1) * 128
+            here = slice(rb * 128, keys)
+            att_scr[here, heads[head]] = dot(
+                attn_scr[head, here, :keys], act_scr[1, :keys, heads[head]]
+            )
+
+        ahead = [scores_of(*order[0]), scores_of(*order[1])]
+        for step, (rb, head) in enumerate(order):
+            keys = (rb + 1) * 128
+            here = slice(rb * 128, keys)
+            if step + 2 < len(order):
+                ahead.append(scores_of(*order[step + 2]))
+            lean = ahead.pop(0) * (0.5 * scale)
+            twice = jnp.tanh(lean) + 1.0
+            attn = lean * twice
+            key_pos = iota((128, keys), 1)
+            keep = (key_pos <= iota((128, keys), 0) + rb * 128) & (key_pos < length)
+            attn_scr[head, here, :keys] = jnp.where(keep, attn, 0.0).astype(BF16)
+            tilt_scr[head, here, :keys] = jnp.where(
+                keep, (twice + attn * (2.0 - twice)) * (0.5 * scale), 0.0
+            )
+            if step:
+                attend(*order[step - 1])
+        attend(*order[-1])
         attended = att_scr[...]
         att_c = attended - jnp.mean(attended, axis=1, keepdims=True)
         att_inv = lax.rsqrt(jnp.mean(att_c * att_c, axis=1, keepdims=True) + 1e-05)
@@ -351,10 +387,11 @@
         gated = (att_n * gate).astype(BF16)
         gated_scr[rows, :] = gated
         out_w = wb[:, width : 2 * width]
-        out_ref[q] = (emb + dot(gated, out_w)).astype(BF16)
-        og = jnp.where(valid > 0.5, cot_ref[q].astype(F32), 0.0).astype(BF16)
+        og = jnp.where(valid > 0.5, cot_scr[q].astype(F32), 0.0).astype(BF16)
         og_scr[rows, :] = og
         d_gated = dot(og, out_w, NT).astype(BF16).astype(F32)
+        out_scr[q] = (emb + dot(gated, out_w)).astype(BF16)
+        out_copy(q).start()
         d_gate = (d_gated * att_n).astype(BF16).astype(F32)
         dproj_scr[rows, :width] = (d_gate * slope_scr[0]).astype(BF16)
         d_n = d_gated * gate
@@ -364,39 +401,48 @@
             - att_n * jnp.mean(d_n * att_n, axis=1, keepdims=True)
         )
         datt_scr[...] = d_att.astype(BF16)
-        for head in range(HEADS):
-            cols = slice(head * head_dim, (head + 1) * head_dim)
-            for rb in range(blocks):
-                keys = (rb + 1) * 128
-                here = slice(rb * 128, keys)
-                d_attn = dot(datt_scr[here, cols], act_scr[1, :keys, cols], NT)
-                d_attn = d_attn.astype(BF16).astype(F32)
-                tilt = (d_attn * tilt_scr[head, here, :keys]).astype(BF16)
-                dact_scr[head, here, :keys] = tilt
-                d_query = dot(tilt, act_scr[3, :keys, cols]).astype(BF16).astype(F32)
-                low = 2 * width + head * head_dim
-                dproj_scr[pl.ds(base + rb * 128, 128), low : low + head_dim] = (
-                    d_query * slope_scr[2, here, cols]
-                ).astype(BF16)
-            for kb in range(blocks):
-                here = slice(kb * 128, (kb + 1) * 128)
-                rest = slice(kb * 128, span)
-                d_value = dot(attn_scr[head, rest, here], datt_scr[rest, cols], TN)
-                d_key = dot(dact_scr[head, rest, here], act_scr[2, rest, cols], TN)
-                low = width + head * head_dim
-                dproj_scr[pl.ds(base + kb * 128, 128), low : low + head_dim] = (
-                    d_value.astype(BF16).astype(F32) * slope_scr[1, here, cols]
-                ).astype(BF16)
-                low = 3 * width + head * head_dim
-                dproj_scr[pl.ds(base + kb * 128, 128), low : low + head_dim] = (
-                    d_key.astype(BF16).astype(F32) * slope_scr[3, here, cols]
-                ).astype(BF16)
+        order = [(rb, head) for rb in reversed(range(blocks)) for head in range(HEADS)]
+
+        def d_attn_of(rb, head):
+            keys = (rb + 1) * 128
+            return dot(
+                datt_scr[rb * 128 : keys, heads[head]], act_scr[1, :keys, heads[head]], NT
+            )
+
+        def put(which, rb, head, grad):
+            here = slice(rb * 128, (rb + 1) * 128)
+            low = which * width + head * head_dim
+            dproj_scr[pl.ds(base + rb * 128, 128), low : low + head_dim] = (
+                grad.astype(BF16).astype(F32) * slope_scr[which, here, heads[head]]
+            ).astype(BF16)
+
+        def settle(rb, head):
+            keys = (rb + 1) * 128
+            here = slice(rb * 128, keys)
+            rest = slice(rb * 128, span)
+            cols = heads[head]
+            put(2, rb, head, dot(dact_scr[head, here, :keys], act_scr[3, :keys, cols]))
+            put(3, rb, head, dot(dact_scr[head, rest, here], act_scr[2, rest, cols], TN))
+
+        ahead = [d_attn_of(*order[0]), d_attn_of(*order[1])]
+        for step, (rb, head) in enumerate(order):
+            keys = (rb + 1) * 128
+            here = slice(rb * 128, keys)
+            rest = slice(rb * 128, span)
+            if step + 2 < len(order):
+                ahead.append(d_attn_of(*order[step + 2]))
+            put(1, rb, head, dot(attn_scr[head, rest, here], datt_scr[rest, heads[head]], TN))
+            d_attn = ahead.pop(0).astype(BF16).astype(F32)
+            dact_scr[head, here, :keys] = (d_attn * tilt_scr[head, here, :keys]).astype(BF16)
+            if step:
+                settle(*order[step - 1])
+        settle(*order[-1])
         d_normed = jnp.zeros((span, width), F32)
-        for j in range(4):
+        for j in (0, 1, 2, 3):
             d_normed = d_normed + dot(
                 dproj_scr[rows, j * width : (j + 1) * width], in_part(j), NT
             )
-        d_normed = d_normed.astype(BF16).astype(F32)
+        d_normed = (d_normed * 0.5).astype(BF16).astype(F32)
         d_emb = inv * (
             d_normed
             - jnp.mean(d_normed, axis=1, keepdims=True)
@@ -422,28 +468,29 @@
         return carry
 
     lax.fori_loop(0, devices, pack, 0)
-    back_ref[...] = pack_scr[...].astype(BF16)
-
-    def emit(grad, low):
-        grad_scr[:, low : low + width] = grad.astype(BF16)
+    back_scr[...] = pack_scr[...].astype(BF16)
+    back_copy = pltpu.make_async_copy(back_scr, back_ref, io_sems.at[1])
+    back_copy.start()
+    middle = dp_count // 2
+
+    def emit(block, grad):
+        side, place = divmod(block, 3)
+        grad_scr[block] = grad.astype(BF16)
+        for index in range(dp_count):
+            chunk = dp ^ mask_of(index, (seq_a, seq_b)[side])
+            rows = pl.ds(pl.multiple_of(chunk * rows_each, rows_each), rows_each)
+            pairs[2 * side + index // middle][
+                index % middle, :, place * width : (place + 1) * width
+            ] = grad_scr[block, rows, :]
 
     for j in range(4):
-        emit(dot(norm_scr[...], dproj_scr[:, j * width : (j + 1) * width], TN), j * width)
-    emit(dot(gated_scr[...], og_scr[...], TN), 4 * width)
-    emit(dot(cat_scr[...], demb_scr[...], TN), 5 * width)
-    middle = dp_count // 2
-    size = 2 * half // planes
-    for part in range(planes):
-        side, slot_at = divmod(part, planes // 2)
-        seq = (seq_a, seq_b)[side]
-        pair = ((ga_keep, ga_send), (gb_keep, gb_send))[side]
-        lanes = pl.ds(pl.multiple_of((me_ref[2] ^ part) * size, 128), size)
-        for index in range(dp_count):
-            chunk = dp ^ mask_of(index, seq)
-            rows = pl.ds(pl.multiple_of(chunk * rows_each, rows_each), rows_each)
-            pair[index // middle][
-                index % middle, :, slot_at * size : (slot_at + 1) * size
-            ] = grad_scr[rows, lanes]
+        grad = dot(norm_scr[...], dproj_scr[:, j * width : (j + 1) * width], TN)
+        emit(j, grad * 0.5)
+    emit(4, dot(gated_scr[...], og_scr[...], TN))
+    emit(5, dot(cat_scr[...], demb_scr[...], TN))
+    for q in range(seq_count):
+        out_copy(q).wait()
+    back_copy.wait()
 
 
 def carry_len(q, info_ref, span):
@@ -588,19 +635,16 @@
 
     first_a = exchange(own_a, "dp", 1 << seq_a[-1])
     first_b = exchange(own_b, "dp", 1 << seq_b[-1])
-    send, idxc, idxr, info, infot = pl.pallas_call(
+    send, idxc = pl.pallas_call(
         functools.partial(
             plan_kernel, devices, seq_count, span, capacity, row_counts, widths
         ),
         out_shape=(
             jax.ShapeDtypeStruct((devices, 4 * capacity, 128), BF16),
             jax.ShapeDtypeStruct((slots, 128), F32),
-            jax.ShapeDtypeStruct((128, slots), F32),
-            jax.ShapeDtypeStruct((8, toks), F32),
-            jax.ShapeDtypeStruct((toks, 128), F32),
         ),
         in_specs=[SM, VM] + [HB] * 4,
-        out_specs=(VM,) * 5,
+        out_specs=(VM,) * 2,
         scratch_shapes=[
             pltpu.VMEM((widths[0], row_counts[0]), BF16),
             pltpu.VMEM((widths[1], row_counts[1]), BF16),
@@ -619,19 +663,31 @@
     got = lax.all_to_all(send, ("dp", "table"), 0, 0, tiled=True)
     wa = (near_a, exchange(near_a, "dp", 1 << seq_a[0]))
     wb = (near_b, exchange(near_b, "dp", 1 << seq_b[0]))
+    idxr, info, infot = pl.pallas_call(
+        functools.partial(own_kernel, devices, seq_count, span, capacity, row_counts),
+        out_shape=(
+            jax.ShapeDtypeStruct((128, slots), F32),
+            jax.ShapeDtypeStruct((8, toks), F32),
+            jax.ShapeDtypeStruct((toks, 128), F32),
+        ),
+        in_specs=[SM, VM, VM],
+        out_specs=(VM,) * 3,
+        compiler_params=params(16),
+        name="own",
+    )(me, ids, idxc)
     pieces = len(wa)
-    output, back, keep_a, send_a, keep_b, send_b = pl.pallas_call(
+    output, back, *pairs = pl.pallas_call(
         functools.partial(
-            layer_kernel, devices, planes, seq_count, span, capacity, widths, dp_count, half,
-            seq_a, seq_b, pieces,
+            layer_kernel, devices, seq_count, span, capacity, widths, dp_count, seq_a, seq_b,
+            pieces,
         ),
         out_shape=(
             jax.ShapeDtypeStruct((seq_count, span, width), BF16),
             jax.ShapeDtypeStruct((devices, 4 * capacity, 128), BF16),
         )
         + (jax.ShapeDtypeStruct((dp_count // 2, rows_each, half), BF16),) * 4,
-        in_specs=[SM] + [VM] * (4 + 2 * pieces),
-        out_specs=(VM,) * 6,
+        in_specs=[SM] + [VM] * 3 + [HB] * (1 + 2 * pieces),
+        out_specs=(HB, HB) + (VM,) * 4,
         scratch_shapes=[
             pltpu.VMEM((width, half), BF16),
             pltpu.VMEM((width, half), BF16),
@@ -651,35 +707,43 @@
             pltpu.VMEM((toks, width), BF16),
             pltpu.VMEM((toks, width), BF16),
             pltpu.VMEM((HEADS, span, span), BF16),
-            pltpu.VMEM((width, 2 * half), BF16),
+            pltpu.VMEM((6, width, width), BF16),
+            pltpu.VMEM((seq_count, span, width), BF16),
+            pltpu.VMEM((seq_count, span, width), BF16),
+            pltpu.VMEM((devices, 4 * capacity, 128), BF16),
+            pltpu.SemaphoreType.DMA((2 * dp_count,)),
+            pltpu.SemaphoreType.DMA((2 + seq_count,)),
         ],
         compiler_params=params(48),
         name="layer",
     )(me, got, info, infot, cotangent, *wa, *wb)
 
-    def halve(keep, send, seq):
+    size = 2 * half // planes
+
+    def add(left, right):
+        return (left.astype(F32) + right.astype(F32)).astype(BF16)
+
+    returned = lax.all_to_all(back, ("dp", "table"), 0, 0, tiled=True)
+    parts = []
+    for side, seq in enumerate((seq_a, seq_b)):
+        keep, send = pairs[2 * side], pairs[2 * side + 1]
         for place, bit in enumerate(seq):
             taken = exchange(send, "dp", 1 << bit)
-            if place == len(seq) - 1:
-                return keep[0], taken[0]
-            mid = keep.shape[0] // 2
-            send = (keep[mid:].astype(F32) + taken[mid:].astype(F32)).astype(BF16)
-            keep = (keep[:mid].astype(F32) + taken[:mid].astype(F32)).astype(BF16)
-
-    returned = lax.all_to_all(back, ("dp", "table"), 0, 0, tiled=True)
-    kept_a, sent_a = halve(keep_a, send_a, seq_a)
-    kept_b, sent_b = halve(keep_b, send_b, seq_b)
-    size = 2 * half // planes
-    parts = []
-    for kept, sent in ((kept_a, sent_a), (kept_b, sent_b)):
+            if place < len(seq) - 1:
+                mid = keep.shape[0] // 2
+                send = add(keep[mid:], taken[mid:])
+                keep = add(keep[:mid], taken[:mid])
         for low in range(0, half, size):
-            cut = slice(low, low + size)
-            parts.append((kept[:, cut].astype(F32) + sent[:, cut].astype(F32)).astype(BF16))
-    total = parts[0].astype(F32)
+            parts.append(add(keep[0, :, low : low + size], taken[0, :, low : low + size]))
+    parts = jnp.stack(parts)
+    own = [lax.dynamic_index_in_dim(parts, plane ^ m, 0, False) for m in range(planes)]
+    total = own[0].astype(F32)
     for m in range(1, planes):
-        total = total + exchange(parts[m], "table", m).astype(F32)
+        total = total + exchange(own[m], "table", m).astype(F32)
     summed = total.astype(BF16)
-    whole = [summed] + [exchange(summed, "table", m) for m in range(1, planes)]
+    whole = [summed]
+    for m in range(1, planes):
+        whole.append(exchange(summed, "table", m))
     grad_proj, grad_in, grad_out = pl.pallas_call(
         functools.partial(join_kernel, planes, width),
         out_shape=(

time: 129 us -> 126 us (0.977)
  blocking collectives: 14.6 us -> 0 us
  waiting for transfers between devices: 31.5 us -> 42.6 us
  Pallas kernels: 41.2 us -> 37.6 us
  starting transfers between devices: 32 us -> 34.6 us
  local copies, waits for them, and re-layouts: 3.6 us -> 5.44 us
    all_to_all x1 -> x0, blocking collectives: 14.6 us -> none  [step(): got = lax.all_to_all(send, ('dp', 'table'), 0, 0, tiled=True)]
    all_to_all x0 -> x1, waiting for transfers between devices: none -> 9.88 us  [step(): got = lax.all_to_all(send, ('dp', 'table'), 0, 0, tiled=True)]
    pallas_call x1 -> x2, Pallas kernels: 24.7 us -> 21.3 us  [the longest x1 20.1 us: step(): pl.pallas_call(functools.partial(layer_kernel, devices, seq_count, span,...]
    all_to_all x0 -> x1, starting transfers between devices: none -> 2.78 us  [step(): got = lax.all_to_all(send, ('dp', 'table'), 0, 0, tiled=True)]
    unnamed x22 -> x18, local copies, waits for them, and re-layouts: 1.82 us -> 3.62 us
    convert_element_type x4 -> x6, other arithmetic: 2.8 us -> 1.85 us  [add(): return (left.astype(F32) + right.astype(F32)).astype(BF16)]
  transfers between devices with their start and end apart: 20 -> 21, of which waited for: 8 -> 8; matrix products, arithmetic and copies ran while one was open for 5% -> 5% of each run, Pallas kernels for 11% -> 12%
where the time goes in v2:
time: 126 us
  waiting for transfers between devices  42.6 us (34%)
  Pallas kernels  37.6 us (30%)
  starting transfers between devices  34.6 us (27%)
  local copies, waits for them, and re-layouts  5.44 us (4%)
  other arithmetic  4.54 us (4%)
    ppermute x18, waiting for transfers between devices, exchange(): return lax.ppermute(value, axis, [(i, i ^ mask) for i in range(count)])  30.8 us
    ppermute x18, starting transfers between devices, exchange(): return lax.ppermute(value, axis, [(i, i ^ mask) for i in range(count)])  21.2 us
    pallas_call x1, Pallas kernels, step(): pl.pallas_call(functools.partial(layer_kernel, devices, seq_count, span,...  20.1 us
    all_to_all x1, waiting for transfers between devices, step(): got = lax.all_to_all(send, ('dp', 'table'), 0, 0, tiled=True)  9.88 us
    pallas_call x1, Pallas kernels, step(): pl.pallas_call(functools.partial(plan_kernel, devices, seq_count, span, c...  7.78 us
    all_to_all x1, starting transfers between devices, step(): ids = lax.all_to_all(packed, ('dp', 'table'), 0, 0, tiled=True)  7.33 us
    pallas_call x1, Pallas kernels, step(): pl.pallas_call(functools.partial(scatter_kernel, devices, capacity, row_c...  5.67 us
    unnamed x18, local copies, waits for them, and re-layouts  3.62 us
  transfers between devices with their start and end apart: 21, of which 8 were waited for; matrix products, arithmetic and copies ran while one was open for 5% of the time, Pallas kernels for 12%

profile of v2, /device:TPU:0, one launch (start us, length us, event | category | flops | bytes accessed | tf_op | source)
XLA Modules:
  0.0 125.7 jit_solution(17280789790682720214)
XLA Ops:
  0.6 1.4 %key.1 = s32[32,8,128]{2,1,0:T(8,128)} custom-call(s32[2]{0:T(128)} %len_ref.1, s32[2]{0:T(128)} %to_ref.1, s32[2,384]{1,0:T(2,128)} %item_ref.1, s32[2,384]{1,0:T(2,128)} %kind_ref.1), custom_call_target="tpu_custom_call" | custom-call | tf_op jit(solution)/shard_map/key/pallas_call | solution.py:613
  2.0 7.3 %all-to-all-start = ((s32[32,8,128]{2,1,0:T(8,128)}), s32[32,8,128]{2,1,0:T(8,128)S(1)}, u32[]{:S(2)}, u32[]{:S(2)}) async-start(s32[32,8,128]{2,1,0:T(8,128)} %key.1), calls=%async_computation | async-start | bytes 262144 | tf_op jit(solution)/shard_map/all_to_all | solution.py:624
  10.2 0.9 maximum_bitcast_fusion
  11.1 1.8 %collective-permute-start.1 = (bf16[1,64,1536]{2,1,0:T(8,128)(2,1)S(1)}, bf16[1,64,1536]{2,1,0:T(8,128)(2,1)S(1)}, u32[]{:S(2)}, u32[]{:S(2)}) collective-permute-start(bf16[1,64,1536]{2,1,0:T(8,128)(2,1)S(1)} %maximum_bitcast_fusion), channel_id=1, source_target_pairs={{0,8},{4,12},{8,0},{12,4},{16,24},{20,28},{24,16},{28,20},{1,9},{5... | collective-permute-start | bytes 589832 | tf_op jit(solution)/shard_map/ppermute | solution.py:581
  12.9 0.9 slice_bitcast_fusion
  13.9 1.5 %collective-permute-start = (bf16[1,64,1536]{2,1,0:T(8,128)(2,1)S(1)}, bf16[1,64,1536]{2,1,0:T(8,128)(2,1)S(1)}, u32[]{:S(2)}, u32[]{:S(2)}) collective-permute-start(bf16[1,64,1536]{2,1,0:T(8,128)(2,1)S(1)} %slice_bitcast_fusion), channel_id=1, source_target_pairs={{0,16},{4,20},{8,24},{12,28},{16,0},{20,4},{24,8},{28,12},{1,17},{... | collective-permute-start | bytes 589832 | tf_op jit(solution)/shard_map/ppermute | solution.py:581
  16.0 1.9 %all-to-all-done.refs_1_ = s32[32,8,128]{2,1,0:T(8,128)S(1)} async-done(((s32[32,8,128]{2,1,0:T(8,128)}), s32[32,8,128]{2,1,0:T(8,128)S(1)}, u32[]{:S(2)}, u32[]{:S(2)}) %all-to-all-start) | async-done | bytes 131104 | tf_op jit(solution)/shard_map/all_to_all | solution.py:624
  18.5 7.8 %plan.1 = (bf16[32,48,128]{2,1,0:T(8,128)(2,1)}, f32[384,128]{1,0:T(8,128)}) custom-call(s32[3]{0:T(128)} %pad_add_fusion.refs_0_.me_ref, s32[32,8,128]{2,1,0:T(8,128)} %copy-done, bf16[64,12288]{1,0:T(8,128)(2,1)} %bitcast.20, bf16[64,12288]{1,0:T(8,128)(2,1)} %bitcast.21, bf16[6144,128]{1,0:T(8,128)(2,1)} %refs_4_.2, bf16[2048,256]{1,0:T(8,128)(2,1)} %refs_5_.1), custom_call_target="tpu_custom_call" | custom-call | tf_op jit(solution)/shard_map/plan/pallas_call | solution.py:638
  27.7 8.9 %collective-permute-done.4 = bf16[2,64,1536]{2,1,0:T(8,128)(2,1)S(1)} collective-permute-done((bf16[2,64,1536]{2,1,0:T(8,128)(2,1)S(1)}, bf16[2,64,1536]{2,1,0:T(8,128)(2,1)S(1)}, u32[]{:S(2)}, u32[]{:S(2)}) %collective-permute-start.4) | collective-permute-done | bytes 393248 | tf_op jit(solution)/shard_map/ppermute | solution.py:581
  36.6 1.0 pad_maximum_fusion.1.refs_7_
  38.3 2.8 %all-to-all-start.1 = ((bf16[32,48,128]{2,1,0:T(8,128)(2,1)}), bf16[32,48,128]{2,1,0:T(8,128)(2,1)S(1)}, u32[]{:S(2)}, u32[]{:S(2)}) async-start(bf16[32,48,128]{2,1,0:T(8,128)(2,1)} %get-tuple-element.38), calls=%async_computation.1 | async-start | bytes 786432 | tf_op jit(solution)/shard_map/all_to_all | solution.py:663
  41.1 1.1 own.1
  42.8 9.9 %all-to-all-done.1.refs_1_ = bf16[32,48,128]{2,1,0:T(8,128)(2,1)S(1)} async-done(((bf16[32,48,128]{2,1,0:T(8,128)(2,1)}), bf16[32,48,128]{2,1,0:T(8,128)(2,1)S(1)}, u32[]{:S(2)}, u32[]{:S(2)}) %all-to-all-start.1) | async-done | bytes 393248 | tf_op jit(solution)/shard_map/all_to_all | solution.py:663
  53.5 20.1 %layer.1 = (bf16[2,384,512]{2,1,0:T(8,128)(2,1)}, bf16[32,48,128]{2,1,0:T(8,128)(2,1)S(1)}, bf16[4,64,1536]{2,1,0:T(8,128)(2,1)S(1)}, bf16[4,64,1536]{2,1,0:T(8,...) custom-call(s32[3]{0:T(128)S(1)} %copy-done.8, ...), custom_call_target="tpu_custom_call" | custom-call | tf_op jit(solution)/shard_map/layer/pallas_call | solution.py:679
  75.2 1.2 collective-permute-start.6
  76.5 3.3 %all-to-all-start.2 = ((bf16[32,48,128]{2,1,0:T(8,128)(2,1)}), bf16[32,48,128]{2,1,0:T(8,128)(2,1)S(1)}, u32[]{:S(2)}, u32[]{:S(2)}) async-start(bf16[32,48,128]{2,1,0:T(8,128)(2,1)} %copy-done.5), calls=%async_computation.2 | async-start | bytes 786432 | tf_op jit(solution)/shard_map/all_to_all | solution.py:726
  79.8 1.4 %add_convert_fusion.3 = (bf16[2,64,1536]{2,1,0:T(8,128)(2,1)S(1)}, bf16[2,64,1536]{2,1,0:T(8,128)(2,1)S(1)}) fusion(bf16[4,64,1536]{2,1,0:T(8,128)(2,1)S(1)} %collective-permute-done.6, bf16[4,64,1536]{2,1,0:T(8,128)(2,1)} %copy-done.4), kind=kLoop, calls=%fused_computation.5 | loop fusion | flops 1572864 | bytes 2359296 | tf_op jit(solution)/shard_map/convert_element_type | solution.py:724
  81.1 1.6 %collective-permute-start.7 = (bf16[2,64,1536]{2,1,0:T(8,128)(2,1)S(1)}, bf16[2,64,1536]{2,1,0:T(8,128)(2,1)S(1)}, u32[]{:S(2)}, u32[]{:S(2)}) collective-permute-start(bf16[2,64,1536]{2,1,0:T(8,128)(2,1)S(1)} %get-tuple-element.59), channel_id=1, source_target_pairs={{0,8},{4,12},{8,0},{12,4},{16,24},{20,28},{24,16},{28,20},{1,9},{5... | collective-permute-start | bytes 1179656 | tf_op jit(solution)/shard_map/ppermute | solution.py:581
  82.9 1.5 %collective-permute-start.10 = (bf16[2,64,1536]{2,1,0:T(8,128)(2,1)S(1)}, bf16[2,64,1536]{2,1,0:T(8,128)(2,1)S(1)}, u32[]{:S(2)}, u32[]{:S(2)}) collective-permute-start(bf16[2,64,1536]{2,1,0:T(8,128)(2,1)S(1)} %get-tuple-element.61), channel_id=1, source_target_pairs={{0,16},{4,20},{8,24},{12,28},{16,0},{20,4},{24,8},{28,12},{1,17},{... | collective-permute-start | bytes 1179656 | tf_op jit(solution)/shard_map/ppermute | solution.py:581
  84.5 10.7 %collective-permute-done.7 = bf16[2,64,1536]{2,1,0:T(8,128)(2,1)S(1)} collective-permute-done((bf16[2,64,1536]{2,1,0:T(8,128)(2,1)S(1)}, bf16[2,64,1536]{2,1,0:T(8,128)(2,1)S(1)}, u32[]{:S(2)}, u32[]{:S(2)}) %collective-permute-start.7) | collective-permute-done | bytes 393248 | tf_op jit(solution)/shard_map/ppermute | solution.py:581
  95.2 1.6 %collective-permute-start.8 = (bf16[1,64,1536]{2,1,0:T(8,128)(2,1)S(1)}, bf16[1,64,1536]{2,1,0:T(8,128)(2,1)S(1)}, u32[]{:S(2)}, u32[]{:S(2)}) collective-permute-start(bf16[1,64,1536]{2,1,0:T(8,128)(2,1)S(1)} %get-tuple-element.63), channel_id=1, source_target_pairs={{0,16},{4,20},{8,24},{12,28},{16,0},{20,4},{24,8},{28,12},{1,17},{... | collective-permute-start | bytes 589832 | tf_op jit(solution)/shard_map/ppermute | solution.py:581
  97.0 1.0 collective-permute-start.11
  98.0 3.8 %collective-permute-done.8 = bf16[1,64,1536]{2,1,0:T(8,128)(2,1)S(1)} collective-permute-done((bf16[1,64,1536]{2,1,0:T(8,128)(2,1)S(1)}, bf16[1,64,1536]{2,1,0:T(8,128)(2,1)S(1)}, u32[]{:S(2)}, u32[]{:S(2)}) %collective-permute-start.8) | collective-permute-done | bytes 196640 | tf_op jit(solution)/shard_map/ppermute | solution.py:581
  101.8 1.5 %collective-permute-done.11 = bf16[1,64,1536]{2,1,0:T(8,128)(2,1)S(1)} collective-permute-done((bf16[1,64,1536]{2,1,0:T(8,128)(2,1)S(1)}, bf16[1,64,1536]{2,1,0:T(8,128)(2,1)S(1)}, u32[]{:S(2)}, u32[]{:S(2)}) %collective-permute-start.11) | collective-permute-done | bytes 196640 | tf_op jit(solution)/shard_map/ppermute | solution.py:581
  103.4 1.3 %collective-permute-start.12 = (bf16[64,768]{1,0:T(8,128)(2,1)S(1)}, bf16[64,768]{1,0:T(8,128)(2,1)S(1)}, u32[]{:S(2)}, u32[]{:S(2)}) collective-permute-start(bf16[64,768]{1,0:T(8,128)(2,1)S(1)} %get-tuple-element.66), channel_id=1, source_target_pairs={{0,1},{1,0},{2,3},{3,2},{4,5},{5,4},{6,7},{7,6},{8,9},{9,8},{10,11... | collective-permute-start | bytes 294920 | tf_op jit(solution)/shard_map/ppermute | solution.py:581
  104.7 2.6 %collective-permute-start.13 = (bf16[64,768]{1,0:T(8,128)(2,1)S(1)}, bf16[64,768]{1,0:T(8,128)(2,1)S(1)}, u32[]{:S(2)}, u32[]{:S(2)}) collective-permute-start(bf16[64,768]{1,0:T(8,128)(2,1)S(1)} %get-tuple-element.68), channel_id=1, source_target_pairs={{0,2},{1,3},{2,0},{3,1},{4,6},{5,7},{6,4},{7,5},{8,10},{9,11},{10,... | collective-permute-start | bytes 294920 | tf_op jit(solution)/shard_map/ppermute | solution.py:581
  108.5 5.4 %collective-permute-done.13 = bf16[64,768]{1,0:T(8,128)(2,1)S(1)} collective-permute-done((bf16[64,768]{1,0:T(8,128)(2,1)S(1)}, bf16[64,768]{1,0:T(8,128)(2,1)S(1)}, u32[]{:S(2)}, u32[]{:S(2)}) %collective-permute-start.13) | collective-permute-done | bytes 98336 | tf_op jit(solution)/shard_map/ppermute | solution.py:581
  114.0 1.7 %collective-permute-start.15 = (bf16[64,768]{1,0:T(8,128)(2,1)S(1)}, bf16[64,768]{1,0:T(8,128)(2,1)S(1)}, u32[]{:S(2)}, u32[]{:S(2)}) collective-permute-start(bf16[64,768]{1,0:T(8,128)(2,1)S(1)} %fusion.2.refs_0_), channel_id=1, source_target_pairs={{0,1},{1,0},{2,3},{3,2},{4,5},{5,4},{6,7},{7,6},{8,9},{9,8},{10,11... | collective-permute-start | bytes 294920 | tf_op jit(solution)/shard_map/ppermute | solution.py:581
  115.7 1.4 %collective-permute-start.16 = (bf16[64,768]{1,0:T(8,128)(2,1)S(1)}, bf16[64,768]{1,0:T(8,128)(2,1)S(1)}, u32[]{:S(2)}, u32[]{:S(2)}) collective-permute-start(bf16[64,768]{1,0:T(8,128)(2,1)S(1)} %fusion.2.refs_0_), channel_id=1, source_target_pairs={{0,2},{1,3},{2,0},{3,1},{4,6},{5,7},{6,4},{7,5},{8,10},{9,11},{10,... | collective-permute-start | bytes 294920 | tf_op jit(solution)/shard_map/ppermute | solution.py:581
  117.1 1.4 %collective-permute-start.17 = (bf16[64,768]{1,0:T(8,128)(2,1)S(1)}, bf16[64,768]{1,0:T(8,128)(2,1)S(1)}, u32[]{:S(2)}, u32[]{:S(2)}) collective-permute-start(bf16[64,768]{1,0:T(8,128)(2,1)S(1)} %fusion.2.refs_0_), channel_id=1, source_target_pairs={{0,3},{1,2},{2,1},{3,0},{4,7},{5,6},{6,5},{7,4},{8,11},{9,10},{10,... | collective-permute-start | bytes 294920 | tf_op jit(solution)/shard_map/ppermute | solution.py:581
  118.5 5.7 %scatter.1 = (bf16[64,12288]{1,0:T(8,128)(2,1)}, bf16[64,12288]{1,0:T(8,128)(2,1)}, bf16[6144,128]{1,0:T(8,128)(2,1)}, bf16[2048,256]{1,0:T(8,128)(2,1)}) custom-call(bf16[32,48,128]{2,1,0:T(8,128)(2,1)S(1)} %all-to-all-done.2.refs_0_, f32[384,128]{1,0:T(8,128)S(1)} %copy-done.3, f32[128,384]{1,0:T(8,128)S(1)} %get-tuple-element.46.refs_2_), custom_call_target="tpu_custom_call" | custom-call | tf_op jit(solution)/shard_map/scatter/pallas_call | solution.py:760
  124.2 1.5 %join.1 = (f32[64,512]{1,0:T(8,128)}, f32[64,2048]{1,0:T(8,128)}, f32[64,512]{1,0:T(8,128)}) custom-call(s32[3]{0:T(128)S(1)} %copy-done.8, bf16[64,768]{1,0:T(8,128)(2,1)S(1)} %fusion.2.refs_0_, bf16[64,768]{1,0:T(8,128)(2,1)S(1)} %collective-permute-done.15.refs_1_, bf16[64,768]{1,0:T(8,128)(2,1)S(1)} %collective-permute-done.16.refs_2_, ...), custom_call_target="tpu_custom_call" | custom-call | tf_op jit(solution)/shard_map/join/pallas_call | solution.py:747
  (51 shorter events, 9.0 us)
Async XLA Ops:
  2.0 15.8 %all-to-all-start = ((s32[32,8,128]{2,1,0:T(8,128)}), s32[32,8,128]{2,1,0:T(8,128)S(1)}, u32[]{:S(2)}, u32[]{:S(2)}) async-start(s32[32,8,128]{2,1,0:T(8,128)} %key.1), calls=%async_computation | async-start | bytes 262144 | tf_op jit(solution)/shard_map/all_to_all | solution.py:624
  11.1 15.2 %collective-permute-start.1 = (bf16[1,64,1536]{2,1,0:T(8,128)(2,1)S(1)}, bf16[1,64,1536]{2,1,0:T(8,128)(2,1)S(1)}, u32[]{:S(2)}, u32[]{:S(2)}) collective-permute-start(bf16[1,64,1536]{2,1,0:T(8,128)(2,1)S(1)} %maximum_bitcast_fusion), channel_id=1, source_target_pairs={{0,8},{4,12},{8,0},{12,4},{16,24},{20,28},{24,16},{28,20},{1,9},{5... | collective-permute-start | bytes 589832 | tf_op jit(solution)/shard_map/ppermute | solution.py:581
  13.9 12.4 %collective-permute-start = (bf16[1,64,1536]{2,1,0:T(8,128)(2,1)S(1)}, bf16[1,64,1536]{2,1,0:T(8,128)(2,1)S(1)}, u32[]{:S(2)}, u32[]{:S(2)}) collective-permute-start(bf16[1,64,1536]{2,1,0:T(8,128)(2,1)S(1)} %slice_bitcast_fusion), channel_id=1, source_target_pairs={{0,16},{4,20},{8,24},{12,28},{16,0},{20,4},{24,8},{28,12},{1,17},{... | collective-permute-start | bytes 589832 | tf_op jit(solution)/shard_map/ppermute | solution.py:581
  17.8 0.7 copy-start
  26.3 10.2 %collective-permute-start.4 = (bf16[2,64,1536]{2,1,0:T(8,128)(2,1)S(1)}, bf16[2,64,1536]{2,1,0:T(8,128)(2,1)S(1)}, u32[]{:S(2)}, u32[]{:S(2)}) collective-permute-start(bf16[2,64,1536]{2,1,0:T(8,128)(2,1)S(1)} %pad_maximum_fusion.3), channel_id=1, source_target_pairs={{0,16},{4,20},{8,24},{12,28},{16,0},{20,4},{24,8},{28,12},{1,17},{... | collective-permute-start | bytes 1179656 | tf_op jit(solution)/shard_map/ppermute | solution.py:581
  27.1 10.5 %collective-permute-start.2 = (bf16[2,64,1536]{2,1,0:T(8,128)(2,1)S(1)}, bf16[2,64,1536]{2,1,0:T(8,128)(2,1)S(1)}, u32[]{:S(2)}, u32[]{:S(2)}) collective-permute-start(bf16[2,64,1536]{2,1,0:T(8,128)(2,1)S(1)} %pad_maximum_fusion.2), channel_id=1, source_target_pairs={{0,8},{4,12},{8,0},{12,4},{16,24},{20,28},{24,16},{28,20},{1,9},{5... | collective-permute-start | bytes 1179656 | tf_op jit(solution)/shard_map/ppermute | solution.py:581
  37.5 3.5 %copy-start.1 = (s32[32,8,128]{2,1,0:T(8,128)S(1)}, s32[32,8,128]{2,1,0:T(8,128)}, u32[]{:S(2)}) copy-start(s32[32,8,128]{2,1,0:T(8,128)} %copy-done) | copy-start | bytes 393220
  37.5 3.5 %copy-start.3 = (f32[384,128]{1,0:T(8,128)S(1)}, f32[384,128]{1,0:T(8,128)}, u32[]{:S(2)}) copy-start(f32[384,128]{1,0:T(8,128)} %get-tuple-element.39.refs_2_.refs_1_) | copy-start | bytes 589828
  37.5 3.5 %copy-start.8 = (s32[3]{0:T(128)S(1)}, s32[3]{0:T(128)}, u32[]{:S(2)}) copy-start(s32[3]{0:T(128)} %pad_add_fusion.refs_0_.me_ref) | copy-start | bytes 40
  37.5 15.2 %copy-start.2 = (bf16[2,384,512]{2,1,0:T(8,128)(2,1)S(1)}, bf16[2,384,512]{2,1,0:T(8,128)(2,1)}, u32[]{:S(2)}) copy-start(bf16[2,384,512]{2,1,0:T(8,128)(2,1)} %refs_4_.3) | copy-start | bytes 2359300
  37.5 15.2 %collective-permute-start.5 = (bf16[4,64,1536]{2,1,0:T(8,128)(2,1)}, bf16[4,64,1536]{2,1,0:T(8,128)(2,1)}, u32[]{:S(2)}, u32[]{:S(2)}) collective-permute-start(bf16[4,64,1536]{2,1,0:T(8,128)(2,1)} %pad_maximum_fusion.1.refs_7_), channel_id=1, source_target_pairs={{0,4},{4,0},{8,12},{12,8},{16,20},{20,16},{24,28},{28,24},{1,5},{5... | collective-permute-start | bytes 2359304 | tf_op jit(solution)/shard_map/ppermute | solution.py:581
  37.7 15.0 %collective-permute-start.3 = (bf16[4,64,1536]{2,1,0:T(8,128)(2,1)S(1)}, bf16[4,64,1536]{2,1,0:T(8,128)(2,1)}, u32[]{:S(2)}, u32[]{:S(2)}) collective-permute-start(bf16[4,64,1536]{2,1,0:T(8,128)(2,1)S(1)} %pad_maximum_fusion.refs_5_), channel_id=1, source_target_pairs={{0,4},{4,0},{8,12},{12,8},{16,20},{20,16},{24,28},{28,24},{1,5},{5... | collective-permute-start | bytes 2359304 | tf_op jit(solution)/shard_map/ppermute | solution.py:581
  38.3 14.4 %all-to-all-start.1 = ((bf16[32,48,128]{2,1,0:T(8,128)(2,1)}), bf16[32,48,128]{2,1,0:T(8,128)(2,1)S(1)}, u32[]{:S(2)}, u32[]{:S(2)}) async-start(bf16[32,48,128]{2,1,0:T(8,128)(2,1)} %get-tuple-element.38), calls=%async_computation.1 | async-start | bytes 786432 | tf_op jit(solution)/shard_map/all_to_all | solution.py:663
  42.2 0.6 copy-start.6
  52.7 0.7 copy-start.7
  73.6 0.9 copy-start.4
  74.5 0.7 copy-start.5
  75.2 4.5 %collective-permute-start.6 = (bf16[4,64,1536]{2,1,0:T(8,128)(2,1)}, bf16[4,64,1536]{2,1,0:T(8,128)(2,1)S(1)}, u32[]{:S(2)}, u32[]{:S(2)}) collective-permute-start(bf16[4,64,1536]{2,1,0:T(8,128)(2,1)} %get-tuple-element.52), channel_id=1, source_target_pairs={{0,4},{4,0},{8,12},{12,8},{16,20},{20,16},{24,28},{28,24},{1,5},{5... | collective-permute-start | bytes 2359304 | tf_op jit(solution)/shard_map/ppermute | solution.py:581
  76.5 6.3 %collective-permute-start.9 = (bf16[4,64,1536]{2,1,0:T(8,128)(2,1)}, bf16[4,64,1536]{2,1,0:T(8,128)(2,1)S(1)}, u32[]{:S(2)}, u32[]{:S(2)}) collective-permute-start(bf16[4,64,1536]{2,1,0:T(8,128)(2,1)} %get-tuple-element.54), channel_id=1, source_target_pairs={{0,4},{4,0},{8,12},{12,8},{16,20},{20,16},{24,28},{28,24},{1,5},{5... | collective-permute-start | bytes 2359304 | tf_op jit(solution)/shard_map/ppermute | solution.py:581
  76.5 42.0 %all-to-all-start.2 = ((bf16[32,48,128]{2,1,0:T(8,128)(2,1)}), bf16[32,48,128]{2,1,0:T(8,128)(2,1)S(1)}, u32[]{:S(2)}, u32[]{:S(2)}) async-start(bf16[32,48,128]{2,1,0:T(8,128)(2,1)} %copy-done.5), calls=%async_computation.2 | async-start | bytes 786432 | tf_op jit(solution)/shard_map/all_to_all | solution.py:726
  81.1 14.0 %collective-permute-start.7 = (bf16[2,64,1536]{2,1,0:T(8,128)(2,1)S(1)}, bf16[2,64,1536]{2,1,0:T(8,128)(2,1)S(1)}, u32[]{:S(2)}, u32[]{:S(2)}) collective-permute-start(bf16[2,64,1536]{2,1,0:T(8,128)(2,1)S(1)} %get-tuple-element.59), channel_id=1, source_target_pairs={{0,8},{4,12},{8,0},{12,4},{16,24},{20,28},{24,16},{28,20},{1,9},{5... | collective-permute-start | bytes 1179656 | tf_op jit(solution)/shard_map/ppermute | solution.py:581
  82.9 13.9 %collective-permute-start.10 = (bf16[2,64,1536]{2,1,0:T(8,128)(2,1)S(1)}, bf16[2,64,1536]{2,1,0:T(8,128)(2,1)S(1)}, u32[]{:S(2)}, u32[]{:S(2)}) collective-permute-start(bf16[2,64,1536]{2,1,0:T(8,128)(2,1)S(1)} %get-tuple-element.61), channel_id=1, source_target_pairs={{0,16},{4,20},{8,24},{12,28},{16,0},{20,4},{24,8},{28,12},{1,17},{... | collective-permute-start | bytes 1179656 | tf_op jit(solution)/shard_map/ppermute | solution.py:581
  95.2 6.5 %collective-permute-start.8 = (bf16[1,64,1536]{2,1,0:T(8,128)(2,1)S(1)}, bf16[1,64,1536]{2,1,0:T(8,128)(2,1)S(1)}, u32[]{:S(2)}, u32[]{:S(2)}) collective-permute-start(bf16[1,64,1536]{2,1,0:T(8,128)(2,1)S(1)} %get-tuple-element.63), channel_id=1, source_target_pairs={{0,16},{4,20},{8,24},{12,28},{16,0},{20,4},{24,8},{28,12},{1,17},{... | collective-permute-start | bytes 589832 | tf_op jit(solution)/shard_map/ppermute | solution.py:581
  97.0 6.3 %collective-permute-start.11 = (bf16[1,64,1536]{2,1,0:T(8,128)(2,1)S(1)}, bf16[1,64,1536]{2,1,0:T(8,128)(2,1)S(1)}, u32[]{:S(2)}, u32[]{:S(2)}) collective-permute-start(bf16[1,64,1536]{2,1,0:T(8,128)(2,1)S(1)} %get-tuple-element.65), channel_id=1, source_target_pairs={{0,8},{4,12},{8,0},{12,4},{16,24},{20,28},{24,16},{28,20},{1,9},{5... | collective-permute-start | bytes 589832 | tf_op jit(solution)/shard_map/ppermute | solution.py:581
  103.4 5.1 %collective-permute-start.12 = (bf16[64,768]{1,0:T(8,128)(2,1)S(1)}, bf16[64,768]{1,0:T(8,128)(2,1)S(1)}, u32[]{:S(2)}, u32[]{:S(2)}) collective-permute-start(bf16[64,768]{1,0:T(8,128)(2,1)S(1)} %get-tuple-element.66), channel_id=1, source_target_pairs={{0,1},{1,0},{2,3},{3,2},{4,5},{5,4},{6,7},{7,6},{8,9},{9,8},{10,11... | collective-permute-start | bytes 294920 | tf_op jit(solution)/shard_map/ppermute | solution.py:581
  104.7 9.2 %collective-permute-start.13 = (bf16[64,768]{1,0:T(8,128)(2,1)S(1)}, bf16[64,768]{1,0:T(8,128)(2,1)S(1)}, u32[]{:S(2)}, u32[]{:S(2)}) collective-permute-start(bf16[64,768]{1,0:T(8,128)(2,1)S(1)} %get-tuple-element.68), channel_id=1, source_target_pairs={{0,2},{1,3},{2,0},{3,1},{4,6},{5,7},{6,4},{7,5},{8,10},{9,11},{10,... | collective-permute-start | bytes 294920 | tf_op jit(solution)/shard_map/ppermute | solution.py:581
  107.3 6.6 %collective-permute-start.14 = (bf16[64,768]{1,0:T(8,128)(2,1)S(1)}, bf16[64,768]{1,0:T(8,128)(2,1)S(1)}, u32[]{:S(2)}, u32[]{:S(2)}) collective-permute-start(bf16[64,768]{1,0:T(8,128)(2,1)S(1)} %get-tuple-element.67), channel_id=1, source_target_pairs={{0,3},{1,2},{2,1},{3,0},{4,7},{5,6},{6,5},{7,4},{8,11},{9,10},{10,... | collective-permute-start | bytes 294920 | tf_op jit(solution)/shard_map/ppermute | solution.py:581
  114.0 10.1 %collective-permute-start.15 = (bf16[64,768]{1,0:T(8,128)(2,1)S(1)}, bf16[64,768]{1,0:T(8,128)(2,1)S(1)}, u32[]{:S(2)}, u32[]{:S(2)}) collective-permute-start(bf16[64,768]{1,0:T(8,128)(2,1)S(1)} %fusion.2.refs_0_), channel_id=1, source_target_pairs={{0,1},{1,0},{2,3},{3,2},{4,5},{5,4},{6,7},{7,6},{8,9},{9,8},{10,11... | collective-permute-start | bytes 294920 | tf_op jit(solution)/shard_map/ppermute | solution.py:581
  115.7 8.5 %collective-permute-start.16 = (bf16[64,768]{1,0:T(8,128)(2,1)S(1)}, bf16[64,768]{1,0:T(8,128)(2,1)S(1)}, u32[]{:S(2)}, u32[]{:S(2)}) collective-permute-start(bf16[64,768]{1,0:T(8,128)(2,1)S(1)} %fusion.2.refs_0_), channel_id=1, source_target_pairs={{0,2},{1,3},{2,0},{3,1},{4,6},{5,7},{6,4},{7,5},{8,10},{9,11},{10,... | collective-permute-start | bytes 294920 | tf_op jit(solution)/shard_map/ppermute | solution.py:581
  117.1 7.1 %collective-permute-start.17 = (bf16[64,768]{1,0:T(8,128)(2,1)S(1)}, bf16[64,768]{1,0:T(8,128)(2,1)S(1)}, u32[]{:S(2)}, u32[]{:S(2)}) collective-permute-start(bf16[64,768]{1,0:T(8,128)(2,1)S(1)} %fusion.2.refs_0_), channel_id=1, source_target_pairs={{0,3},{1,2},{2,1},{3,0},{4,7},{5,6},{6,5},{7,4},{8,11},{9,10},{10,... | collective-permute-start | bytes 294920 | tf_op jit(solution)/shard_map/ppermute | solution.py:581

commit v3 on v2

--- a/solution.py
+++ b/solution.py
@@ -33,6 +33,10 @@
 
 def floor_div(values, by):
     return jnp.floor((values.astype(F32) + 0.5) * (1.0 / by)).astype(jnp.int32)
+
+
+def slope_of(twice, part):
+    return twice + part * (2.0 - twice)
 
 
 def log2(value):
@@ -272,7 +276,7 @@
     (
         wa, wb, slot_scr, pack_scr, cat_scr, norm_scr, act_scr, slope_scr, attn_scr, tilt_scr,
         att_scr, datt_scr, dproj_scr, gated_scr, og_scr, demb_scr, drow_scr, dact_scr,
-        grad_scr, cot_scr, out_scr, back_scr, w_sems, io_sems,
+        grad_scr, cot_scr, out_scr, back_scr, keep_scr, w_sems, io_sems,
     ) = refs
     dp = me_ref[1]
     width = out_ref.shape[2]
@@ -281,6 +285,7 @@
     rows_each = width // dp_count
     head_dim = width // HEADS
     scale = head_dim**-0.5
+    half_scale = jnp.asarray(0.5 * scale, BF16)
     fetches = []
     for refs_in, held, seq in ((b_refs, wb, seq_b), (a_refs, wa, seq_a)):
         index = 0
@@ -331,7 +336,8 @@
         slot = infot_ref[rows, 0:1].astype(jnp.int32)
         kind = infot_ref[rows, 1:2].astype(jnp.int32)
         valid = infot_ref[rows, 2:3]
-        length = carry_len(q, info_ref, span)
+        inside = info_ref[2:3, pl.ds(base, span)]
+        keep_scr[...] = jnp.where(iota((span, span), 1) <= iota((span, span), 0), inside, 0.0)
         chosen = onehot(iota((span, slots), 1) == slot)
         cat = jnp.where(kind_of_lane == kind, dot(chosen, arrived), 0.0).astype(BF16)
         cat_scr[rows, :] = cat
@@ -343,9 +349,9 @@
         for j in (2, 3, 1, 0):
             lean = dot(norm_scr[rows, :], in_part(j)) * 0.5
             twice = jnp.tanh(lean) + 1.0
-            part = lean * twice
-            act_scr[j] = part.astype(BF16)
-            slope_scr[j] = twice + part * (2.0 - twice)
+            part = (lean * twice).astype(BF16)
+            act_scr[j] = part
+            slope_scr[j] = slope_of(twice.astype(BF16), part)
         order = [(rb, head) for rb in range(blocks) for head in range(HEADS)]
 
         def scores_of(rb, head):
@@ -368,14 +374,10 @@
             if step + 2 < len(order):
                 ahead.append(scores_of(*order[step + 2]))
             lean = ahead.pop(0) * (0.5 * scale)
-            twice = jnp.tanh(lean) + 1.0
-            attn = lean * twice
-            key_pos = iota((128, keys), 1)
-            keep = (key_pos <= iota((128, keys), 0) + rb * 128) & (key_pos < length)
-            attn_scr[head, here, :keys] = jnp.where(keep, attn, 0.0).astype(BF16)
-            tilt_scr[head, here, :keys] = jnp.where(
-                keep, (twice + attn * (2.0 - twice)) * (0.5 * scale), 0.0
-            )
+            twice = (jnp.tanh(lean) + 1.0) * keep_scr[here, :keys]
+            attn = (lean * twice).astype(BF16)
+            attn_scr[head, here, :keys] = attn
+            tilt_scr[head, here, :keys] = slope_of(twice.astype(BF16), attn) * half_scale
             if step:
                 attend(*order[step - 1])
         attend(*order[-1])
@@ -392,8 +394,7 @@
         d_gated = dot(og, out_w, NT).astype(BF16).astype(F32)
         out_scr[q] = (emb + dot(gated, out_w)).astype(BF16)
         out_copy(q).start()
-        d_gate = (d_gated * att_n).astype(BF16).astype(F32)
-        dproj_scr[rows, :width] = (d_gate * slope_scr[0]).astype(BF16)
+        dproj_scr[rows, :width] = (d_gated * att_n).astype(BF16) * slope_scr[0]
         d_n = d_gated * gate
         d_att = att_inv * (
             d_n
@@ -413,8 +414,8 @@
             here = slice(rb * 128, (rb + 1) * 128)
             low = which * width + head * head_dim
             dproj_scr[pl.ds(base + rb * 128, 128), low : low + head_dim] = (
-                grad.astype(BF16).astype(F32) * slope_scr[which, here, heads[head]]
-            ).astype(BF16)
+                grad.astype(BF16) * slope_scr[which, here, heads[head]]
+            )
 
         def settle(rb, head):
             keys = (rb + 1) * 128
@@ -432,8 +433,9 @@
             if step + 2 < len(order):
                 ahead.append(d_attn_of(*order[step + 2]))
             put(1, rb, head, dot(attn_scr[head, rest, here], datt_scr[rest, heads[head]], TN))
-            d_attn = ahead.pop(0).astype(BF16).astype(F32)
-            dact_scr[head, here, :keys] = (d_attn * tilt_scr[head, here, :keys]).astype(BF16)
+            dact_scr[head, here, :keys] = (
+                ahead.pop(0).astype(BF16) * tilt_scr[head, here, :keys]
+            )
             if step:
                 settle(*order[step - 1])
         settle(*order[-1])
@@ -491,11 +493,6 @@
     for q in range(seq_count):
         out_copy(q).wait()
     back_copy.wait()
-
-
-def carry_len(q, info_ref, span):
-    flags = info_ref[2:3, pl.ds(pl.multiple_of(q * span, 128), span)]
-    return jnp.sum(flags, axis=1, keepdims=True).astype(jnp.int32)
 
 
 def scatter_kernel(devices, capacity, row_counts, widths, *refs):
@@ -696,9 +693,9 @@
             pltpu.VMEM((toks, width), BF16),
             pltpu.VMEM((toks, width), BF16),
             pltpu.VMEM((4, span, width), BF16),
-            pltpu.VMEM((4, span, width), F32),
+            pltpu.VMEM((4, span, width), BF16),
             pltpu.VMEM((HEADS, span, span), BF16),
-            pltpu.VMEM((HEADS, span, span), F32),
+            pltpu.VMEM((HEADS, span, span), BF16),
             pltpu.VMEM((span, width), F32),
             pltpu.VMEM((span, width), BF16),
             pltpu.VMEM((toks, 4 * width), BF16),
@@ -711,6 +708,7 @@
             pltpu.VMEM((seq_count, span, width), BF16),
             pltpu.VMEM((seq_count, span, width), BF16),
             pltpu.VMEM((devices, 4 * capacity, 128), BF16),
+            pltpu.VMEM((span, span), F32),
             pltpu.SemaphoreType.DMA((2 * dp_count,)),
             pltpu.SemaphoreType.DMA((2 + seq_count,)),
         ],

time: 126 us -> 126 us (level)
  no operation moved by 1% of the time
where the time goes in v3:
time: 126 us; the launch traced here: 125 us
  waiting for transfers between devices  42.6 us (34%)
  Pallas kernels  37.2 us (30%)
  starting transfers between devices  34.6 us (27%)
  local copies, waits for them, and re-layouts  5.44 us (4%)
  other arithmetic  4.54 us (4%)
    ppermute x18, waiting for transfers between devices, exchange(): return lax.ppermute(value, axis, [(i, i ^ mask) for i in range(count)])  30.8 us
    ppermute x18, starting transfers between devices, exchange(): return lax.ppermute(value, axis, [(i, i ^ mask) for i in range(count)])  21.2 us
    pallas_call x1, Pallas kernels, step(): pl.pallas_call(functools.partial(layer_kernel, devices, seq_count, span,...  19.7 us
    all_to_all x1, waiting for transfers between devices, step(): got = lax.all_to_all(send, ('dp', 'table'), 0, 0, tiled=True)  9.88 us
    pallas_call x1, Pallas kernels, step(): pl.pallas_call(functools.partial(plan_kernel, devices, seq_count, span, c...  7.78 us
    all_to_all x1, starting transfers between devices, step(): ids = lax.all_to_all(packed, ('dp', 'table'), 0, 0, tiled=True)  7.33 us
    pallas_call x1, Pallas kernels, step(): pl.pallas_call(functools.partial(scatter_kernel, devices, capacity, row_c...  5.67 us
    unnamed x18, local copies, waits for them, and re-layouts  3.62 us
  transfers between devices with their start and end apart: 21, of which 8 were waited for; matrix products, arithmetic and copies ran while one was open for 5% of the time, Pallas kernels for 12%

profile of v3, /device:TPU:0, one launch (start us, length us, event | category | flops | bytes accessed | tf_op | source)
XLA Modules:
  0.0 125.2 jit_solution(9754392026153033469)
XLA Ops:
  0.6 1.4 %key.1 = s32[32,8,128]{2,1,0:T(8,128)} custom-call(s32[2]{0:T(128)} %len_ref.1, s32[2]{0:T(128)} %to_ref.1, s32[2,384]{1,0:T(2,128)} %item_ref.1, s32[2,384]{1,0:T(2,128)} %kind_ref.1), custom_call_target="tpu_custom_call" | custom-call | tf_op jit(solution)/shard_map/key/pallas_call | solution.py:610
  2.0 7.3 %all-to-all-start = ((s32[32,8,128]{2,1,0:T(8,128)}), s32[32,8,128]{2,1,0:T(8,128)S(1)}, u32[]{:S(2)}, u32[]{:S(2)}) async-start(s32[32,8,128]{2,1,0:T(8,128)} %key.1), calls=%async_computation | async-start | bytes 262144 | tf_op jit(solution)/shard_map/all_to_all | solution.py:621
  10.2 0.9 maximum_bitcast_fusion
  11.1 1.8 %collective-permute-start.1 = (bf16[1,64,1536]{2,1,0:T(8,128)(2,1)S(1)}, bf16[1,64,1536]{2,1,0:T(8,128)(2,1)S(1)}, u32[]{:S(2)}, u32[]{:S(2)}) collective-permute-start(bf16[1,64,1536]{2,1,0:T(8,128)(2,1)S(1)} %maximum_bitcast_fusion), channel_id=1, source_target_pairs={{0,8},{4,12},{8,0},{12,4},{16,24},{20,28},{24,16},{28,20},{1,9},{5... | collective-permute-start | bytes 589832 | tf_op jit(solution)/shard_map/ppermute | solution.py:578
  12.9 0.9 slice_bitcast_fusion
  13.9 1.5 %collective-permute-start = (bf16[1,64,1536]{2,1,0:T(8,128)(2,1)S(1)}, bf16[1,64,1536]{2,1,0:T(8,128)(2,1)S(1)}, u32[]{:S(2)}, u32[]{:S(2)}) collective-permute-start(bf16[1,64,1536]{2,1,0:T(8,128)(2,1)S(1)} %slice_bitcast_fusion), channel_id=1, source_target_pairs={{0,16},{4,20},{8,24},{12,28},{16,0},{20,4},{24,8},{28,12},{1,17},{... | collective-permute-start | bytes 589832 | tf_op jit(solution)/shard_map/ppermute | solution.py:578
  16.0 1.9 %all-to-all-done.refs_1_ = s32[32,8,128]{2,1,0:T(8,128)S(1)} async-done(((s32[32,8,128]{2,1,0:T(8,128)}), s32[32,8,128]{2,1,0:T(8,128)S(1)}, u32[]{:S(2)}, u32[]{:S(2)}) %all-to-all-start) | async-done | bytes 131104 | tf_op jit(solution)/shard_map/all_to_all | solution.py:621
  18.5 7.8 %plan.1 = (bf16[32,48,128]{2,1,0:T(8,128)(2,1)}, f32[384,128]{1,0:T(8,128)}) custom-call(s32[3]{0:T(128)} %pad_add_fusion.refs_0_.me_ref, s32[32,8,128]{2,1,0:T(8,128)} %copy-done, bf16[64,12288]{1,0:T(8,128)(2,1)} %bitcast.20, bf16[64,12288]{1,0:T(8,128)(2,1)} %bitcast.21, bf16[6144,128]{1,0:T(8,128)(2,1)} %refs_4_.2, bf16[2048,256]{1,0:T(8,128)(2,1)} %refs_5_.1), custom_call_target="tpu_custom_call" | custom-call | tf_op jit(solution)/shard_map/plan/pallas_call | solution.py:635
  27.7 8.9 %collective-permute-done.4 = bf16[2,64,1536]{2,1,0:T(8,128)(2,1)S(1)} collective-permute-done((bf16[2,64,1536]{2,1,0:T(8,128)(2,1)S(1)}, bf16[2,64,1536]{2,1,0:T(8,128)(2,1)S(1)}, u32[]{:S(2)}, u32[]{:S(2)}) %collective-permute-start.4) | collective-permute-done | bytes 393248 | tf_op jit(solution)/shard_map/ppermute | solution.py:578
  36.6 1.0 pad_maximum_fusion.1.refs_7_
  38.3 2.8 %all-to-all-start.1 = ((bf16[32,48,128]{2,1,0:T(8,128)(2,1)}), bf16[32,48,128]{2,1,0:T(8,128)(2,1)S(1)}, u32[]{:S(2)}, u32[]{:S(2)}) async-start(bf16[32,48,128]{2,1,0:T(8,128)(2,1)} %get-tuple-element.38), calls=%async_computation.1 | async-start | bytes 786432 | tf_op jit(solution)/shard_map/all_to_all | solution.py:660
  41.1 1.1 own.1
  42.8 9.9 %all-to-all-done.1.refs_1_ = bf16[32,48,128]{2,1,0:T(8,128)(2,1)S(1)} async-done(((bf16[32,48,128]{2,1,0:T(8,128)(2,1)}), bf16[32,48,128]{2,1,0:T(8,128)(2,1)S(1)}, u32[]{:S(2)}, u32[]{:S(2)}) %all-to-all-start.1) | async-done | bytes 393248 | tf_op jit(solution)/shard_map/all_to_all | solution.py:660
  53.5 19.7 %layer.1 = (bf16[2,384,512]{2,1,0:T(8,128)(2,1)}, bf16[32,48,128]{2,1,0:T(8,128)(2,1)S(1)}, bf16[4,64,1536]{2,1,0:T(8,128)(2,1)S(1)}, bf16[4,64,1536]{2,1,0:T(8,...) custom-call(s32[3]{0:T(128)S(1)} %copy-done.8, ...), custom_call_target="tpu_custom_call" | custom-call | tf_op jit(solution)/shard_map/layer/pallas_call | solution.py:676
  74.8 1.2 collective-permute-start.6
  76.0 3.3 %all-to-all-start.2 = ((bf16[32,48,128]{2,1,0:T(8,128)(2,1)}), bf16[32,48,128]{2,1,0:T(8,128)(2,1)S(1)}, u32[]{:S(2)}, u32[]{:S(2)}) async-start(bf16[32,48,128]{2,1,0:T(8,128)(2,1)} %copy-done.5), calls=%async_computation.2 | async-start | bytes 786432 | tf_op jit(solution)/shard_map/all_to_all | solution.py:724
  79.3 1.4 %add_convert_fusion.3 = (bf16[2,64,1536]{2,1,0:T(8,128)(2,1)S(1)}, bf16[2,64,1536]{2,1,0:T(8,128)(2,1)S(1)}) fusion(bf16[4,64,1536]{2,1,0:T(8,128)(2,1)S(1)} %collective-permute-done.6, bf16[4,64,1536]{2,1,0:T(8,128)(2,1)} %copy-done.4), kind=kLoop, calls=%fused_computation.5 | loop fusion | flops 1572864 | bytes 2359296 | tf_op jit(solution)/shard_map/convert_element_type | solution.py:722
  80.7 1.6 %collective-permute-start.7 = (bf16[2,64,1536]{2,1,0:T(8,128)(2,1)S(1)}, bf16[2,64,1536]{2,1,0:T(8,128)(2,1)S(1)}, u32[]{:S(2)}, u32[]{:S(2)}) collective-permute-start(bf16[2,64,1536]{2,1,0:T(8,128)(2,1)S(1)} %get-tuple-element.59), channel_id=1, source_target_pairs={{0,8},{4,12},{8,0},{12,4},{16,24},{20,28},{24,16},{28,20},{1,9},{5... | collective-permute-start | bytes 1179656 | tf_op jit(solution)/shard_map/ppermute | solution.py:578
  82.5 1.5 %collective-permute-start.10 = (bf16[2,64,1536]{2,1,0:T(8,128)(2,1)S(1)}, bf16[2,64,1536]{2,1,0:T(8,128)(2,1)S(1)}, u32[]{:S(2)}, u32[]{:S(2)}) collective-permute-start(bf16[2,64,1536]{2,1,0:T(8,128)(2,1)S(1)} %get-tuple-element.61), channel_id=1, source_target_pairs={{0,16},{4,20},{8,24},{12,28},{16,0},{20,4},{24,8},{28,12},{1,17},{... | collective-permute-start | bytes 1179656 | tf_op jit(solution)/shard_map/ppermute | solution.py:578
  84.0 10.7 %collective-permute-done.7 = bf16[2,64,1536]{2,1,0:T(8,128)(2,1)S(1)} collective-permute-done((bf16[2,64,1536]{2,1,0:T(8,128)(2,1)S(1)}, bf16[2,64,1536]{2,1,0:T(8,128)(2,1)S(1)}, u32[]{:S(2)}, u32[]{:S(2)}) %collective-permute-start.7) | collective-permute-done | bytes 393248 | tf_op jit(solution)/shard_map/ppermute | solution.py:578
  94.8 1.6 %collective-permute-start.8 = (bf16[1,64,1536]{2,1,0:T(8,128)(2,1)S(1)}, bf16[1,64,1536]{2,1,0:T(8,128)(2,1)S(1)}, u32[]{:S(2)}, u32[]{:S(2)}) collective-permute-start(bf16[1,64,1536]{2,1,0:T(8,128)(2,1)S(1)} %get-tuple-element.63), channel_id=1, source_target_pairs={{0,16},{4,20},{8,24},{12,28},{16,0},{20,4},{24,8},{28,12},{1,17},{... | collective-permute-start | bytes 589832 | tf_op jit(solution)/shard_map/ppermute | solution.py:578
  96.5 1.0 collective-permute-start.11
  97.5 3.8 %collective-permute-done.8 = bf16[1,64,1536]{2,1,0:T(8,128)(2,1)S(1)} collective-permute-done((bf16[1,64,1536]{2,1,0:T(8,128)(2,1)S(1)}, bf16[1,64,1536]{2,1,0:T(8,128)(2,1)S(1)}, u32[]{:S(2)}, u32[]{:S(2)}) %collective-permute-start.8) | collective-permute-done | bytes 196640 | tf_op jit(solution)/shard_map/ppermute | solution.py:578
  101.4 1.5 %collective-permute-done.11 = bf16[1,64,1536]{2,1,0:T(8,128)(2,1)S(1)} collective-permute-done((bf16[1,64,1536]{2,1,0:T(8,128)(2,1)S(1)}, bf16[1,64,1536]{2,1,0:T(8,128)(2,1)S(1)}, u32[]{:S(2)}, u32[]{:S(2)}) %collective-permute-start.11) | collective-permute-done | bytes 196640 | tf_op jit(solution)/shard_map/ppermute | solution.py:578
  103.0 1.3 %collective-permute-start.12 = (bf16[64,768]{1,0:T(8,128)(2,1)S(1)}, bf16[64,768]{1,0:T(8,128)(2,1)S(1)}, u32[]{:S(2)}, u32[]{:S(2)}) collective-permute-start(bf16[64,768]{1,0:T(8,128)(2,1)S(1)} %get-tuple-element.66), channel_id=1, source_target_pairs={{0,1},{1,0},{2,3},{3,2},{4,5},{5,4},{6,7},{7,6},{8,9},{9,8},{10,11... | collective-permute-start | bytes 294920 | tf_op jit(solution)/shard_map/ppermute | solution.py:578
  104.3 2.6 %collective-permute-start.13 = (bf16[64,768]{1,0:T(8,128)(2,1)S(1)}, bf16[64,768]{1,0:T(8,128)(2,1)S(1)}, u32[]{:S(2)}, u32[]{:S(2)}) collective-permute-start(bf16[64,768]{1,0:T(8,128)(2,1)S(1)} %get-tuple-element.68), channel_id=1, source_target_pairs={{0,2},{1,3},{2,0},{3,1},{4,6},{5,7},{6,4},{7,5},{8,10},{9,11},{10,... | collective-permute-start | bytes 294920 | tf_op jit(solution)/shard_map/ppermute | solution.py:578
  108.1 5.4 %collective-permute-done.13 = bf16[64,768]{1,0:T(8,128)(2,1)S(1)} collective-permute-done((bf16[64,768]{1,0:T(8,128)(2,1)S(1)}, bf16[64,768]{1,0:T(8,128)(2,1)S(1)}, u32[]{:S(2)}, u32[]{:S(2)}) %collective-permute-start.13) | collective-permute-done | bytes 98336 | tf_op jit(solution)/shard_map/ppermute | solution.py:578
  113.6 1.7 %collective-permute-start.15 = (bf16[64,768]{1,0:T(8,128)(2,1)S(1)}, bf16[64,768]{1,0:T(8,128)(2,1)S(1)}, u32[]{:S(2)}, u32[]{:S(2)}) collective-permute-start(bf16[64,768]{1,0:T(8,128)(2,1)S(1)} %fusion.2.refs_0_), channel_id=1, source_target_pairs={{0,1},{1,0},{2,3},{3,2},{4,5},{5,4},{6,7},{7,6},{8,9},{9,8},{10,11... | collective-permute-start | bytes 294920 | tf_op jit(solution)/shard_map/ppermute | solution.py:578
  115.2 1.4 %collective-permute-start.16 = (bf16[64,768]{1,0:T(8,128)(2,1)S(1)}, bf16[64,768]{1,0:T(8,128)(2,1)S(1)}, u32[]{:S(2)}, u32[]{:S(2)}) collective-permute-start(bf16[64,768]{1,0:T(8,128)(2,1)S(1)} %fusion.2.refs_0_), channel_id=1, source_target_pairs={{0,2},{1,3},{2,0},{3,1},{4,6},{5,7},{6,4},{7,5},{8,10},{9,11},{10,... | collective-permute-start | bytes 294920 | tf_op jit(solution)/shard_map/ppermute | solution.py:578
  116.6 1.4 %collective-permute-start.17 = (bf16[64,768]{1,0:T(8,128)(2,1)S(1)}, bf16[64,768]{1,0:T(8,128)(2,1)S(1)}, u32[]{:S(2)}, u32[]{:S(2)}) collective-permute-start(bf16[64,768]{1,0:T(8,128)(2,1)S(1)} %fusion.2.refs_0_), channel_id=1, source_target_pairs={{0,3},{1,2},{2,1},{3,0},{4,7},{5,6},{6,5},{7,4},{8,11},{9,10},{10,... | collective-permute-start | bytes 294920 | tf_op jit(solution)/shard_map/ppermute | solution.py:578
  118.0 5.7 %scatter.1 = (bf16[64,12288]{1,0:T(8,128)(2,1)}, bf16[64,12288]{1,0:T(8,128)(2,1)}, bf16[6144,128]{1,0:T(8,128)(2,1)}, bf16[2048,256]{1,0:T(8,128)(2,1)}) custom-call(bf16[32,48,128]{2,1,0:T(8,128)(2,1)S(1)} %all-to-all-done.2.refs_0_, f32[384,128]{1,0:T(8,128)S(1)} %copy-done.3, f32[128,384]{1,0:T(8,128)S(1)} %get-tuple-element.46.refs_2_), custom_call_target="tpu_custom_call" | custom-call | tf_op jit(solution)/shard_map/scatter/pallas_call | solution.py:758
  123.7 1.5 %join.1 = (f32[64,512]{1,0:T(8,128)}, f32[64,2048]{1,0:T(8,128)}, f32[64,512]{1,0:T(8,128)}) custom-call(s32[3]{0:T(128)S(1)} %copy-done.8, bf16[64,768]{1,0:T(8,128)(2,1)S(1)} %fusion.2.refs_0_, bf16[64,768]{1,0:T(8,128)(2,1)S(1)} %collective-permute-done.15.refs_1_, bf16[64,768]{1,0:T(8,128)(2,1)S(1)} %collective-permute-done.16.refs_2_, ...), custom_call_target="tpu_custom_call" | custom-call | tf_op jit(solution)/shard_map/join/pallas_call | solution.py:745
  (51 shorter events, 9.0 us)
Async XLA Ops:
  2.0 15.8 %all-to-all-start = ((s32[32,8,128]{2,1,0:T(8,128)}), s32[32,8,128]{2,1,0:T(8,128)S(1)}, u32[]{:S(2)}, u32[]{:S(2)}) async-start(s32[32,8,128]{2,1,0:T(8,128)} %key.1), calls=%async_computation | async-start | bytes 262144 | tf_op jit(solution)/shard_map/all_to_all | solution.py:621
  11.1 15.2 %collective-permute-start.1 = (bf16[1,64,1536]{2,1,0:T(8,128)(2,1)S(1)}, bf16[1,64,1536]{2,1,0:T(8,128)(2,1)S(1)}, u32[]{:S(2)}, u32[]{:S(2)}) collective-permute-start(bf16[1,64,1536]{2,1,0:T(8,128)(2,1)S(1)} %maximum_bitcast_fusion), channel_id=1, source_target_pairs={{0,8},{4,12},{8,0},{12,4},{16,24},{20,28},{24,16},{28,20},{1,9},{5... | collective-permute-start | bytes 589832 | tf_op jit(solution)/shard_map/ppermute | solution.py:578
  13.9 12.4 %collective-permute-start = (bf16[1,64,1536]{2,1,0:T(8,128)(2,1)S(1)}, bf16[1,64,1536]{2,1,0:T(8,128)(2,1)S(1)}, u32[]{:S(2)}, u32[]{:S(2)}) collective-permute-start(bf16[1,64,1536]{2,1,0:T(8,128)(2,1)S(1)} %slice_bitcast_fusion), channel_id=1, source_target_pairs={{0,16},{4,20},{8,24},{12,28},{16,0},{20,4},{24,8},{28,12},{1,17},{... | collective-permute-start | bytes 589832 | tf_op jit(solution)/shard_map/ppermute | solution.py:578
  17.8 0.7 copy-start
  26.3 10.2 %collective-permute-start.4 = (bf16[2,64,1536]{2,1,0:T(8,128)(2,1)S(1)}, bf16[2,64,1536]{2,1,0:T(8,128)(2,1)S(1)}, u32[]{:S(2)}, u32[]{:S(2)}) collective-permute-start(bf16[2,64,1536]{2,1,0:T(8,128)(2,1)S(1)} %pad_maximum_fusion.3), channel_id=1, source_target_pairs={{0,16},{4,20},{8,24},{12,28},{16,0},{20,4},{24,8},{28,12},{1,17},{... | collective-permute-start | bytes 1179656 | tf_op jit(solution)/shard_map/ppermute | solution.py:578
  27.1 10.5 %collective-permute-start.2 = (bf16[2,64,1536]{2,1,0:T(8,128)(2,1)S(1)}, bf16[2,64,1536]{2,1,0:T(8,128)(2,1)S(1)}, u32[]{:S(2)}, u32[]{:S(2)}) collective-permute-start(bf16[2,64,1536]{2,1,0:T(8,128)(2,1)S(1)} %pad_maximum_fusion.2), channel_id=1, source_target_pairs={{0,8},{4,12},{8,0},{12,4},{16,24},{20,28},{24,16},{28,20},{1,9},{5... | collective-permute-start | bytes 1179656 | tf_op jit(solution)/shard_map/ppermute | solution.py:578
  37.5 3.5 %copy-start.1 = (s32[32,8,128]{2,1,0:T(8,128)S(1)}, s32[32,8,128]{2,1,0:T(8,128)}, u32[]{:S(2)}) copy-start(s32[32,8,128]{2,1,0:T(8,128)} %copy-done) | copy-start | bytes 393220
  37.5 3.5 %copy-start.3 = (f32[384,128]{1,0:T(8,128)S(1)}, f32[384,128]{1,0:T(8,128)}, u32[]{:S(2)}) copy-start(f32[384,128]{1,0:T(8,128)} %get-tuple-element.39.refs_2_.refs_1_) | copy-start | bytes 589828
  37.5 3.5 %copy-start.8 = (s32[3]{0:T(128)S(1)}, s32[3]{0:T(128)}, u32[]{:S(2)}) copy-start(s32[3]{0:T(128)} %pad_add_fusion.refs_0_.me_ref) | copy-start | bytes 40
  37.5 15.2 %copy-start.2 = (bf16[2,384,512]{2,1,0:T(8,128)(2,1)S(1)}, bf16[2,384,512]{2,1,0:T(8,128)(2,1)}, u32[]{:S(2)}) copy-start(bf16[2,384,512]{2,1,0:T(8,128)(2,1)} %refs_4_.3) | copy-start | bytes 2359300
  37.5 15.2 %collective-permute-start.5 = (bf16[4,64,1536]{2,1,0:T(8,128)(2,1)}, bf16[4,64,1536]{2,1,0:T(8,128)(2,1)}, u32[]{:S(2)}, u32[]{:S(2)}) collective-permute-start(bf16[4,64,1536]{2,1,0:T(8,128)(2,1)} %pad_maximum_fusion.1.refs_7_), channel_id=1, source_target_pairs={{0,4},{4,0},{8,12},{12,8},{16,20},{20,16},{24,28},{28,24},{1,5},{5... | collective-permute-start | bytes 2359304 | tf_op jit(solution)/shard_map/ppermute | solution.py:578
  37.7 15.0 %collective-permute-start.3 = (bf16[4,64,1536]{2,1,0:T(8,128)(2,1)S(1)}, bf16[4,64,1536]{2,1,0:T(8,128)(2,1)}, u32[]{:S(2)}, u32[]{:S(2)}) collective-permute-start(bf16[4,64,1536]{2,1,0:T(8,128)(2,1)S(1)} %pad_maximum_fusion.refs_5_), channel_id=1, source_target_pairs={{0,4},{4,0},{8,12},{12,8},{16,20},{20,16},{24,28},{28,24},{1,5},{5... | collective-permute-start | bytes 2359304 | tf_op jit(solution)/shard_map/ppermute | solution.py:578
  38.3 14.4 %all-to-all-start.1 = ((bf16[32,48,128]{2,1,0:T(8,128)(2,1)}), bf16[32,48,128]{2,1,0:T(8,128)(2,1)S(1)}, u32[]{:S(2)}, u32[]{:S(2)}) async-start(bf16[32,48,128]{2,1,0:T(8,128)(2,1)} %get-tuple-element.38), calls=%async_computation.1 | async-start | bytes 786432 | tf_op jit(solution)/shard_map/all_to_all | solution.py:660
  42.2 0.6 copy-start.6
  52.7 0.7 copy-start.7
  73.2 0.9 copy-start.4
  74.0 0.7 copy-start.5
  74.8 4.5 %collective-permute-start.6 = (bf16[4,64,1536]{2,1,0:T(8,128)(2,1)}, bf16[4,64,1536]{2,1,0:T(8,128)(2,1)S(1)}, u32[]{:S(2)}, u32[]{:S(2)}) collective-permute-start(bf16[4,64,1536]{2,1,0:T(8,128)(2,1)} %get-tuple-element.52), channel_id=1, source_target_pairs={{0,4},{4,0},{8,12},{12,8},{16,20},{20,16},{24,28},{28,24},{1,5},{5... | collective-permute-start | bytes 2359304 | tf_op jit(solution)/shard_map/ppermute | solution.py:578
  76.0 6.3 %collective-permute-start.9 = (bf16[4,64,1536]{2,1,0:T(8,128)(2,1)}, bf16[4,64,1536]{2,1,0:T(8,128)(2,1)S(1)}, u32[]{:S(2)}, u32[]{:S(2)}) collective-permute-start(bf16[4,64,1536]{2,1,0:T(8,128)(2,1)} %get-tuple-element.54), channel_id=1, source_target_pairs={{0,4},{4,0},{8,12},{12,8},{16,20},{20,16},{24,28},{28,24},{1,5},{5... | collective-permute-start | bytes 2359304 | tf_op jit(solution)/shard_map/ppermute | solution.py:578
  76.0 42.0 %all-to-all-start.2 = ((bf16[32,48,128]{2,1,0:T(8,128)(2,1)}), bf16[32,48,128]{2,1,0:T(8,128)(2,1)S(1)}, u32[]{:S(2)}, u32[]{:S(2)}) async-start(bf16[32,48,128]{2,1,0:T(8,128)(2,1)} %copy-done.5), calls=%async_computation.2 | async-start | bytes 786432 | tf_op jit(solution)/shard_map/all_to_all | solution.py:724
  80.7 14.0 %collective-permute-start.7 = (bf16[2,64,1536]{2,1,0:T(8,128)(2,1)S(1)}, bf16[2,64,1536]{2,1,0:T(8,128)(2,1)S(1)}, u32[]{:S(2)}, u32[]{:S(2)}) collective-permute-start(bf16[2,64,1536]{2,1,0:T(8,128)(2,1)S(1)} %get-tuple-element.59), channel_id=1, source_target_pairs={{0,8},{4,12},{8,0},{12,4},{16,24},{20,28},{24,16},{28,20},{1,9},{5... | collective-permute-start | bytes 1179656 | tf_op jit(solution)/shard_map/ppermute | solution.py:578
  82.5 13.9 %collective-permute-start.10 = (bf16[2,64,1536]{2,1,0:T(8,128)(2,1)S(1)}, bf16[2,64,1536]{2,1,0:T(8,128)(2,1)S(1)}, u32[]{:S(2)}, u32[]{:S(2)}) collective-permute-start(bf16[2,64,1536]{2,1,0:T(8,128)(2,1)S(1)} %get-tuple-element.61), channel_id=1, source_target_pairs={{0,16},{4,20},{8,24},{12,28},{16,0},{20,4},{24,8},{28,12},{1,17},{... | collective-permute-start | bytes 1179656 | tf_op jit(solution)/shard_map/ppermute | solution.py:578
  94.8 6.5 %collective-permute-start.8 = (bf16[1,64,1536]{2,1,0:T(8,128)(2,1)S(1)}, bf16[1,64,1536]{2,1,0:T(8,128)(2,1)S(1)}, u32[]{:S(2)}, u32[]{:S(2)}) collective-permute-start(bf16[1,64,1536]{2,1,0:T(8,128)(2,1)S(1)} %get-tuple-element.63), channel_id=1, source_target_pairs={{0,16},{4,20},{8,24},{12,28},{16,0},{20,4},{24,8},{28,12},{1,17},{... | collective-permute-start | bytes 589832 | tf_op jit(solution)/shard_map/ppermute | solution.py:578
  96.5 6.3 %collective-permute-start.11 = (bf16[1,64,1536]{2,1,0:T(8,128)(2,1)S(1)}, bf16[1,64,1536]{2,1,0:T(8,128)(2,1)S(1)}, u32[]{:S(2)}, u32[]{:S(2)}) collective-permute-start(bf16[1,64,1536]{2,1,0:T(8,128)(2,1)S(1)} %get-tuple-element.65), channel_id=1, source_target_pairs={{0,8},{4,12},{8,0},{12,4},{16,24},{20,28},{24,16},{28,20},{1,9},{5... | collective-permute-start | bytes 589832 | tf_op jit(solution)/shard_map/ppermute | solution.py:578
  103.0 5.1 %collective-permute-start.12 = (bf16[64,768]{1,0:T(8,128)(2,1)S(1)}, bf16[64,768]{1,0:T(8,128)(2,1)S(1)}, u32[]{:S(2)}, u32[]{:S(2)}) collective-permute-start(bf16[64,768]{1,0:T(8,128)(2,1)S(1)} %get-tuple-element.66), channel_id=1, source_target_pairs={{0,1},{1,0},{2,3},{3,2},{4,5},{5,4},{6,7},{7,6},{8,9},{9,8},{10,11... | collective-permute-start | bytes 294920 | tf_op jit(solution)/shard_map/ppermute | solution.py:578
  104.3 9.2 %collective-permute-start.13 = (bf16[64,768]{1,0:T(8,128)(2,1)S(1)}, bf16[64,768]{1,0:T(8,128)(2,1)S(1)}, u32[]{:S(2)}, u32[]{:S(2)}) collective-permute-start(bf16[64,768]{1,0:T(8,128)(2,1)S(1)} %get-tuple-element.68), channel_id=1, source_target_pairs={{0,2},{1,3},{2,0},{3,1},{4,6},{5,7},{6,4},{7,5},{8,10},{9,11},{10,... | collective-permute-start | bytes 294920 | tf_op jit(solution)/shard_map/ppermute | solution.py:578
  106.9 6.6 %collective-permute-start.14 = (bf16[64,768]{1,0:T(8,128)(2,1)S(1)}, bf16[64,768]{1,0:T(8,128)(2,1)S(1)}, u32[]{:S(2)}, u32[]{:S(2)}) collective-permute-start(bf16[64,768]{1,0:T(8,128)(2,1)S(1)} %get-tuple-element.67), channel_id=1, source_target_pairs={{0,3},{1,2},{2,1},{3,0},{4,7},{5,6},{6,5},{7,4},{8,11},{9,10},{10,... | collective-permute-start | bytes 294920 | tf_op jit(solution)/shard_map/ppermute | solution.py:578
  113.6 10.1 %collective-permute-start.15 = (bf16[64,768]{1,0:T(8,128)(2,1)S(1)}, bf16[64,768]{1,0:T(8,128)(2,1)S(1)}, u32[]{:S(2)}, u32[]{:S(2)}) collective-permute-start(bf16[64,768]{1,0:T(8,128)(2,1)S(1)} %fusion.2.refs_0_), channel_id=1, source_target_pairs={{0,1},{1,0},{2,3},{3,2},{4,5},{5,4},{6,7},{7,6},{8,9},{9,8},{10,11... | collective-permute-start | bytes 294920 | tf_op jit(solution)/shard_map/ppermute | solution.py:578
  115.2 8.5 %collective-permute-start.16 = (bf16[64,768]{1,0:T(8,128)(2,1)S(1)}, bf16[64,768]{1,0:T(8,128)(2,1)S(1)}, u32[]{:S(2)}, u32[]{:S(2)}) collective-permute-start(bf16[64,768]{1,0:T(8,128)(2,1)S(1)} %fusion.2.refs_0_), channel_id=1, source_target_pairs={{0,2},{1,3},{2,0},{3,1},{4,6},{5,7},{6,4},{7,5},{8,10},{9,11},{10,... | collective-permute-start | bytes 294920 | tf_op jit(solution)/shard_map/ppermute | solution.py:578
  116.6 7.1 %collective-permute-start.17 = (bf16[64,768]{1,0:T(8,128)(2,1)S(1)}, bf16[64,768]{1,0:T(8,128)(2,1)S(1)}, u32[]{:S(2)}, u32[]{:S(2)}) collective-permute-start(bf16[64,768]{1,0:T(8,128)(2,1)S(1)} %fusion.2.refs_0_), channel_id=1, source_target_pairs={{0,3},{1,2},{2,1},{3,0},{4,7},{5,6},{6,5},{7,4},{8,11},{9,10},{10,... | collective-permute-start | bytes 294920 | tf_op jit(solution)/shard_map/ppermute | solution.py:578

commit v4 on v3

--- a/solution.py
+++ b/solution.py
@@ -146,14 +146,17 @@
     table_refs, refs = refs[:4], refs[4:]
     send_ref, idxc_ref = refs[:2]
     held = refs[2:6]
-    rows_scr, pack_scr, sems = refs[6:]
+    rows_scr, pack_scr, ids_scr, sems = refs[6:]
+    ids_copy = pltpu.make_async_copy(ids_ref, ids_scr, sems.at[4])
+    ids_copy.start()
     copies = [pltpu.make_async_copy(table_refs[i], held[i], sems.at[i]) for i in range(4)]
     for copy in copies:
         copy.start()
     me = me_ref[0]
     seqs = devices * seq_count
     slots = devices * capacity
-    items, kinds, _, target = read_ids(ids_ref, devices, seq_count, span, row_counts)
+    ids_copy.wait()
+    items, kinds, _, target = read_ids(ids_scr, devices, seq_count, span, row_counts)
     owner, row = owner_and_row(items, kinds, row_counts)
     fields = jnp.concatenate(
         [
@@ -242,7 +245,7 @@
             folded = folded + total[:, b * 128 : (b + 1) * 128]
         folded = folded + pltpu.roll(folded, 64, 1)
         narrow.append(folded)
-    rows_scr[0] = jnp.where(iota((slots, 128), 1) < widths[0], narrow[0], narrow[1])
+    rows_scr[0, :slots] = jnp.where(iota((slots, 128), 1) < widths[0], narrow[0], narrow[1])
     for which in range(2, 4):
         width = widths[which]
         chosen = pick(which)
@@ -251,7 +254,7 @@
             found = dot(chosen, held[which][step * SPLIT : (step + 1) * SPLIT, :])
             total = jnp.where(highs[which] == float(step), found, total)
         for b in range(width // 128):
-            rows_scr[which - 1 + b] = total[:, b * 128 : (b + 1) * 128]
+            rows_scr[which - 1 + b, :slots] = total[:, b * 128 : (b + 1) * 128]
 
     def pack(device, carry):
         for j in range(4):
@@ -261,7 +264,7 @@
         return carry
 
     lax.fori_loop(0, devices, pack, 0)
-    send_ref[...] = pack_scr[...].astype(BF16)
+    send_ref[...] = pack_scr[:devices].astype(BF16)
 
 
 def layer_kernel(
@@ -301,7 +304,7 @@
     fetches.append(pltpu.make_async_copy(cot_ref, cot_scr, io_sems.at[0]))
     for copy in fetches:
         copy.start()
-    pack_scr[...] = got_ref[...].astype(F32)
+    pack_scr[:devices] = got_ref[...].astype(F32)
 
     def unpack(device, carry):
         for j in range(4):
@@ -311,7 +314,7 @@
         return carry
 
     lax.fori_loop(0, devices, unpack, 0)
-    arrived = jnp.concatenate([slot_scr[j].astype(BF16) for j in range(4)], axis=1)
+    arrived = jnp.concatenate([slot_scr[j, :slots].astype(BF16) for j in range(4)], axis=1)
 
     def in_part(j):
         return wa[:, j * width : (j + 1) * width] if j < 3 else wb[:, :width]
@@ -460,7 +463,7 @@
     chosen = onehot(iota((slots, toks), 0) == info_ref[0:1, :].astype(jnp.int32))
     outgoing = dot(chosen, drow_scr[...])
     for j in range(4):
-        slot_scr[j] = outgoing[:, j * 128 : (j + 1) * 128]
+        slot_scr[j, :slots] = outgoing[:, j * 128 : (j + 1) * 128]
 
     def pack(device, carry):
         for j in range(4):
@@ -470,7 +473,7 @@
         return carry
 
     lax.fori_loop(0, devices, pack, 0)
-    back_scr[...] = pack_scr[...].astype(BF16)
+    back_scr[...] = pack_scr[:devices].astype(BF16)
     back_copy = pltpu.make_async_copy(back_scr, back_ref, io_sems.at[1])
     back_copy.start()
     middle = dp_count // 2
@@ -501,7 +504,7 @@
     held = refs[7:11]
     slot_scr, pack_scr, sems = refs[11:]
     slots = devices * capacity
-    pack_scr[...] = got_ref[...].astype(F32)
+    pack_scr[:devices] = got_ref[...].astype(F32)
 
     def unpack(device, carry):
         for j in range(4):
@@ -512,7 +515,7 @@
 
     lax.fori_loop(0, devices, unpack, 0)
     copies = [pltpu.make_async_copy(held[i], outs[i], sems.at[i]) for i in range(4)]
-    first = slot_scr[0]
+    first = slot_scr[0, :slots]
     rolled = pltpu.roll(first, 64, 1)
     left = iota((slots, 128), 1) < widths[0]
     pairs = [jnp.where(left, first, rolled), jnp.where(left, rolled, first)]
@@ -545,7 +548,7 @@
         low = idxr_ref[4 + which : 5 + which, :].astype(jnp.int32)
         chosen = onehot(iota((SPLIT, slots), 0) == low)
         wide = jnp.concatenate(
-            [slot_scr[which - 1 + b] for b in range(width // 128)], axis=1
+            [slot_scr[which - 1 + b, :slots] for b in range(width // 128)], axis=1
         )
         for g in range(steps // group):
             part = jnp.concatenate(
@@ -640,16 +643,17 @@
             jax.ShapeDtypeStruct((devices, 4 * capacity, 128), BF16),
             jax.ShapeDtypeStruct((slots, 128), F32),
         ),
-        in_specs=[SM, VM] + [HB] * 4,
+        in_specs=[SM, HB] + [HB] * 4,
         out_specs=(VM,) * 2,
         scratch_shapes=[
             pltpu.VMEM((widths[0], row_counts[0]), BF16),
             pltpu.VMEM((widths[1], row_counts[1]), BF16),
             pltpu.VMEM((row_counts[2], widths[2]), BF16),
             pltpu.VMEM((row_counts[3], widths[3]), BF16),
-            pltpu.VMEM((4, slots, 128), F32),
-            pltpu.VMEM((devices, 4 * capacity, 128), F32),
-            pltpu.SemaphoreType.DMA((4,)),
+            pltpu.VMEM((4, slots + 8, 128), F32),
+            pltpu.VMEM((devices + 1, 4 * capacity, 128), F32),
+            pltpu.VMEM((devices, seq_count * lanes, 128), jnp.int32),
+            pltpu.SemaphoreType.DMA((5,)),
         ],
         compiler_params=params(60),
         name="plan",
@@ -688,8 +692,8 @@
         scratch_shapes=[
             pltpu.VMEM((width, half), BF16),
             pltpu.VMEM((width, half), BF16),
-            pltpu.VMEM((4, slots, 128), F32),
-            pltpu.VMEM((devices, 4 * capacity, 128), F32),
+            pltpu.VMEM((4, slots + 8, 128), F32),
+            pltpu.VMEM((devices + 1, 4 * capacity, 128), F32),
             pltpu.VMEM((toks, width), BF16),
             pltpu.VMEM((toks, width), BF16),
             pltpu.VMEM((4, span, width), BF16),
@@ -712,7 +716,7 @@
             pltpu.SemaphoreType.DMA((2 * dp_count,)),
             pltpu.SemaphoreType.DMA((2 + seq_count,)),
         ],
-        compiler_params=params(48),
+        compiler_params=params(50),
         name="layer",
     )(me, got, info, infot, cotangent, *wa, *wb)
 
@@ -770,8 +774,8 @@
             pltpu.VMEM((widths[1], row_counts[1]), BF16),
             pltpu.VMEM((row_counts[2], widths[2]), BF16),
             pltpu.VMEM((row_counts[3], widths[3]), BF16),
-            pltpu.VMEM((4, slots, 128), F32),
-            pltpu.VMEM((devices, 4 * capacity, 128), F32),
+            pltpu.VMEM((4, slots + 8, 128), F32),
+            pltpu.VMEM((devices + 1, 4 * capacity, 128), F32),
             pltpu.SemaphoreType.DMA((4,)),
         ],
         compiler_params=params(26),

time: 126 us -> 124 us (0.984)
  local copies, waits for them, and re-layouts: 5.44 us -> 2.5 us
  waiting for transfers between devices: 42.6 us -> 44 us
    unnamed x18 -> x12, local copies, waits for them, and re-layouts: 3.62 us -> 0.69 us
  transfers between devices with their start and end apart: 21 -> 21, of which waited for: 8 -> 10; matrix products, arithmetic and copies ran while one was open for 5% -> 5% of each run, Pallas kernels for 12% -> 12%
where the time goes in v4:
time: 124 us
  waiting for transfers between devices  44 us (35%)
  Pallas kernels  37.4 us (30%)
  starting transfers between devices  34.3 us (28%)
  other arithmetic  4.82 us (4%)
  local copies, waits for them, and re-layouts  2.5 us (2%)
    ppermute x18, waiting for transfers between devices, exchange(): return lax.ppermute(value, axis, [(i, i ^ mask) for i in range(count)])  31.6 us
    ppermute x18, starting transfers between devices, exchange(): return lax.ppermute(value, axis, [(i, i ^ mask) for i in range(count)])  20.9 us
    pallas_call x1, Pallas kernels, step(): pl.pallas_call(functools.partial(layer_kernel, devices, seq_count, span,...  20.1 us
    all_to_all x1, waiting for transfers between devices, step(): got = lax.all_to_all(send, ('dp', 'table'), 0, 0, tiled=True)  10.5 us
    pallas_call x1, Pallas kernels, step(): pl.pallas_call(functools.partial(plan_kernel, devices, seq_count, span, c...  7.59 us
    all_to_all x1, starting transfers between devices, step(): ids = lax.all_to_all(packed, ('dp', 'table'), 0, 0, tiled=True)  7.33 us
    pallas_call x1, Pallas kernels, step(): pl.pallas_call(functools.partial(scatter_kernel, devices, capacity, row_c...  5.67 us
    all_to_all x1, starting transfers between devices, step(): returned = lax.all_to_all(back, ('dp', 'table'), 0, 0, tiled=True)  3.24 us
  transfers between devices with their start and end apart: 21, of which 10 were waited for; matrix products, arithmetic and copies ran while one was open for 5% of the time, Pallas kernels for 12%

profile of v4, /device:TPU:0, one launch (start us, length us, event | category | flops | bytes accessed | tf_op | source)
XLA Modules:
  0.0 123.9 jit_solution(7499458417540611584)
XLA Ops:
  0.6 1.4 %key.1 = s32[32,8,128]{2,1,0:T(8,128)} custom-call(s32[2]{0:T(128)} %len_ref.1, s32[2]{0:T(128)} %to_ref.1, s32[2,384]{1,0:T(2,128)} %item_ref.1, s32[2,384]{1,0:T(2,128)} %kind_ref.1), custom_call_target="tpu_custom_call" | custom-call | tf_op jit(solution)/shard_map/key/pallas_call | solution.py:613
  2.0 7.3 %all-to-all-start = ((s32[32,8,128]{2,1,0:T(8,128)}), s32[32,8,128]{2,1,0:T(8,128)S(1)}, u32[]{:S(2)}, u32[]{:S(2)}) async-start(s32[32,8,128]{2,1,0:T(8,128)} %key.1), calls=%async_computation | async-start | bytes 262144 | tf_op jit(solution)/shard_map/all_to_all | solution.py:624
  10.2 0.9 maximum_bitcast_fusion
  11.1 1.8 %collective-permute-start.1 = (bf16[1,64,1536]{2,1,0:T(8,128)(2,1)S(1)}, bf16[1,64,1536]{2,1,0:T(8,128)(2,1)S(1)}, u32[]{:S(2)}, u32[]{:S(2)}) collective-permute-start(bf16[1,64,1536]{2,1,0:T(8,128)(2,1)S(1)} %maximum_bitcast_fusion), channel_id=1, source_target_pairs={{0,8},{4,12},{8,0},{12,4},{16,24},{20,28},{24,16},{28,20},{1,9},{5... | collective-permute-start | bytes 589832 | tf_op jit(solution)/shard_map/ppermute | solution.py:581
  12.9 0.9 slice_bitcast_fusion
  13.9 1.5 %collective-permute-start = (bf16[1,64,1536]{2,1,0:T(8,128)(2,1)S(1)}, bf16[1,64,1536]{2,1,0:T(8,128)(2,1)S(1)}, u32[]{:S(2)}, u32[]{:S(2)}) collective-permute-start(bf16[1,64,1536]{2,1,0:T(8,128)(2,1)S(1)} %slice_bitcast_fusion), channel_id=1, source_target_pairs={{0,16},{4,20},{8,24},{12,28},{16,0},{20,4},{24,8},{28,12},{1,17},{... | collective-permute-start | bytes 589832 | tf_op jit(solution)/shard_map/ppermute | solution.py:581
  16.0 1.9 %all-to-all-done.refs_1_ = s32[32,8,128]{2,1,0:T(8,128)S(1)} async-done(((s32[32,8,128]{2,1,0:T(8,128)}), s32[32,8,128]{2,1,0:T(8,128)S(1)}, u32[]{:S(2)}, u32[]{:S(2)}) %all-to-all-start) | async-done | bytes 131104 | tf_op jit(solution)/shard_map/all_to_all | solution.py:624
  18.5 7.6 %plan.1 = (bf16[32,48,128]{2,1,0:T(8,128)(2,1)}, f32[384,128]{1,0:T(8,128)}) custom-call(s32[3]{0:T(128)} %pad_add_fusion.refs_0_.me_ref, s32[32,8,128]{2,1,0:T(8,128)} %copy-done, bf16[64,12288]{1,0:T(8,128)(2,1)} %bitcast.20, bf16[64,12288]{1,0:T(8,128)(2,1)} %bitcast.21, bf16[6144,128]{1,0:T(8,128)(2,1)} %refs_4_.2, bf16[2048,256]{1,0:T(8,128)(2,1)} %refs_5_.1), custom_call_target="tpu_custom_call" | custom-call | tf_op jit(solution)/shard_map/plan/pallas_call | solution.py:638
  27.5 8.9 %collective-permute-done.4 = bf16[2,64,1536]{2,1,0:T(8,128)(2,1)S(1)} collective-permute-done((bf16[2,64,1536]{2,1,0:T(8,128)(2,1)S(1)}, bf16[2,64,1536]{2,1,0:T(8,128)(2,1)S(1)}, u32[]{:S(2)}, u32[]{:S(2)}) %collective-permute-start.4) | collective-permute-done | bytes 393248 | tf_op jit(solution)/shard_map/ppermute | solution.py:581
  37.6 2.9 %all-to-all-start.1 = ((bf16[32,48,128]{2,1,0:T(8,128)(2,1)}), bf16[32,48,128]{2,1,0:T(8,128)(2,1)S(1)}, u32[]{:S(2)}, u32[]{:S(2)}) async-start(bf16[32,48,128]{2,1,0:T(8,128)(2,1)} %get-tuple-element.38), calls=%async_computation.1 | async-start | bytes 786432 | tf_op jit(solution)/shard_map/all_to_all | solution.py:664
  40.5 1.1 own.1
  41.6 10.5 %all-to-all-done.1.refs_1_ = bf16[32,48,128]{2,1,0:T(8,128)(2,1)S(1)} async-done(((bf16[32,48,128]{2,1,0:T(8,128)(2,1)}), bf16[32,48,128]{2,1,0:T(8,128)(2,1)S(1)}, u32[]{:S(2)}, u32[]{:S(2)}) %all-to-all-start.1) | async-done | bytes 393248 | tf_op jit(solution)/shard_map/all_to_all | solution.py:664
  52.1 20.1 %layer.1 = (bf16[2,384,512]{2,1,0:T(8,128)(2,1)}, bf16[32,48,128]{2,1,0:T(8,128)(2,1)}, bf16[4,64,1536]{2,1,0:T(8,128)(2,1)S(1)}, bf16[4,64,1536]{2,1,0:T(8,128)...) custom-call(s32[3]{0:T(128)S(1)} %copy-done.3, bf16[32,48,128]{2,1,0:T(8,128)(2,1)S(1)} %all-to-all-done.1.refs_1_, ...), custom_call_target="tpu_custom_call" | custom-call | tf_op jit(solution)/shard_map/layer/pallas_call | solution.py:680
  72.2 1.3 %collective-permute-start.6 = (bf16[4,64,1536]{2,1,0:T(8,128)(2,1)}, bf16[4,64,1536]{2,1,0:T(8,128)(2,1)}, u32[]{:S(2)}, u32[]{:S(2)}) collective-permute-start(bf16[4,64,1536]{2,1,0:T(8,128)(2,1)} %get-tuple-element.52), channel_id=1, source_target_pairs={{0,4},{4,0},{8,12},{12,8},{16,20},{20,16},{24,28},{28,24},{1,5},{5... | collective-permute-start | bytes 2359304 | tf_op jit(solution)/shard_map/ppermute | solution.py:581
  73.6 3.2 %all-to-all-start.2 = ((bf16[32,48,128]{2,1,0:T(8,128)(2,1)}), bf16[32,48,128]{2,1,0:T(8,128)(2,1)S(1)}, u32[]{:S(2)}, u32[]{:S(2)}) async-start(bf16[32,48,128]{2,1,0:T(8,128)(2,1)} %get-tuple-element.45), calls=%async_computation.2 | async-start | bytes 786432 | tf_op jit(solution)/shard_map/all_to_all | solution.py:728
  76.8 1.4 %add_convert_fusion.3 = (bf16[2,64,1536]{2,1,0:T(8,128)(2,1)S(1)}, bf16[2,64,1536]{2,1,0:T(8,128)(2,1)S(1)}) fusion(bf16[4,64,1536]{2,1,0:T(8,128)(2,1)} %collective-permute-done.6, bf16[4,64,1536]{2,1,0:T(8,128)(2,1)S(1)} %get-tuple-element.51), kind=kLoop, calls=%fused_computation.5 | loop fusion | flops 1572864 | bytes 2359296 | tf_op jit(solution)/shard_map/convert_element_type | solution.py:726
  78.2 1.6 %collective-permute-start.7 = (bf16[2,64,1536]{2,1,0:T(8,128)(2,1)S(1)}, bf16[2,64,1536]{2,1,0:T(8,128)(2,1)S(1)}, u32[]{:S(2)}, u32[]{:S(2)}) collective-permute-start(bf16[2,64,1536]{2,1,0:T(8,128)(2,1)S(1)} %get-tuple-element.59), channel_id=1, source_target_pairs={{0,8},{4,12},{8,0},{12,4},{16,24},{20,28},{24,16},{28,20},{1,9},{5... | collective-permute-start | bytes 1179656 | tf_op jit(solution)/shard_map/ppermute | solution.py:581
  79.8 1.4 %add_convert_fusion.1 = (bf16[2,64,1536]{2,1,0:T(8,128)(2,1)S(1)}, bf16[2,64,1536]{2,1,0:T(8,128)(2,1)S(1)}) fusion(bf16[4,64,1536]{2,1,0:T(8,128)(2,1)} %collective-permute-done.9, bf16[4,64,1536]{2,1,0:T(8,128)(2,1)S(1)} %get-tuple-element.53), kind=kLoop, calls=%fused_computation.3 | loop fusion | flops 1572864 | bytes 2359296 | tf_op jit(solution)/shard_map/convert_element_type | solution.py:726
  81.2 1.5 %collective-permute-start.10 = (bf16[2,64,1536]{2,1,0:T(8,128)(2,1)S(1)}, bf16[2,64,1536]{2,1,0:T(8,128)(2,1)S(1)}, u32[]{:S(2)}, u32[]{:S(2)}) collective-permute-start(bf16[2,64,1536]{2,1,0:T(8,128)(2,1)S(1)} %get-tuple-element.61), channel_id=1, source_target_pairs={{0,16},{4,20},{8,24},{12,28},{16,0},{20,4},{24,8},{28,12},{1,17},{... | collective-permute-start | bytes 1179656 | tf_op jit(solution)/shard_map/ppermute | solution.py:581
  82.7 9.5 %collective-permute-done.7 = bf16[2,64,1536]{2,1,0:T(8,128)(2,1)S(1)} collective-permute-done((bf16[2,64,1536]{2,1,0:T(8,128)(2,1)S(1)}, bf16[2,64,1536]{2,1,0:T(8,128)(2,1)S(1)}, u32[]{:S(2)}, u32[]{:S(2)}) %collective-permute-start.7) | collective-permute-done | bytes 393248 | tf_op jit(solution)/shard_map/ppermute | solution.py:581
  92.3 1.6 %collective-permute-start.8 = (bf16[1,64,1536]{2,1,0:T(8,128)(2,1)S(1)}, bf16[1,64,1536]{2,1,0:T(8,128)(2,1)S(1)}, u32[]{:S(2)}, u32[]{:S(2)}) collective-permute-start(bf16[1,64,1536]{2,1,0:T(8,128)(2,1)S(1)} %get-tuple-element.63), channel_id=1, source_target_pairs={{0,16},{4,20},{8,24},{12,28},{16,0},{20,4},{24,8},{28,12},{1,17},{... | collective-permute-start | bytes 589832 | tf_op jit(solution)/shard_map/ppermute | solution.py:581
  94.0 1.0 collective-permute-start.11
  95.1 3.8 %collective-permute-done.8 = bf16[1,64,1536]{2,1,0:T(8,128)(2,1)S(1)} collective-permute-done((bf16[1,64,1536]{2,1,0:T(8,128)(2,1)S(1)}, bf16[1,64,1536]{2,1,0:T(8,128)(2,1)S(1)}, u32[]{:S(2)}, u32[]{:S(2)}) %collective-permute-start.8) | collective-permute-done | bytes 196640 | tf_op jit(solution)/shard_map/ppermute | solution.py:581
  98.9 1.4 %collective-permute-done.11 = bf16[1,64,1536]{2,1,0:T(8,128)(2,1)S(1)} collective-permute-done((bf16[1,64,1536]{2,1,0:T(8,128)(2,1)S(1)}, bf16[1,64,1536]{2,1,0:T(8,128)(2,1)S(1)}, u32[]{:S(2)}, u32[]{:S(2)}) %collective-permute-start.11) | collective-permute-done | bytes 196640 | tf_op jit(solution)/shard_map/ppermute | solution.py:581
  100.5 1.3 %collective-permute-start.12 = (bf16[64,768]{1,0:T(8,128)(2,1)S(1)}, bf16[64,768]{1,0:T(8,128)(2,1)S(1)}, u32[]{:S(2)}, u32[]{:S(2)}) collective-permute-start(bf16[64,768]{1,0:T(8,128)(2,1)S(1)} %get-tuple-element.66), channel_id=1, source_target_pairs={{0,1},{1,0},{2,3},{3,2},{4,5},{5,4},{6,7},{7,6},{8,9},{9,8},{10,11... | collective-permute-start | bytes 294920 | tf_op jit(solution)/shard_map/ppermute | solution.py:581
  101.8 2.6 %collective-permute-start.13 = (bf16[64,768]{1,0:T(8,128)(2,1)S(1)}, bf16[64,768]{1,0:T(8,128)(2,1)S(1)}, u32[]{:S(2)}, u32[]{:S(2)}) collective-permute-start(bf16[64,768]{1,0:T(8,128)(2,1)S(1)} %get-tuple-element.68), channel_id=1, source_target_pairs={{0,2},{1,3},{2,0},{3,1},{4,6},{5,7},{6,4},{7,5},{8,10},{9,11},{10,... | collective-permute-start | bytes 294920 | tf_op jit(solution)/shard_map/ppermute | solution.py:581
  105.7 5.7 %collective-permute-done.13 = bf16[64,768]{1,0:T(8,128)(2,1)S(1)} collective-permute-done((bf16[64,768]{1,0:T(8,128)(2,1)S(1)}, bf16[64,768]{1,0:T(8,128)(2,1)S(1)}, u32[]{:S(2)}, u32[]{:S(2)}) %collective-permute-start.13) | collective-permute-done | bytes 98336 | tf_op jit(solution)/shard_map/ppermute | solution.py:581
  111.5 1.7 %collective-permute-start.15 = (bf16[64,768]{1,0:T(8,128)(2,1)S(1)}, bf16[64,768]{1,0:T(8,128)(2,1)S(1)}, u32[]{:S(2)}, u32[]{:S(2)}) collective-permute-start(bf16[64,768]{1,0:T(8,128)(2,1)S(1)} %fusion.2.refs_0_), channel_id=1, source_target_pairs={{0,1},{1,0},{2,3},{3,2},{4,5},{5,4},{6,7},{7,6},{8,9},{9,8},{10,11... | collective-permute-start | bytes 294920 | tf_op jit(solution)/shard_map/ppermute | solution.py:581
  113.2 1.6 %collective-permute-start.16 = (bf16[64,768]{1,0:T(8,128)(2,1)S(1)}, bf16[64,768]{1,0:T(8,128)(2,1)S(1)}, u32[]{:S(2)}, u32[]{:S(2)}) collective-permute-start(bf16[64,768]{1,0:T(8,128)(2,1)S(1)} %fusion.2.refs_0_), channel_id=1, source_target_pairs={{0,2},{1,3},{2,0},{3,1},{4,6},{5,7},{6,4},{7,5},{8,10},{9,11},{10,... | collective-permute-start | bytes 294920 | tf_op jit(solution)/shard_map/ppermute | solution.py:581
  114.8 1.2 collective-permute-start.17
  116.0 5.7 %scatter.1 = (bf16[64,12288]{1,0:T(8,128)(2,1)}, bf16[64,12288]{1,0:T(8,128)(2,1)}, bf16[6144,128]{1,0:T(8,128)(2,1)}, bf16[2048,256]{1,0:T(8,128)(2,1)}) custom-call(bf16[32,48,128]{2,1,0:T(8,128)(2,1)S(1)} %all-to-all-done.2.refs_0_, f32[384,128]{1,0:T(8,128)S(1)} %copy-done.2, f32[128,384]{1,0:T(8,128)S(1)} %get-tuple-element.46.refs_2_), custom_call_target="tpu_custom_call" | custom-call | tf_op jit(solution)/shard_map/scatter/pallas_call | solution.py:762
  122.4 1.5 %join.1 = (f32[64,512]{1,0:T(8,128)}, f32[64,2048]{1,0:T(8,128)}, f32[64,512]{1,0:T(8,128)}) custom-call(s32[3]{0:T(128)S(1)} %copy-done.3, bf16[64,768]{1,0:T(8,128)(2,1)S(1)} %fusion.2.refs_0_, bf16[64,768]{1,0:T(8,128)(2,1)S(1)} %collective-permute-done.15.refs_1_, bf16[64,768]{1,0:T(8,128)(2,1)S(1)} %collective-permute-done.16.refs_2_, ...), custom_call_target="tpu_custom_call" | custom-call | tf_op jit(solution)/shard_map/join/pallas_call | solution.py:749
  (45 shorter events, 7.2 us)
Async XLA Ops:
  2.0 15.8 %all-to-all-start = ((s32[32,8,128]{2,1,0:T(8,128)}), s32[32,8,128]{2,1,0:T(8,128)S(1)}, u32[]{:S(2)}, u32[]{:S(2)}) async-start(s32[32,8,128]{2,1,0:T(8,128)} %key.1), calls=%async_computation | async-start | bytes 262144 | tf_op jit(solution)/shard_map/all_to_all | solution.py:624
  11.1 15.0 %collective-permute-start.1 = (bf16[1,64,1536]{2,1,0:T(8,128)(2,1)S(1)}, bf16[1,64,1536]{2,1,0:T(8,128)(2,1)S(1)}, u32[]{:S(2)}, u32[]{:S(2)}) collective-permute-start(bf16[1,64,1536]{2,1,0:T(8,128)(2,1)S(1)} %maximum_bitcast_fusion), channel_id=1, source_target_pairs={{0,8},{4,12},{8,0},{12,4},{16,24},{20,28},{24,16},{28,20},{1,9},{5... | collective-permute-start | bytes 589832 | tf_op jit(solution)/shard_map/ppermute | solution.py:581
  13.9 12.2 %collective-permute-start = (bf16[1,64,1536]{2,1,0:T(8,128)(2,1)S(1)}, bf16[1,64,1536]{2,1,0:T(8,128)(2,1)S(1)}, u32[]{:S(2)}, u32[]{:S(2)}) collective-permute-start(bf16[1,64,1536]{2,1,0:T(8,128)(2,1)S(1)} %slice_bitcast_fusion), channel_id=1, source_target_pairs={{0,16},{4,20},{8,24},{12,28},{16,0},{20,4},{24,8},{28,12},{1,17},{... | collective-permute-start | bytes 589832 | tf_op jit(solution)/shard_map/ppermute | solution.py:581
  17.8 0.7 copy-start
  26.2 10.2 %collective-permute-start.4 = (bf16[2,64,1536]{2,1,0:T(8,128)(2,1)S(1)}, bf16[2,64,1536]{2,1,0:T(8,128)(2,1)S(1)}, u32[]{:S(2)}, u32[]{:S(2)}) collective-permute-start(bf16[2,64,1536]{2,1,0:T(8,128)(2,1)S(1)} %pad_maximum_fusion.3), channel_id=1, source_target_pairs={{0,16},{4,20},{8,24},{12,28},{16,0},{20,4},{24,8},{28,12},{1,17},{... | collective-permute-start | bytes 1179656 | tf_op jit(solution)/shard_map/ppermute | solution.py:581
  26.9 10.4 %collective-permute-start.2 = (bf16[2,64,1536]{2,1,0:T(8,128)(2,1)S(1)}, bf16[2,64,1536]{2,1,0:T(8,128)(2,1)S(1)}, u32[]{:S(2)}, u32[]{:S(2)}) collective-permute-start(bf16[2,64,1536]{2,1,0:T(8,128)(2,1)S(1)} %pad_maximum_fusion.2), channel_id=1, source_target_pairs={{0,8},{4,12},{8,0},{12,4},{16,24},{20,28},{24,16},{28,20},{1,9},{5... | collective-permute-start | bytes 1179656 | tf_op jit(solution)/shard_map/ppermute | solution.py:581
  36.5 15.6 %copy-start.4 = (bf16[4,64,1536]{2,1,0:T(8,128)(2,1)}, bf16[4,64,1536]{2,1,0:T(8,128)(2,1)S(1)}, u32[]{:S(2)}) copy-start(bf16[4,64,1536]{2,1,0:T(8,128)(2,1)S(1)} %pad_maximum_fusion.1.refs_7_) | copy-start | bytes 2359300
  36.5 4.0 %copy-start.1 = (s32[32,8,128]{2,1,0:T(8,128)S(1)}, s32[32,8,128]{2,1,0:T(8,128)}, u32[]{:S(2)}) copy-start(s32[32,8,128]{2,1,0:T(8,128)} %copy-done) | copy-start | bytes 393220
  36.5 4.0 %copy-start.2 = (f32[384,128]{1,0:T(8,128)S(1)}, f32[384,128]{1,0:T(8,128)}, u32[]{:S(2)}) copy-start(f32[384,128]{1,0:T(8,128)} %get-tuple-element.39.refs_2_.refs_1_) | copy-start | bytes 589828
  36.5 4.0 %copy-start.3 = (s32[3]{0:T(128)S(1)}, s32[3]{0:T(128)}, u32[]{:S(2)}) copy-start(s32[3]{0:T(128)} %pad_add_fusion.refs_0_.me_ref) | copy-start | bytes 40
  36.5 15.6 %collective-permute-start.5 = (bf16[4,64,1536]{2,1,0:T(8,128)(2,1)S(1)}, bf16[4,64,1536]{2,1,0:T(8,128)(2,1)}, u32[]{:S(2)}, u32[]{:S(2)}) collective-permute-start(bf16[4,64,1536]{2,1,0:T(8,128)(2,1)S(1)} %pad_maximum_fusion.1.refs_7_), channel_id=1, source_target_pairs={{0,4},{4,0},{8,12},{12,8},{16,20},{20,16},{24,28},{28,24},{1,5},{5... | collective-permute-start | bytes 2359304 | tf_op jit(solution)/shard_map/ppermute | solution.py:581
  37.5 14.7 %copy-start.5 = (bf16[4,64,1536]{2,1,0:T(8,128)(2,1)}, bf16[4,64,1536]{2,1,0:T(8,128)(2,1)S(1)}, u32[]{:S(2)}) copy-start(bf16[4,64,1536]{2,1,0:T(8,128)(2,1)S(1)} %pad_maximum_fusion.refs_5_) | copy-start | bytes 2359300
  37.5 14.6 %collective-permute-start.3 = (bf16[4,64,1536]{2,1,0:T(8,128)(2,1)S(1)}, bf16[4,64,1536]{2,1,0:T(8,128)(2,1)}, u32[]{:S(2)}, u32[]{:S(2)}) collective-permute-start(bf16[4,64,1536]{2,1,0:T(8,128)(2,1)S(1)} %pad_maximum_fusion.refs_5_), channel_id=1, source_target_pairs={{0,4},{4,0},{8,12},{12,8},{16,20},{20,16},{24,28},{28,24},{1,5},{5... | collective-permute-start | bytes 2359304 | tf_op jit(solution)/shard_map/ppermute | solution.py:581
  37.6 14.5 %all-to-all-start.1 = ((bf16[32,48,128]{2,1,0:T(8,128)(2,1)}), bf16[32,48,128]{2,1,0:T(8,128)(2,1)S(1)}, u32[]{:S(2)}, u32[]{:S(2)}) async-start(bf16[32,48,128]{2,1,0:T(8,128)(2,1)} %get-tuple-element.38), calls=%async_computation.1 | async-start | bytes 786432 | tf_op jit(solution)/shard_map/all_to_all | solution.py:664
  72.2 4.6 %collective-permute-start.6 = (bf16[4,64,1536]{2,1,0:T(8,128)(2,1)}, bf16[4,64,1536]{2,1,0:T(8,128)(2,1)}, u32[]{:S(2)}, u32[]{:S(2)}) collective-permute-start(bf16[4,64,1536]{2,1,0:T(8,128)(2,1)} %get-tuple-element.52), channel_id=1, source_target_pairs={{0,4},{4,0},{8,12},{12,8},{16,20},{20,16},{24,28},{28,24},{1,5},{5... | collective-permute-start | bytes 2359304 | tf_op jit(solution)/shard_map/ppermute | solution.py:581
  73.5 6.3 %collective-permute-start.9 = (bf16[4,64,1536]{2,1,0:T(8,128)(2,1)}, bf16[4,64,1536]{2,1,0:T(8,128)(2,1)}, u32[]{:S(2)}, u32[]{:S(2)}) collective-permute-start(bf16[4,64,1536]{2,1,0:T(8,128)(2,1)} %get-tuple-element.54), channel_id=1, source_target_pairs={{0,4},{4,0},{8,12},{12,8},{16,20},{20,16},{24,28},{28,24},{1,5},{5... | collective-permute-start | bytes 2359304 | tf_op jit(solution)/shard_map/ppermute | solution.py:581
  73.6 42.4 %all-to-all-start.2 = ((bf16[32,48,128]{2,1,0:T(8,128)(2,1)}), bf16[32,48,128]{2,1,0:T(8,128)(2,1)S(1)}, u32[]{:S(2)}, u32[]{:S(2)}) async-start(bf16[32,48,128]{2,1,0:T(8,128)(2,1)} %get-tuple-element.45), calls=%async_computation.2 | async-start | bytes 786432 | tf_op jit(solution)/shard_map/all_to_all | solution.py:728
  78.2 14.0 %collective-permute-start.7 = (bf16[2,64,1536]{2,1,0:T(8,128)(2,1)S(1)}, bf16[2,64,1536]{2,1,0:T(8,128)(2,1)S(1)}, u32[]{:S(2)}, u32[]{:S(2)}) collective-permute-start(bf16[2,64,1536]{2,1,0:T(8,128)(2,1)S(1)} %get-tuple-element.59), channel_id=1, source_target_pairs={{0,8},{4,12},{8,0},{12,4},{16,24},{20,28},{24,16},{28,20},{1,9},{5... | collective-permute-start | bytes 1179656 | tf_op jit(solution)/shard_map/ppermute | solution.py:581
  81.2 12.8 %collective-permute-start.10 = (bf16[2,64,1536]{2,1,0:T(8,128)(2,1)S(1)}, bf16[2,64,1536]{2,1,0:T(8,128)(2,1)S(1)}, u32[]{:S(2)}, u32[]{:S(2)}) collective-permute-start(bf16[2,64,1536]{2,1,0:T(8,128)(2,1)S(1)} %get-tuple-element.61), channel_id=1, source_target_pairs={{0,16},{4,20},{8,24},{12,28},{16,0},{20,4},{24,8},{28,12},{1,17},{... | collective-permute-start | bytes 1179656 | tf_op jit(solution)/shard_map/ppermute | solution.py:581
  92.3 6.5 %collective-permute-start.8 = (bf16[1,64,1536]{2,1,0:T(8,128)(2,1)S(1)}, bf16[1,64,1536]{2,1,0:T(8,128)(2,1)S(1)}, u32[]{:S(2)}, u32[]{:S(2)}) collective-permute-start(bf16[1,64,1536]{2,1,0:T(8,128)(2,1)S(1)} %get-tuple-element.63), channel_id=1, source_target_pairs={{0,16},{4,20},{8,24},{12,28},{16,0},{20,4},{24,8},{28,12},{1,17},{... | collective-permute-start | bytes 589832 | tf_op jit(solution)/shard_map/ppermute | solution.py:581
  94.0 6.3 %collective-permute-start.11 = (bf16[1,64,1536]{2,1,0:T(8,128)(2,1)S(1)}, bf16[1,64,1536]{2,1,0:T(8,128)(2,1)S(1)}, u32[]{:S(2)}, u32[]{:S(2)}) collective-permute-start(bf16[1,64,1536]{2,1,0:T(8,128)(2,1)S(1)} %get-tuple-element.65), channel_id=1, source_target_pairs={{0,8},{4,12},{8,0},{12,4},{16,24},{20,28},{24,16},{28,20},{1,9},{5... | collective-permute-start | bytes 589832 | tf_op jit(solution)/shard_map/ppermute | solution.py:581
  100.5 5.3 %collective-permute-start.12 = (bf16[64,768]{1,0:T(8,128)(2,1)S(1)}, bf16[64,768]{1,0:T(8,128)(2,1)S(1)}, u32[]{:S(2)}, u32[]{:S(2)}) collective-permute-start(bf16[64,768]{1,0:T(8,128)(2,1)S(1)} %get-tuple-element.66), channel_id=1, source_target_pairs={{0,1},{1,0},{2,3},{3,2},{4,5},{5,4},{6,7},{7,6},{8,9},{9,8},{10,11... | collective-permute-start | bytes 294920 | tf_op jit(solution)/shard_map/ppermute | solution.py:581
  101.8 9.7 %collective-permute-start.13 = (bf16[64,768]{1,0:T(8,128)(2,1)S(1)}, bf16[64,768]{1,0:T(8,128)(2,1)S(1)}, u32[]{:S(2)}, u32[]{:S(2)}) collective-permute-start(bf16[64,768]{1,0:T(8,128)(2,1)S(1)} %get-tuple-element.68), channel_id=1, source_target_pairs={{0,2},{1,3},{2,0},{3,1},{4,6},{5,7},{6,4},{7,5},{8,10},{9,11},{10,... | collective-permute-start | bytes 294920 | tf_op jit(solution)/shard_map/ppermute | solution.py:581
  104.4 7.1 %collective-permute-start.14 = (bf16[64,768]{1,0:T(8,128)(2,1)S(1)}, bf16[64,768]{1,0:T(8,128)(2,1)S(1)}, u32[]{:S(2)}, u32[]{:S(2)}) collective-permute-start(bf16[64,768]{1,0:T(8,128)(2,1)S(1)} %get-tuple-element.67), channel_id=1, source_target_pairs={{0,3},{1,2},{2,1},{3,0},{4,7},{5,6},{6,5},{7,4},{8,11},{9,10},{10,... | collective-permute-start | bytes 294920 | tf_op jit(solution)/shard_map/ppermute | solution.py:581
  111.5 10.1 %collective-permute-start.15 = (bf16[64,768]{1,0:T(8,128)(2,1)S(1)}, bf16[64,768]{1,0:T(8,128)(2,1)S(1)}, u32[]{:S(2)}, u32[]{:S(2)}) collective-permute-start(bf16[64,768]{1,0:T(8,128)(2,1)S(1)} %fusion.2.refs_0_), channel_id=1, source_target_pairs={{0,1},{1,0},{2,3},{3,2},{4,5},{5,4},{6,7},{7,6},{8,9},{9,8},{10,11... | collective-permute-start | bytes 294920 | tf_op jit(solution)/shard_map/ppermute | solution.py:581
  113.2 9.2 %collective-permute-start.16 = (bf16[64,768]{1,0:T(8,128)(2,1)S(1)}, bf16[64,768]{1,0:T(8,128)(2,1)S(1)}, u32[]{:S(2)}, u32[]{:S(2)}) collective-permute-start(bf16[64,768]{1,0:T(8,128)(2,1)S(1)} %fusion.2.refs_0_), channel_id=1, source_target_pairs={{0,2},{1,3},{2,0},{3,1},{4,6},{5,7},{6,4},{7,5},{8,10},{9,11},{10,... | collective-permute-start | bytes 294920 | tf_op jit(solution)/shard_map/ppermute | solution.py:581
  114.8 7.6 %collective-permute-start.17 = (bf16[64,768]{1,0:T(8,128)(2,1)S(1)}, bf16[64,768]{1,0:T(8,128)(2,1)S(1)}, u32[]{:S(2)}, u32[]{:S(2)}) collective-permute-start(bf16[64,768]{1,0:T(8,128)(2,1)S(1)} %fusion.2.refs_0_), channel_id=1, source_target_pairs={{0,3},{1,2},{2,1},{3,0},{4,7},{5,6},{6,5},{7,4},{8,11},{9,10},{10,... | collective-permute-start | bytes 294920 | tf_op jit(solution)/shard_map/ppermute | solution.py:581
